TPU v7x, 32 devices: a whole 2x2x4 slice. The times are simulated.
32 devices in a mesh: fsdp: 8 (over z, core), tp: 4 (over y, x).
Axes of the slice: x: 2, y: 2, z: 4, core: 2. Of those that a mesh axis runs over, the one named last changes fastest.
Arguments:
- tokens: float32 [3, 1024, 2048], P(None, 'fsdp'), may hold values from -6 to 6
- cotangent: float32 [3, 1024, 2048], P(None, 'fsdp'), may hold values from -6 to 6
- w_query: bfloat16 [2048, 2048], P('fsdp', 'tp'), may hold values from -0.125 to 0.125
- w_key: bfloat16 [2048, 2048], P('fsdp', 'tp'), may hold values from -0.125 to 0.125
- w_value: bfloat16 [2048, 2048], P('fsdp', 'tp'), may hold values from -0.125 to 0.125
- w_out: bfloat16 [2048, 2048], P('tp', 'fsdp'), may hold values from -0.125 to 0.125
- query_gain: bfloat16 [2048], P(('tp', 'fsdp')), may hold values from 0.25 to 1.75
- key_gain: bfloat16 [2048], P(('tp', 'fsdp')), may hold values from 0.25 to 1.75
- attn_gain: bfloat16 [2048], P('fsdp'), may hold values from 0.25 to 1.75
- w_gate: bfloat16 [2048, 8192], P('fsdp', 'tp'), may hold values from -0.125 to 0.125
- w_up: bfloat16 [2048, 8192], P('fsdp', 'tp'), may hold values from -0.125 to 0.125
- w_down: bfloat16 [8192, 2048], P('tp', 'fsdp'), may hold values from -0.0625 to 0.0625
- mlp_gain: bfloat16 [2048], P('fsdp'), may hold values from 0.25 to 1.75
- group_ids: int32 [3, 1], replicated, may hold values from 0 to 1
- span_order: int32 [16], replicated, may hold values from 0 to 15, each once
Outputs:
- layer_out: float32 [3, 1024, 2048], P(None, 'fsdp')
- input_grad: float32 [3, 1024, 2048], P(None, 'fsdp')
- grad_query: float32 [2048, 2048], P('fsdp', 'tp')
- grad_key: float32 [2048, 2048], P('fsdp', 'tp')
- grad_value: float32 [2048, 2048], P('fsdp', 'tp')
- grad_out: float32 [2048, 2048], P('tp', 'fsdp')
- grad_query_gain: float32 [2048], P(('tp', 'fsdp'))
- grad_key_gain: float32 [2048], P(('tp', 'fsdp'))
- grad_attn_gain: float32 [2048], P('fsdp')
- grad_gate: float32 [2048, 8192], P('fsdp', 'tp')
- grad_up: float32 [2048, 8192], P('fsdp', 'tp')
- grad_down: float32 [8192, 2048], P('tp', 'fsdp')
- grad_mlp_gain: float32 [2048], P('fsdp')
- grad_out_groups: float32 [2, 2048, 2048], P(None, 'tp', 'fsdp')
Inputs may be any that keep to these rules, and one draw needn't show every extreme that they name: `span_order`: a permutation: every stored span holds a different block of 64 positions. `group_ids`: every group holds at least one sequence.
All inputs are finite; a program needn't handle non-finite values.
Results may differ from a plain program's by a relative error of at most 0.024.
Values may be sent and summed in bfloat16 or wider, within the bound.
No kernel may reach another device: no remote copies, remote signals or barrier semaphores. Data moves between devices by JAX's collectives and lax.ppermute only.
A program may use at most 192 MiB of HBM per device.

v0:
```python
from functools import partial

import jax
import jax.numpy as jnp
from jax import lax
from jax.sharding import PartitionSpec as P

HEAD_DIM = 128
GROUPS = 2


epsilon = 1e-06
rope_base = 500000.0


def positions_of(span_order, start_row, count, span_len):
    row_index = start_row + jnp.arange(count, dtype=jnp.int32)
    span_ids = row_index // span_len
    span_table = jnp.arange(span_order.shape[0], dtype=jnp.int32)
    picked = jnp.sum(
        jnp.where(span_ids[:, None] == span_table[None, :], span_order[None, :], 0), axis=1
    )
    return picked * span_len + row_index % span_len


def rotary(inputs, positions, direction):
    half_dim = inputs.shape[-1] // 2
    inv_freq = jnp.power(
        rope_base, -(jnp.arange(half_dim, dtype=jnp.float32) * 2.0 / inputs.shape[-1])
    )
    angles = positions.astype(jnp.float32)[:, None] * inv_freq[None, :]
    cosine = jnp.cos(angles)[None, :, None, :]
    sine = direction * jnp.sin(angles)[None, :, None, :]
    front_half = inputs[..., :half_dim]
    back_half = inputs[..., half_dim:]
    return jnp.concatenate(
        [front_half * cosine - back_half * sine, back_half * cosine + front_half * sine], axis=-1
    )


def score_block(query_rot, key_rot, query_pos, key_pos):
    raw_scores = jnp.einsum(
        "rqhd,rkhd->rhqk", query_rot, key_rot, preferred_element_type=jnp.float32
    )
    scaled = raw_scores * query_rot.shape[-1] ** (-0.5)
    visible = key_pos[None, :] <= query_pos[:, None]
    return (scaled, visible)


def attend(query_rot, keys_all, values_all, query_pos, key_pos):
    scaled, visible = score_block(query_rot, keys_all, query_pos, key_pos)
    scaled = jnp.where(visible[None, None], scaled, -1e30)
    row_peak = jnp.max(scaled, axis=-1, keepdims=True)
    log_total = row_peak + jnp.log(jnp.sum(jnp.exp(scaled - row_peak), axis=-1, keepdims=True))
    attn_prob = jnp.exp(scaled - log_total).astype(jnp.bfloat16)
    attended = jnp.einsum(
        "rhqk,rkhd->rqhd", attn_prob, values_all, preferred_element_type=jnp.float32
    )
    return (attended, log_total[..., 0])


def query_step(
    carried,
    pieces,
    start_row,
    query_rot,
    grad_attended,
    log_total,
    row_delta,
    query_pos,
    span_order,
    span_len,
    skipping,
):
    key_piece, value_piece = pieces
    key_pos = positions_of(span_order, start_row, key_piece.shape[1], span_len)
    scaled, visible = score_block(query_rot, key_piece, query_pos, key_pos)
    attn_prob = jnp.where(visible[None, None], jnp.exp(scaled - log_total[..., None]), 0.0)
    grad_prob = jnp.einsum(
        "rqhd,rkhd->rhqk", grad_attended, value_piece, preferred_element_type=jnp.float32
    )
    grad_scores = (attn_prob * (grad_prob - row_delta[..., None])).astype(jnp.bfloat16)
    return jnp.einsum("rhqk,rkhd->rqhd", grad_scores, key_piece, preferred_element_type=jnp.float32)


def key_step(
    carried,
    pieces,
    start_row,
    key_rot,
    values_low,
    key_pos,
    lse_all,
    delta_all,
    span_order,
    span_len,
    skipping,
):
    query_low, grad_low = pieces
    count = query_low.shape[1]
    query_pos = positions_of(span_order, start_row, count, span_len)
    scaled, visible = score_block(query_low, key_rot, query_pos, key_pos)
    lse_rows = jnp.transpose(lse_all, (0, 2, 1))[..., None]
    delta_rows = jnp.transpose(delta_all, (0, 2, 1))[..., None]
    attn_prob = jnp.where(visible[None, None], jnp.exp(scaled - lse_rows), 0.0)
    grad_values = jnp.einsum(
        "rhqk,rqhd->rkhd",
        attn_prob.astype(jnp.bfloat16),
        grad_low,
        preferred_element_type=jnp.float32,
    )
    grad_prob = jnp.einsum(
        "rqhd,rkhd->rhqk", grad_low, values_low, preferred_element_type=jnp.float32
    )
    grad_scores = (attn_prob * (grad_prob - delta_rows)).astype(jnp.bfloat16)
    grad_keys = jnp.einsum(
        "rhqk,rqhd->rkhd", grad_scores, query_low, preferred_element_type=jnp.float32
    )
    return (grad_keys, grad_values)


def norm_back(branch, inv_root, gain, grad_output):
    gained = grad_output * gain
    grad_gain = jnp.sum(grad_output * branch * inv_root, axis=(0, 1))
    row_total = jnp.sum(branch * gained, axis=-1, keepdims=True)
    grad_branch = inv_root * gained - branch * inv_root**3 * row_total / branch.shape[-1]
    return (grad_gain, grad_branch)


def local(
    tokens,
    cotangent,
    w_query,
    w_key,
    w_value,
    w_out,
    query_gain,
    key_gain,
    attn_gain,
    w_gate,
    w_up,
    w_down,
    mlp_gain,
    group_ids,
    span_order,
):
    batch_rows, local_len, model_width = tokens.shape
    span_len = local_len // 2
    seq_len = local_len * lax.axis_size("fsdp")
    query_pos = positions_of(span_order, lax.axis_index("fsdp") * local_len, local_len, span_len)
    all_pos = positions_of(span_order, 0, seq_len, span_len)
    attn_set = (
        lax.all_gather(w_query, "fsdp", axis=0, tiled=True),
        lax.all_gather(w_key, "fsdp", axis=0, tiled=True),
        lax.all_gather(w_value, "fsdp", axis=0, tiled=True),
        lax.all_gather(w_out, "fsdp", axis=1, tiled=True),
        lax.all_gather(query_gain, "fsdp", axis=0, tiled=True),
        lax.all_gather(key_gain, "fsdp", axis=0, tiled=True),
        lax.all_gather(attn_gain, "fsdp", axis=0, tiled=True),
    )
    gain_query = attn_set[4].astype(jnp.float32)
    gain_key = attn_set[5].astype(jnp.float32)
    gain_attn = attn_set[6].astype(jnp.float32)
    tokens_low = tokens.astype(jnp.bfloat16)
    queries = jnp.einsum("rsd,de->rse", tokens_low, attn_set[0], preferred_element_type=jnp.float32)
    keys = jnp.einsum("rsd,de->rse", tokens_low, attn_set[1], preferred_element_type=jnp.float32)
    values = jnp.einsum("rsd,de->rse", tokens_low, attn_set[2], preferred_element_type=jnp.float32)
    square_sums = lax.psum(
        (jnp.sum(queries * queries, axis=-1), jnp.sum(keys * keys, axis=-1)), "tp"
    )
    query_scale = lax.rsqrt(square_sums[0] / model_width + epsilon)[..., None]
    key_scale = lax.rsqrt(square_sums[1] / model_width + epsilon)[..., None]
    local_width = queries.shape[-1]
    head_count = local_width // HEAD_DIM
    head_shape = (batch_rows, local_len, head_count, HEAD_DIM)
    query_rot = rotary(
        (queries * query_scale * gain_query).reshape(head_shape), query_pos, 1.0
    ).astype(jnp.bfloat16)
    key_rot = rotary((keys * key_scale * gain_key).reshape(head_shape), query_pos, 1.0).astype(
        jnp.bfloat16
    )
    values_low = values.astype(jnp.bfloat16).reshape(head_shape)
    keys_gathered, values_gathered = (
        lax.all_gather(key_rot, "fsdp", axis=1, tiled=True),
        lax.all_gather(values_low, "fsdp", axis=1, tiled=True),
    )
    attended, log_total = attend(query_rot, keys_gathered, values_gathered, query_pos, all_pos)
    attended_low = attended.reshape(batch_rows, local_len, local_width).astype(jnp.bfloat16)
    branch_attn = lax.psum(
        jnp.einsum(
            "rse,ed->rsd", attended_low, attn_set[3], preferred_element_type=jnp.float32
        ).astype(jnp.bfloat16),
        "tp",
    ).astype(jnp.float32)
    attn_norm = lax.rsqrt(jnp.mean(branch_attn * branch_attn, axis=-1, keepdims=True) + epsilon)
    hidden = tokens + branch_attn * attn_norm * gain_attn
    mlp_set = (
        lax.all_gather(w_gate, "fsdp", axis=0, tiled=True),
        lax.all_gather(w_up, "fsdp", axis=0, tiled=True),
        lax.all_gather(w_down, "fsdp", axis=1, tiled=True),
        lax.all_gather(mlp_gain, "fsdp", axis=0, tiled=True),
    )
    gain_mlp = mlp_set[3].astype(jnp.float32)
    hidden_low = hidden.astype(jnp.bfloat16)
    gate_act = jnp.einsum("rsd,df->rsf", hidden_low, mlp_set[0], preferred_element_type=jnp.float32)
    up_act = jnp.einsum("rsd,df->rsf", hidden_low, mlp_set[1], preferred_element_type=jnp.float32)
    mixed_low = (jax.nn.silu(gate_act) * up_act).astype(jnp.bfloat16)
    branch_mlp = lax.psum(
        jnp.einsum("rsf,fd->rsd", mixed_low, mlp_set[2], preferred_element_type=jnp.float32).astype(
            jnp.bfloat16
        ),
        "tp",
    ).astype(jnp.float32)
    mlp_norm = lax.rsqrt(jnp.mean(branch_mlp * branch_mlp, axis=-1, keepdims=True) + epsilon)
    layer_out = hidden + branch_mlp * mlp_norm * gain_mlp
    back_set = (
        lax.all_gather(w_query, "fsdp", axis=0, tiled=True),
        lax.all_gather(w_key, "fsdp", axis=0, tiled=True),
        lax.all_gather(w_value, "fsdp", axis=0, tiled=True),
        lax.all_gather(w_out, "fsdp", axis=1, tiled=True),
        lax.all_gather(w_gate, "fsdp", axis=0, tiled=True),
        lax.all_gather(w_up, "fsdp", axis=0, tiled=True),
        lax.all_gather(w_down, "fsdp", axis=1, tiled=True),
    )
    query_back, key_back, value_back, out_back, gate_back, up_back, down_back = back_set
    grad_gain_mlp, grad_branch_mlp = norm_back(branch_mlp, mlp_norm, gain_mlp, cotangent)
    grad_mlp_low = grad_branch_mlp.astype(jnp.bfloat16)
    grad_down_w = jnp.einsum(
        "rsf,rsd->fd", mixed_low, grad_mlp_low, preferred_element_type=jnp.float32
    )
    grad_mixed = jnp.einsum(
        "rsd,fd->rsf", grad_mlp_low, down_back, preferred_element_type=jnp.float32
    )
    gate_sigma = jax.nn.sigmoid(gate_act)
    grad_gate_act = (
        grad_mixed * up_act * gate_sigma * (1.0 + gate_act * (1.0 - gate_sigma))
    ).astype(jnp.bfloat16)
    grad_up_act = (grad_mixed * gate_act * gate_sigma).astype(jnp.bfloat16)
    mlp_back_in = jnp.einsum(
        "rsf,df->rsd", grad_gate_act, gate_back, preferred_element_type=jnp.float32
    ) + jnp.einsum("rsf,df->rsd", grad_up_act, up_back, preferred_element_type=jnp.float32)
    grad_hidden = cotangent + lax.psum(mlp_back_in.astype(jnp.bfloat16), "tp").astype(jnp.float32)
    grad_gate_w = jnp.einsum(
        "rsd,rsf->df", hidden_low, grad_gate_act, preferred_element_type=jnp.float32
    )
    grad_up_w = jnp.einsum(
        "rsd,rsf->df", hidden_low, grad_up_act, preferred_element_type=jnp.float32
    )
    grad_gain_attn, grad_branch_attn = norm_back(branch_attn, attn_norm, gain_attn, grad_hidden)
    grad_attn_low = grad_branch_attn.astype(jnp.bfloat16)
    per_row = jnp.einsum(
        "rse,rsd->red", attended_low, grad_attn_low, preferred_element_type=jnp.float32
    )
    member = (group_ids[:, 0][:, None] == jnp.arange(GROUPS, dtype=jnp.int32)[None, :]).astype(
        jnp.float32
    )
    grad_out_groups = jnp.sum(member[:, :, None, None] * per_row[:, None], axis=0)
    grad_out_w = jnp.sum(per_row, axis=0)
    grad_attended_low = (
        jnp.einsum("rsd,ed->rse", grad_attn_low, out_back, preferred_element_type=jnp.float32)
        .reshape(head_shape)
        .astype(jnp.bfloat16)
    )
    delta_rows = jnp.sum(grad_attended_low.astype(jnp.float32) * attended, axis=-1)
    row_delta = jnp.transpose(delta_rows, (0, 2, 1))
    zero_grad = jnp.zeros(head_shape, jnp.float32)
    query_fn = partial(
        query_step,
        query_rot=query_rot,
        grad_attended=grad_attended_low,
        log_total=log_total,
        row_delta=row_delta,
        query_pos=query_pos,
        span_order=span_order,
        span_len=span_len,
        skipping=False,
    )
    grad_query_rot = query_fn(
        zero_grad,
        (
            lax.all_gather(key_rot, "fsdp", axis=1, tiled=True),
            lax.all_gather(values_low, "fsdp", axis=1, tiled=True),
        ),
        jnp.int32(0),
    )
    lse_rows = jnp.transpose(log_total, (0, 2, 1))
    lse_all, delta_all = (
        lax.all_gather(lse_rows, "fsdp", axis=1, tiled=True),
        lax.all_gather(delta_rows, "fsdp", axis=1, tiled=True),
    )
    key_fn = partial(
        key_step,
        key_rot=key_rot,
        values_low=values_low,
        key_pos=query_pos,
        lse_all=lse_all,
        delta_all=delta_all,
        span_order=span_order,
        span_len=span_len,
        skipping=False,
    )
    grad_key_rot, grad_values = key_fn(
        (zero_grad, zero_grad),
        (
            lax.all_gather(query_rot, "fsdp", axis=1, tiled=True),
            lax.all_gather(grad_attended_low, "fsdp", axis=1, tiled=True),
        ),
        jnp.int32(0),
    )
    scaling = HEAD_DIM ** (-0.5)
    grad_qn = rotary(grad_query_rot * scaling, query_pos, -1.0).reshape(
        batch_rows, local_len, local_width
    )
    grad_kn = rotary(grad_key_rot * scaling, query_pos, -1.0).reshape(
        batch_rows, local_len, local_width
    )
    gained_query = grad_qn * gain_query
    gained_key = grad_kn * gain_key
    cross_sums = lax.psum(
        (jnp.sum(queries * gained_query, axis=-1), jnp.sum(keys * gained_key, axis=-1)), "tp"
    )
    grad_gain_query = jnp.sum(grad_qn * queries * query_scale, axis=(0, 1))
    grad_gain_key = jnp.sum(grad_kn * keys * key_scale, axis=(0, 1))
    grad_queries = (
        query_scale * gained_query
        - queries * query_scale**3 * cross_sums[0][..., None] / model_width
    ).astype(jnp.bfloat16)
    grad_keys = (
        key_scale * gained_key - keys * key_scale**3 * cross_sums[1][..., None] / model_width
    ).astype(jnp.bfloat16)
    grad_values_low = grad_values.reshape(batch_rows, local_len, local_width).astype(jnp.bfloat16)
    attn_back_in = jnp.einsum(
        "rse,de->rsd", grad_queries, query_back, preferred_element_type=jnp.float32
    )
    attn_back_in = attn_back_in + jnp.einsum(
        "rse,de->rsd", grad_keys, key_back, preferred_element_type=jnp.float32
    )
    attn_back_in = attn_back_in + jnp.einsum(
        "rse,de->rsd", grad_values_low, value_back, preferred_element_type=jnp.float32
    )
    input_grad = grad_hidden + lax.psum(attn_back_in.astype(jnp.bfloat16), "tp").astype(jnp.float32)
    grad_query_w = jnp.einsum(
        "rsd,rse->de", tokens_low, grad_queries, preferred_element_type=jnp.float32
    )
    grad_key_w = jnp.einsum(
        "rsd,rse->de", tokens_low, grad_keys, preferred_element_type=jnp.float32
    )
    grad_value_w = jnp.einsum(
        "rsd,rse->de", tokens_low, grad_values_low, preferred_element_type=jnp.float32
    )
    summed = (
        lax.psum_scatter(
            grad_query_w.astype(jnp.bfloat16), "fsdp", scatter_dimension=0, tiled=True
        ).astype(jnp.float32),
        lax.psum_scatter(
            grad_key_w.astype(jnp.bfloat16), "fsdp", scatter_dimension=0, tiled=True
        ).astype(jnp.float32),
        lax.psum_scatter(
            grad_value_w.astype(jnp.bfloat16), "fsdp", scatter_dimension=0, tiled=True
        ).astype(jnp.float32),
        lax.psum_scatter(
            grad_out_w.astype(jnp.bfloat16), "fsdp", scatter_dimension=1, tiled=True
        ).astype(jnp.float32),
        lax.psum_scatter(
            grad_out_groups.astype(jnp.bfloat16), "fsdp", scatter_dimension=2, tiled=True
        ).astype(jnp.float32),
        lax.psum_scatter(
            grad_gain_query.astype(jnp.bfloat16), "fsdp", scatter_dimension=0, tiled=True
        ).astype(jnp.float32),
        lax.psum_scatter(
            grad_gain_key.astype(jnp.bfloat16), "fsdp", scatter_dimension=0, tiled=True
        ).astype(jnp.float32),
        lax.psum_scatter(
            grad_gain_attn.astype(jnp.bfloat16), "fsdp", scatter_dimension=0, tiled=True
        ).astype(jnp.float32),
        lax.psum_scatter(
            grad_gate_w.astype(jnp.bfloat16), "fsdp", scatter_dimension=0, tiled=True
        ).astype(jnp.float32),
        lax.psum_scatter(
            grad_up_w.astype(jnp.bfloat16), "fsdp", scatter_dimension=0, tiled=True
        ).astype(jnp.float32),
        lax.psum_scatter(
            grad_down_w.astype(jnp.bfloat16), "fsdp", scatter_dimension=1, tiled=True
        ).astype(jnp.float32),
        lax.psum_scatter(
            grad_gain_mlp.astype(jnp.bfloat16), "fsdp", scatter_dimension=0, tiled=True
        ).astype(jnp.float32),
    )
    return (
        layer_out,
        input_grad,
        summed[0],
        summed[1],
        summed[2],
        summed[3],
        summed[5],
        summed[6],
        summed[7],
        summed[8],
        summed[9],
        summed[10],
        summed[11],
        summed[4],
    )


def solution(mesh):
    in_specs = (
        P(None, "fsdp", None),
        P(None, "fsdp", None),
        P("fsdp", "tp"),
        P("fsdp", "tp"),
        P("fsdp", "tp"),
        P("tp", "fsdp"),
        P(("tp", "fsdp")),
        P(("tp", "fsdp")),
        P("fsdp"),
        P("fsdp", "tp"),
        P("fsdp", "tp"),
        P("tp", "fsdp"),
        P("fsdp"),
        P(),
        P(),
    )
    out_specs = (
        P(None, "fsdp", None),
        P(None, "fsdp", None),
        P("fsdp", "tp"),
        P("fsdp", "tp"),
        P("fsdp", "tp"),
        P("tp", "fsdp"),
        P(("tp", "fsdp")),
        P(("tp", "fsdp")),
        P("fsdp"),
        P("fsdp", "tp"),
        P("fsdp", "tp"),
        P("tp", "fsdp"),
        P("fsdp"),
        P(None, "tp", "fsdp"),
    )
    return jax.shard_map(local, mesh=mesh, in_specs=in_specs, out_specs=out_specs, check_vma=False)
```

profile of v0, /device:TPU:0, one launch (start us, length us, event | category | flops | bytes accessed | tf_op | source)
XLA Modules:
  0.0 1311.9 jit_solution(8803979867433567628)
XLA Ops:
  9.5 2.1 convert_element_type.202
  13.5 18.7 %all-reduce.9 = (bf16[512]{0:T(512)(128)(2,1)S(1)}, bf16[512]{0:T(512)(128)(2,1)S(1)}) all-reduce(bf16[512]{0:T(512)(128)(2,1)S(1)} %dynamic-update-slice.1, bf16[512]{0:T(512)(128)(2,1)S(1)} %dynamic-update-slice), channel_id=1, replica_groups=mesh['fsdp'=8,'tp'=4] {'fsdp'}, use_global_device_ids=true, to_apply=%add.1 | all-reduce | flops 1024 | bytes 4096
  33.3 8.3 all-gather.20.cloned.1.call-done
  41.6 2.6 multiply_reduce_fusion.4
  44.3 27.6 %all-gather.18.cloned.1.call-done = bf16[2048,512]{1,0:T(8,128)(2,1)} async-done(((bf16[256,512]{1,0:T(8,128)(2,1)}), bf16[2048,512]{1,0:T(8,128)(2,1)}) %all-gather.18.cloned.1.call-update) | async-done | bytes 2097168 | tf_op jit(solution)/shard_map/all_gather | solution.py:153
  71.9 2.6 multiply_reduce_fusion.5
  74.6 9.8 all-reduce.7
  89.1 13.0 all-gather.14.cloned.1.call-done
  102.1 3.0 fusion.98
  107.2 34.5 %all-gather.22.cloned.1.call-done = bf16[3,1024,4,128]{3,1,2,0:T(8,128)(2,1)} async-done(((bf16[3,128,4,128]{3,1,2,0:T(8,128)(2,1)}), bf16[3,1024,4,128]{3,1,2,0:T(8,128)(2,1)}) %all-gather.22.cloned.1.call-update) | async-done | bytes 3145744 | tf_op jit(solution)/shard_map/all_gather | solution.py:184
  141.8 3.2 fusion.14
  147.7 34.2 %all-gather.16.cloned.1.call-done = bf16[3,1024,4,128]{1,3,2,0:T(8,128)(2,1)} async-done(((bf16[3,128,4,128]{1,3,2,0:T(8,128)(2,1)}), bf16[3,1024,4,128]{1,3,2,0:T(8,128)(2,1)}) %all-gather.16.cloned.1.call-update) | async-done | bytes 3145744 | tf_op jit(solution)/shard_map/all_gather | solution.py:185
  181.9 6.6 fusion.139
  188.5 23.7 %all-gather.24.cloned.1.call-done = bf16[512,2048]{1,0:T(8,128)(2,1)} async-done(((bf16[512,256]{1,0:T(8,128)(2,1)}), bf16[512,2048]{1,0:T(8,128)(2,1)}) %all-gather.24.cloned.1.call-update) | async-done | bytes 2097168 | tf_op jit(solution)/shard_map/all_gather | solution.py:156
  212.2 3.7 convolution_convert_fusion
  218.1 11.9 all-gather
  230.1 45.8 %all-reduce.15.cloned.1.call-done = bf16[3,128,2048]{2,1,0:T(8,128)(2,1)} async-done(((bf16[3,128,2048]{2,1,0:T(8,128)(2,1)}), bf16[3,128,2048]{2,1,0:T(8,128)(2,1)}) %all-reduce.15.cloned.1.call-update) | async-done | bytes 1572880 | tf_op jit(solution)/shard_map/psum | solution.py:189
  278.8 3.1 fusion.77
  281.9 77.7 %all-gather.26.cloned.1.call-done = bf16[2048,2048]{1,0:T(8,128)(2,1)} async-done(((bf16[256,2048]{1,0:T(8,128)(2,1)}), bf16[2048,2048]{1,0:T(8,128)(2,1)}) %all-gather.26.cloned.1.call-update) | async-done | bytes 8388624 | tf_op jit(solution)/shard_map/all_gather | solution.py:198
  359.5 8.9 fusion.12
  368.5 73.2 %all-gather.28.cloned.1.call-done = bf16[2048,2048]{1,0:T(8,128)(2,1)} async-done(((bf16[256,2048]{1,0:T(8,128)(2,1)}), bf16[2048,2048]{1,0:T(8,128)(2,1)}) %all-gather.28.cloned.1.call-update) | async-done | bytes 8388624 | tf_op jit(solution)/shard_map/all_gather | solution.py:199
  441.7 10.5 multiply_convert_fusion.4
  452.2 72.0 %all-gather.30.cloned.1.call-done = bf16[2048,2048]{1,0:T(8,128)(2,1)} async-done(((bf16[2048,256]{1,0:T(8,128)(2,1)}), bf16[2048,2048]{1,0:T(8,128)(2,1)}) %all-gather.30.cloned.1.call-update) | async-done | bytes 8388624 | tf_op jit(solution)/shard_map/all_gather | solution.py:200
  524.1 8.4 fusion.53
  532.7 10.1 all-gather.1
  542.8 48.9 %all-reduce.17.cloned.1.call-done = bf16[3,128,2048]{2,1,0:T(8,128)(2,1)} async-done(((bf16[3,128,2048]{2,1,0:T(8,128)(2,1)}), bf16[3,128,2048]{2,1,0:T(8,128)(2,1)}) %all-reduce.17.cloned.1.call-update) | async-done | bytes 1572880 | tf_op jit(solution)/shard_map/psum | solution.py:208
  593.5 14.1 %multiply_convert_fusion.3 = (bf16[3,128,2048]{2,1,0:T(8,128)(2,1)}, bf16[3,128,2048]{2,1,0:T(8,128)(2,1)}) fusion(f32[3,128,2048]{2,1,0:T(8,128)} %fusion.12, f32[3,128,2048]{2,1,0:T(8,128)} %get-tuple-element.116, bf16[2048,2048]{1,0:T(8,128)(2,1)} %all-gather.30.cloned.1.call-done, bf16[3,128,2048]{2,1,0:T(8,128)(2,1)} %all-reduce.17.cloned.1.call-done, ...), kind=kOutput, calls=%fused_computation.67 | convolution fusion | flops 3240102144 | bytes 22555648 | tf_op jit(solution)/shard_map/rsd,fd->rsf/dot_general | solution.py:231
  607.6 6.5 fusion.6
  614.1 10.2 add_convert_fusion.1
  625.1 60.1 %all-reduce.19.cloned.1.call-done = bf16[3,128,2048]{2,1,0:T(8,128)(2,1)} async-done(((bf16[3,128,2048]{2,1,0:T(8,128)(2,1)}), bf16[3,128,2048]{2,1,0:T(8,128)(2,1)}) %all-reduce.19.cloned.1.call-update) | async-done | bytes 1572880 | tf_op jit(solution)/shard_map/psum | solution.py:242
  685.2 8.1 fusion.101
  696.8 15.3 %all_gather.74 = f32[3,1024,4]{1,2,0:T(4,128)} all-gather(f32[3,128,4]{1,2,0:T(4,128)} %bitcast.184), channel_id=1, replica_groups=mesh['fsdp'=8,'tp'=4] {'fsdp'}, dimensions={1}, use_global_device_ids=true | all-gather | bytes 55296 | tf_op jit(solution)/shard_map/all_gather | solution.py:288
  712.1 13.9 %all-gather.32.cloned.1.call-done = bf16[3,1024,4,128]{3,1,2,0:T(8,128)(2,1)} async-done(((bf16[3,128,4,128]{3,1,2,0:T(8,128)(2,1)}), bf16[3,1024,4,128]{3,1,2,0:T(8,128)(2,1)}) %all-gather.32.cloned.1.call-update) | async-done | bytes 3145744 | tf_op jit(solution)/shard_map/all_gather | solution.py:305
  726.0 5.6 fusion.141
  732.3 14.2 %fusion.140 = (bf16[512,2048]{1,0:T(8,128)(2,1)}, f32[3,512,2048]{2,1,0:T(8,128)}) fusion(bf16[3,128,512]{1,2,0:T(8,128)(2,1)} %bitcast.168, bf16[3,128,2048]{2,1,0:T(8,128)(2,1)} %all-reduce.15.cloned.1.call-done, f32[3,128]{1,0:T(4,128)} %get-tuple-element.100, f32[2048]{0:T(1024)S(1)} %bitcast.175, f32[3,128]{1,0:T(4,128)S(1)} %copy-done.40, ...), kind=kOutput, calls=%fused_computation.215 | convolution fusion | flops 819202432 | bytes 21376000 | tf_op jit(solution)/shard_map/rse,rsd->red/dot_general | solution.py:251
  746.6 8.8 fusion.94
  755.4 13.3 %all_gather.76 = f32[3,1024,4]{1,2,0:T(4,128)S(1)} all-gather(f32[3,128,4]{1,2,0:T(4,128)} %multiply_reduce_fusion.3), channel_id=1, replica_groups=mesh['fsdp'=8,'tp'=4] {'fsdp'}, dimensions={1}, use_global_device_ids=true | all-gather | bytes 55296 | tf_op jit(solution)/shard_map/all_gather | solution.py:289
  768.7 9.2 fusion.92
  777.9 2.5 multiply_subtract_fusion
  782.9 10.4 all-reduce.6
  793.3 2.2 subtract_convert_fusion.1
  797.1 2.8 fusion.70
  801.9 2.4 fusion.95
  805.1 2.2 add_convert_fusion
  807.4 11.7 multiply_reduce_fusion
  819.5 4.1 fusion.56
  823.8 4.0 fusion.57
  827.8 4.1 fusion.58
  832.1 9.8 bitcast_convert_fusion.2
  841.9 9.8 bitcast_convert_fusion.1
  852.4 12.4 bitcast_convert_fusion
  868.0 6.5 fusion.36
  874.4 28.7 %all-reduce.8 = (bf16[512]{0:T(512)(128)(2,1)S(1)}, bf16[512]{0:T(512)(128)(2,1)S(1)}, bf16[2048]{0:T(1024)(128)(2,1)S(1)}, bf16[2048]{0:T(1024)(128)(2,1)S(1)}) all-reduce(bf16[512]{0:T(512)(128)(2,1)S(1)} %copy-done.47, bf16[512]{0:T(512)(128)(2,1)S(1)} %copy-done.48, ...), channel_id=6, replica_groups=mesh['fsdp'=8,'tp'=4] {'fsdp'}, use_global_device_ids=true, to_apply=%region_27.28.clone | all-reduce | flops 5120 | bytes 20480
  905.5 13.7 %reduce-scatter.23.cloned.1.call-done = bf16[2,512,256]{2,1,0:T(8,128)(2,1)} async-done(((bf16[2,512,2048]{2,1,0:T(8,128)(2,1)}), bf16[2,512,256]{2,1,0:T(8,128)(2,1)}) %reduce-scatter.23.cloned.1.call-update) | async-done | bytes 524304 | tf_op jit(solution)/shard_map/reduce_scatter | solution.py:364
  919.2 2.1 convert_element_type.264
  921.3 35.2 %reduce-scatter.9.cloned.1.call-done = bf16[256,512]{0,1:T(8,128)(2,1)} async-done(((bf16[2048,512]{0,1:T(8,128)(2,1)}), bf16[256,512]{0,1:T(8,128)(2,1)}) %reduce-scatter.9.cloned.1.call-update) | async-done | bytes 262160 | tf_op jit(solution)/shard_map/reduce_scatter | solution.py:352
  958.4 35.7 %reduce-scatter.11.cloned.1.call-done = bf16[256,512]{0,1:T(8,128)(2,1)} async-done(((bf16[2048,512]{0,1:T(8,128)(2,1)}), bf16[256,512]{0,1:T(8,128)(2,1)}) %reduce-scatter.11.cloned.1.call-update) | async-done | bytes 262160 | tf_op jit(solution)/shard_map/reduce_scatter | solution.py:355
  996.0 35.5 %reduce-scatter.13.cloned.1.call-done = bf16[256,512]{0,1:T(8,128)(2,1)} async-done(((bf16[2048,512]{0,1:T(8,128)(2,1)}), bf16[256,512]{0,1:T(8,128)(2,1)}) %reduce-scatter.13.cloned.1.call-update) | async-done | bytes 262160 | tf_op jit(solution)/shard_map/reduce_scatter | solution.py:358
  1033.4 88.5 %reduce-scatter.17.cloned.1.call-done = bf16[256,2048]{1,0:T(8,128)(2,1)} async-done(((bf16[2048,2048]{1,0:T(8,128)(2,1)}), bf16[256,2048]{1,0:T(8,128)(2,1)}) %reduce-scatter.17.cloned.1.call-update) | async-done | bytes 1048592 | tf_op jit(solution)/shard_map/reduce_scatter | solution.py:376
  1121.9 2.8 convert_element_type.255
  1124.7 87.5 %reduce-scatter.19.cloned.1.call-done = bf16[256,2048]{1,0:T(8,128)(2,1)} async-done(((bf16[2048,2048]{1,0:T(8,128)(2,1)}), bf16[256,2048]{1,0:T(8,128)(2,1)}) %reduce-scatter.19.cloned.1.call-update) | async-done | bytes 1048592 | tf_op jit(solution)/shard_map/reduce_scatter | solution.py:379
  1212.2 2.8 convert_element_type.257
  1215.0 87.5 %reduce-scatter.21.cloned.1.call-done = bf16[2048,256]{1,0:T(8,128)(2,1)} async-done(((bf16[2048,2048]{1,0:T(8,128)(2,1)}), bf16[2048,256]{1,0:T(8,128)(2,1)}) %reduce-scatter.21.cloned.1.call-update) | async-done | bytes 1048592 | tf_op jit(solution)/shard_map/reduce_scatter | solution.py:382
  1302.5 2.7 convert_element_type.259
  (227 shorter events, 43.7 us)
Async XLA Ops:
  7.2 4.5 copy-start.51
  7.2 5.8 copy-start.55
  7.2 6.1 copy-start.56
  7.2 25.0 %copy-start.52 = (s32[16]{0:T(128)S(1)}, s32[16]{0:T(128)}, u32[]{:S(2)}) copy-start(s32[16]{0:T(128)} %param.29) | copy-start | bytes 196
  7.2 34.4 %all-gather.20.cloned.1.call-start = ((), (), s32[]{:S(2)}) async-start(), calls=%async_computation.11 | async-start | bytes 2359296 | tf_op jit(solution)/shard_map/all_gather | solution.py:154
  8.0 64.0 %all-gather.18.cloned.1.call-start = ((), (), s32[]{:S(2)}) async-start(), calls=%async_computation.10 | async-start | bytes 2359296 | tf_op jit(solution)/shard_map/all_gather | solution.py:153
  8.7 93.4 %all-gather.14.cloned.1.call-start = ((), (), s32[]{:S(2)}) async-start(), calls=%async_computation.8 | async-start | bytes 2359296 | tf_op jit(solution)/shard_map/all_gather | solution.py:155
  9.4 132.3 %all-gather.22.cloned.1.call-start = ((), (), s32[]{:S(2)}) async-start(), calls=%async_computation.12 | async-start | bytes 3538944 | tf_op jit(solution)/shard_map/all_gather | solution.py:184
  11.6 62.9 %copy-start.22 = (bf16[3,128,2048]{2,1,0:T(8,128)(2,1)}, bf16[3,128,2048]{2,1,0:T(8,128)(2,1)S(1)}, u32[]{:S(2)}) copy-start(bf16[3,128,2048]{2,1,0:T(8,128)(2,1)S(1)} %convert_element_type.202) | copy-start | bytes 4718596
  32.2 53.3 %copy-start.33 = (f32[512]{0:T(512)}, f32[512]{0:T(512)S(1)}, u32[]{:S(2)}) copy-start(f32[512]{0:T(512)S(1)} %convert_element_type.204) | copy-start | bytes 6148
  32.3 74.5 %copy-start.46 = (s32[128]{0:T(128)}, s32[128]{0:T(128)S(1)}, u32[]{:S(2)}) copy-start(s32[128]{0:T(128)S(1)} %get-tuple-element.73) | copy-start | bytes 1540
  33.3 53.6 %copy-start.25 = (f32[128,64]{1,0:T(8,128)}, f32[128,64]{1,0:T(8,128)S(1)}, u32[]{:S(2)}) copy-start(f32[128,64]{1,0:T(8,128)S(1)} %get-tuple-element.104) | copy-start | bytes 98308
  44.3 40.9 %copy-start.2 = (f32[3,128,512]{2,1,0:T(8,128)}, f32[3,128,512]{2,1,0:T(8,128)S(1)}, u32[]{:S(2)}) copy-start(f32[3,128,512]{2,1,0:T(8,128)S(1)} %get-tuple-element.108) | copy-start | bytes 2359300
  74.6 11.3 copy-start.5
  89.0 18.0 %copy-start.21 = (bf16[3,128,4,64]{3,1,2,0:T(8,128)(2,1)S(1)}, bf16[3,128,4,64]{3,1,2,0:T(8,128)(2,1)}, u32[]{:S(2)}) copy-start(bf16[3,128,4,64]{3,1,2,0:T(8,128)(2,1)} %get-tuple-element.93) | copy-start | bytes 589828
  89.1 92.8 %all-gather.16.cloned.1.call-start = ((), (), s32[]{:S(2)}) async-start(), calls=%async_computation.9 | async-start | bytes 3538944 | tf_op jit(solution)/shard_map/all_gather | solution.py:185
  106.1 106.1 %all-gather.24.cloned.1.call-start = ((), (), s32[]{:S(2)}) async-start(), calls=%async_computation.13 | async-start | bytes 2359296 | tf_op jit(solution)/shard_map/all_gather | solution.py:156
  106.7 169.2 %all-reduce.15.cloned.1.call-start = ((), (), s32[]{:S(2)}) async-start(), calls=%async_computation.14 | async-start | bytes 3145728 | tf_op jit(solution)/shard_map/psum | solution.py:189
  107.0 74.9 %copy-start.20 = (pred[128,1024]{1,0:T(8,128)(4,1)}, pred[128,1024]{1,0:T(8,128)(4,1)S(1)}, u32[]{:S(2)}) copy-start(pred[128,1024]{1,0:T(8,128)(4,1)S(1)} %broadcast_compare_fusion.1) | copy-start | bytes 393220
  107.2 37.7 %copy-start.13 = (bf16[3,128,4,128]{3,1,2,0:T(8,128)(2,1)}, bf16[3,128,4,128]{3,1,2,0:T(8,128)(2,1)S(1)}, u32[]{:S(2)}) copy-start(bf16[3,128,4,128]{3,1,2,0:T(8,128)(2,1)S(1)} %pad_maximum_fusion) | copy-start | bytes 1179652
  145.0 2.7 copy-start
  147.7 40.8 %copy-start.42 = (f32[3,4,128]{2,1,0:T(4,128)}, f32[3,4,128]{2,1,0:T(4,128)S(1)}, u32[]{:S(2)}) copy-start(f32[3,4,128]{2,1,0:T(4,128)S(1)} %log_add_fusion) | copy-start | bytes 18436
  188.5 27.5 %copy-start.17 = (bf16[3,128,4,128]{1,3,2,0:T(8,128)(2,1)}, bf16[3,128,4,128]{1,3,2,0:T(8,128)(2,1)S(1)}, u32[]{:S(2)}) copy-start(bf16[3,128,4,128]{1,3,2,0:T(8,128)(2,1)S(1)} %get-tuple-element.113) | copy-start | bytes 1179652
  216.0 62.8 %copy-start.1 = (f32[3,128,2048]{2,1,0:T(8,128)S(1)}, f32[3,128,2048]{2,1,0:T(8,128)}, u32[]{:S(2)}) copy-start(f32[3,128,2048]{2,1,0:T(8,128)} %param.15) | copy-start | bytes 9437188
  216.0 143.6 %all-gather.26.cloned.1.call-start = ((), (), s32[]{:S(2)}) async-start(), calls=%async_computation.15 | async-start | bytes 9437184 | tf_op jit(solution)/shard_map/all_gather | solution.py:198
  216.7 225.0 %all-gather.28.cloned.1.call-start = ((), (), s32[]{:S(2)}) async-start(), calls=%async_computation.16 | async-start | bytes 9437184 | tf_op jit(solution)/shard_map/all_gather | solution.py:199
  217.5 306.7 %all-gather.30.cloned.1.call-start = ((), (), s32[]{:S(2)}) async-start(), calls=%async_computation.17 | async-start | bytes 9437184 | tf_op jit(solution)/shard_map/all_gather | solution.py:200
  218.1 373.6 %all-reduce.17.cloned.1.call-start = ((), (), s32[]{:S(2)}) async-start(), calls=%async_computation.18 | async-start | bytes 3145728 | tf_op jit(solution)/shard_map/psum | solution.py:208
  524.1 8.5 copy-start.58
  532.6 152.6 %all-reduce.19.cloned.1.call-start = ((), (), s32[]{:S(2)}) async-start(), calls=%async_computation.19 | async-start | bytes 3145728 | tf_op jit(solution)/shard_map/psum | solution.py:242
  542.8 64.8 %copy-start.31 = (f32[8,1,256]{2,1,0:T(1,128)}, f32[8,1,256]{2,1,0:T(1,128)S(1)}, u32[]{:S(2)}) copy-start(f32[8,1,256]{2,1,0:T(1,128)S(1)} %convert_element_type.266) | copy-start | bytes 24580
  593.5 14.1 %copy-start.43 = (f32[3,128]{1,0:T(4,128)}, f32[3,128]{1,0:T(4,128)S(1)}, u32[]{:S(2)}) copy-start(f32[3,128]{1,0:T(4,128)S(1)} %get-tuple-element.99) | copy-start | bytes 4612
  593.5 14.1 %copy-start.49 = (f32[3,128]{1,0:T(4,128)}, f32[3,128]{1,0:T(4,128)S(1)}, u32[]{:S(2)}) copy-start(f32[3,128]{1,0:T(4,128)S(1)} %get-tuple-element.98) | copy-start | bytes 4612
  607.6 6.5 copy-start.59
  624.3 101.7 %all-gather.32.cloned.1.call-start = ((), (), s32[]{:S(2)}) async-start(), calls=%async_computation.20 | async-start | bytes 3538944 | tf_op jit(solution)/shard_map/all_gather | solution.py:305
  625.1 143.6 %all-gather.34.cloned.1.call-start = ((), (), s32[]{:S(2)}) async-start(), calls=%async_computation.21 | async-start | bytes 3538944 | tf_op jit(solution)/shard_map/all_gather | solution.py:306
  685.2 40.8 %copy-start.14 = (bf16[3,128,4,128]{3,1,2,0:T(8,128)(2,1)S(1)}, bf16[3,128,4,128]{3,1,2,0:T(8,128)(2,1)}, u32[]{:S(2)}) copy-start(bf16[3,128,4,128]{3,1,2,0:T(8,128)(2,1)} %pad_maximum_fusion.1) | copy-start | bytes 1179652
  695.3 170.9 %reduce-scatter.15.cloned.1.call-start = ((), (), s32[]{:S(2)}) async-start(), calls=%async_computation.26 | async-start | bytes 2359296 | tf_op jit(solution)/shard_map/reduce_scatter | solution.py:361
  712.1 20.2 %copy-start.40 = (f32[3,128]{1,0:T(4,128)S(1)}, f32[3,128]{1,0:T(4,128)}, u32[]{:S(2)}) copy-start(f32[3,128]{1,0:T(4,128)} %copy-done.39) | copy-start | bytes 4612
  726.0 5.6 copy-start.15
  726.0 5.6 copy-start.24
  732.3 14.3 %copy-start.16 = (bf16[3,128,512]{1,2,0:T(8,128)(2,1)S(1)}, bf16[3,128,512]{1,2,0:T(8,128)(2,1)}, u32[]{:S(2)}) copy-start(bf16[3,128,512]{1,2,0:T(8,128)(2,1)} %copy.79) | copy-start | bytes 1179652
  746.5 121.4 %all-reduce.21.cloned.1.call-start = ((), (), s32[]{:S(2)}) async-start(), calls=%async_computation.22 | async-start | bytes 3145728 | tf_op jit(solution)/shard_map/psum | solution.py:341
  768.7 9.2 copy-start.26
  768.7 9.2 copy-start.28
  777.9 2.7 copy-start.6
  777.9 2.6 copy-start.34
  777.9 4.0 copy-start.3
  777.9 4.0 copy-start.36
  780.5 12.8 copy-start.45
  795.7 5.2 slice-start
  797.0 2.8 copy-start.19
  797.0 3.8 slice-start.1
  801.9 3.2 copy-start.18
  807.3 111.9 %reduce-scatter.23.cloned.1.call-start = ((), (), s32[]{:S(2)}) async-start(), calls=%async_computation.30 | async-start | bytes 4718592 | tf_op jit(solution)/shard_map/reduce_scatter | solution.py:364
  819.1 137.4 %reduce-scatter.9.cloned.1.call-start = ((), (), s32[]{:S(2)}) async-start(), calls=%async_computation.23 | async-start | bytes 2359296 | tf_op jit(solution)/shard_map/reduce_scatter | solution.py:352
  823.7 170.4 %reduce-scatter.11.cloned.1.call-start = ((), (), s32[]{:S(2)}) async-start(), calls=%async_computation.24 | async-start | bytes 2359296 | tf_op jit(solution)/shard_map/reduce_scatter | solution.py:355
  827.8 203.7 %reduce-scatter.13.cloned.1.call-start = ((), (), s32[]{:S(2)}) async-start(), calls=%async_computation.25 | async-start | bytes 2359296 | tf_op jit(solution)/shard_map/reduce_scatter | solution.py:358
  832.0 289.9 %reduce-scatter.17.cloned.1.call-start = ((), (), s32[]{:S(2)}) async-start(), calls=%async_computation.27 | async-start | bytes 9437184 | tf_op jit(solution)/shard_map/reduce_scatter | solution.py:376
  841.9 370.3 %reduce-scatter.19.cloned.1.call-start = ((), (), s32[]{:S(2)}) async-start(), calls=%async_computation.28 | async-start | bytes 9437184 | tf_op jit(solution)/shard_map/reduce_scatter | solution.py:379
  851.8 450.8 %reduce-scatter.21.cloned.1.call-start = ((), (), s32[]{:S(2)}) async-start(), calls=%async_computation.29 | async-start | bytes 9437184 | tf_op jit(solution)/shard_map/reduce_scatter | solution.py:382
  864.8 3.1 copy-start.41
  867.9 6.5 copy-start.47
  867.9 6.5 copy-start.48
  (21 other events, 34.3 us)
Sparse Core Ops, SparseCore 0:
  9.6 31.9 all-gather.19
  43.2 28.6 all-gather.17
  73.5 28.5 all-gather.13
  104.1 37.6 all-gather.21
  143.8 38.0 all-gather.15
  183.3 28.8 all-gather.23
  216.1 59.7 all-reduce.14
  277.5 82.0 all-gather.25
  361.2 80.5 all-gather.27
  443.1 80.9 all-gather.29
  532.7 58.9 all-reduce.16
  624.4 60.7 all-reduce.18
  687.4 38.5 all-gather.31
  728.0 38.3 all-gather.33
  769.1 34.0 reduce-scatter.14
  807.4 59.0 all-reduce.20
  868.6 50.5 reduce-scatter.22
  921.9 34.5 reduce-scatter.8
  959.4 34.6 reduce-scatter.10
  996.8 34.6 reduce-scatter.12
  1033.8 88.0 reduce-scatter.16
  1124.2 87.9 reduce-scatter.18
  1214.5 87.9 reduce-scatter.20
where the time goes:
time: 1320 us; the launch traced here: 1310 us
  waiting for transfers between devices  922 us (70%)
  matrix products  179 us (14%)
  blocking collectives  118 us (9%)
  other arithmetic  59 us (4%)
  between operations  17 us (1%)
  local copies, waits for them, and re-layouts  15.3 us (1%)
    reduce_scatter x1, waiting for transfers between devices, local(): lax.psum_scatter(grad_gate_w.astype(jnp.bfloat16), 'fsdp', scatter_dimens...  88.5 us
    reduce_scatter x1, waiting for transfers between devices, local(): lax.psum_scatter(grad_down_w.astype(jnp.bfloat16), 'fsdp', scatter_dimens...  87.5 us
    reduce_scatter x1, waiting for transfers between devices, local(): lax.psum_scatter(grad_up_w.astype(jnp.bfloat16), 'fsdp', scatter_dimensio...  87.5 us
    all_gather x1, waiting for transfers between devices, local(): lax.all_gather(w_gate, 'fsdp', axis=0, tiled=True)  77.7 us
    all_gather x1, waiting for transfers between devices, local(): lax.all_gather(w_up, 'fsdp', axis=0, tiled=True)  73.2 us
    all_gather x1, waiting for transfers between devices, local(): lax.all_gather(w_down, 'fsdp', axis=1, tiled=True)  72 us
    psum x1, waiting for transfers between devices, local(): lax.psum(mlp_back_in.astype(jnp.bfloat16), 'tp').astype(jnp.float32)  60.1 us
    psum x1, waiting for transfers between devices, local(): lax.psum(jnp.einsum('rsf,fd->rsd', mixed_low, mlp_set[2], preferred_eleme...  48.9 us
  transfers between devices with their start and end apart: 23, of which 20 were waited for; matrix products, arithmetic and copies ran while one was open for 15% of the time, Pallas kernels for 0%

commit v1 on v0

--- a/solution.py
+++ b/solution.py
@@ -3,6 +3,7 @@
 import jax
 import jax.numpy as jnp
 from jax import lax
+from jax.experimental import pallas as pl
 from jax.sharding import PartitionSpec as P
 
 HEAD_DIM = 128
@@ -404,6 +405,544 @@
     )
 
 
+def attend_kernel(q_ref, kv_ref, qpos_ref, kpos_ref, ks_ref, out_ref, lse_ref):
+    width = q_ref.shape[-1]
+    head_of = (lax.broadcasted_iota(jnp.int32, (1, width), 1) // 64) % 2
+    query = q_ref[0]
+    qpos = qpos_ref[...]
+    parts = kv_ref.shape[0]
+    scaling = HEAD_DIM ** (-0.5)
+    total = jnp.zeros(query.shape, jnp.float32)
+    logs = []
+    for head in range(2):
+        picked = jnp.where(head_of == head, query, jnp.zeros_like(query))
+        scores = []
+        for part in range(parts):
+            raw = lax.dot_general(
+                picked,
+                kv_ref[part, 0, :, :width],
+                (((1,), (1,)), ((), ())),
+                preferred_element_type=jnp.float32,
+            )
+            scaled = raw * (ks_ref[part, 0] * scaling)
+            scores.append(jnp.where(kpos_ref[part] <= qpos, scaled, -1e30))
+        peak = jnp.max(scores[0], axis=1, keepdims=True)
+        for part in range(1, parts):
+            peak = jnp.maximum(peak, jnp.max(scores[part], axis=1, keepdims=True))
+        sums = jnp.zeros_like(peak)
+        for part in range(parts):
+            scores[part] = jnp.exp(scores[part] - peak)
+            sums = sums + jnp.sum(scores[part], axis=1, keepdims=True)
+        inverse = 1.0 / sums
+        attended = jnp.zeros(query.shape, jnp.float32)
+        for part in range(parts):
+            attended = attended + jnp.dot(
+                (scores[part] * inverse).astype(jnp.bfloat16),
+                kv_ref[part, 0, :, width:],
+                preferred_element_type=jnp.float32,
+            )
+        total = jnp.where(head_of == head, attended, total)
+        logs.append(peak + jnp.log(sums))
+    out_ref[0] = total
+    lse_ref[0] = jnp.concatenate(logs, axis=1)
+
+
+def attend_back_kernel(
+    q_ref, kv_ref, grad_ref, out_ref, lse_ref, qpos_ref, kpos_ref, ks_ref, dq_ref, dkv_ref
+):
+    width = q_ref.shape[-1]
+    head_of = (lax.broadcasted_iota(jnp.int32, (1, width), 1) // 64) % 2
+    query = q_ref[0]
+    grad = grad_ref[0]
+    qpos = qpos_ref[...]
+    parts = kv_ref.shape[0]
+    scaling = HEAD_DIM ** (-0.5)
+    product = grad.astype(jnp.float32) * out_ref[0]
+    zero = jnp.zeros_like(query)
+    queries = [jnp.where(head_of == head, query, zero) for head in range(2)]
+    grads = [jnp.where(head_of == head, grad, zero) for head in range(2)]
+    deltas = [
+        jnp.sum(jnp.where(head_of == head, product, 0.0), axis=1, keepdims=True)
+        for head in range(2)
+    ]
+    totals = [jnp.zeros(query.shape, jnp.float32) for _ in range(2)]
+    for part in range(parts):
+        key = kv_ref[part, 0, :, :width]
+        value = kv_ref[part, 0, :, width:]
+        visible = kpos_ref[part] <= qpos
+        key_scale = ks_ref[part, 0]
+        grad_key = []
+        grad_value = []
+        for head in range(2):
+            raw = lax.dot_general(
+                queries[head], key, (((1,), (1,)), ((), ())), preferred_element_type=jnp.float32
+            )
+            scaled = raw * (key_scale * scaling)
+            prob = jnp.where(visible, jnp.exp(scaled - lse_ref[0, :, head : head + 1]), 0.0)
+            grad_value.append(
+                lax.dot_general(
+                    prob.astype(jnp.bfloat16),
+                    grad,
+                    (((0,), (0,)), ((), ())),
+                    preferred_element_type=jnp.float32,
+                )
+            )
+            grad_prob = lax.dot_general(
+                grads[head], value, (((1,), (1,)), ((), ())), preferred_element_type=jnp.float32
+            )
+            grad_scores = (prob * (grad_prob - deltas[head]) * key_scale).astype(jnp.bfloat16)
+            totals[head] = totals[head] + jnp.dot(
+                grad_scores, key, preferred_element_type=jnp.float32
+            )
+            grad_key.append(
+                lax.dot_general(
+                    grad_scores,
+                    query,
+                    (((0,), (0,)), ((), ())),
+                    preferred_element_type=jnp.float32,
+                )
+            )
+        dkv_ref[part, 0, :, :width] = (
+            jnp.where(head_of == 0, grad_key[0], grad_key[1]) * scaling
+        ).astype(jnp.bfloat16)
+        dkv_ref[part, 0, :, width:] = jnp.where(head_of == 0, grad_value[0], grad_value[1]).astype(
+            jnp.bfloat16
+        )
+    dq_ref[0] = jnp.where(head_of == 0, totals[0], totals[1]) * scaling
+
+
+def attention_specs(rows, parts, count, width):
+    row = pl.BlockSpec((1, count, width), lambda r: (r, 0, 0))
+    both = pl.BlockSpec((parts, 1, count, 2 * width), lambda r: (0, r, 0, 0))
+    qpos = pl.BlockSpec((count, 1), lambda r: (0, 0))
+    kpos = pl.BlockSpec((parts, 1, count), lambda r: (0, 0, 0))
+    scale = pl.BlockSpec((parts, 1, 1, count), lambda r: (0, r, 0, 0))
+    logs = pl.BlockSpec((1, count, 2), lambda r: (r, 0, 0))
+    return row, both, qpos, kpos, scale, logs
+
+
+def attend_tiles(query, both, qpos, kpos, key_scale):
+    rows, count, width = query.shape
+    parts = both.shape[0]
+    row, pair, qspec, kspec, scale, logs = attention_specs(rows, parts, count, width)
+    return pl.pallas_call(
+        attend_kernel,
+        grid=(rows,),
+        in_specs=[row, pair, qspec, kspec, scale],
+        out_specs=[row, logs],
+        out_shape=[
+            jax.ShapeDtypeStruct((rows, count, width), jnp.float32),
+            jax.ShapeDtypeStruct((rows, count, 2), jnp.float32),
+        ],
+        name="attend",
+    )(query, both, qpos, kpos, key_scale)
+
+
+def attend_back_tiles(query, both, grad, attended, log_total, qpos, kpos, key_scale):
+    rows, count, width = query.shape
+    parts = both.shape[0]
+    row, pair, qspec, kspec, scale, logs = attention_specs(rows, parts, count, width)
+    return pl.pallas_call(
+        attend_back_kernel,
+        grid=(rows,),
+        in_specs=[row, pair, row, row, logs, qspec, kspec, scale],
+        out_specs=[row, pair],
+        out_shape=[
+            jax.ShapeDtypeStruct((rows, count, width), jnp.float32),
+            jax.ShapeDtypeStruct(both.shape, jnp.bfloat16),
+        ],
+        name="attend_back",
+    )(query, both, grad, attended, log_total, qpos, kpos, key_scale)
+
+
+def swap(value, axis, bit):
+    size = lax.axis_size(axis)
+    return lax.ppermute(value, axis, [(i, i ^ bit) for i in range(size)])
+
+
+def spread(blocks, axis):
+    return lax.all_to_all(blocks, axis, split_axis=0, concat_axis=0, tiled=True)
+
+
+def share(value, axis):
+    size = lax.axis_size(axis)
+    return spread(jnp.broadcast_to(value[None], (size,) + value.shape), axis)
+
+
+def gather_tp(piece, first):
+    one = swap(piece, "tp", 1)
+    two = swap(piece, "tp", 2)
+    three = swap(one, "tp", 2) if first == 1 else swap(two, "tp", 1)
+    return (piece, one, two, three)
+
+
+def scatter_tp(keep, send, second, axis):
+    first = 3 - second
+    merged = keep + swap(send.astype(jnp.bfloat16), "tp", first).astype(jnp.float32)
+    mine, other = jnp.split(merged, 2, axis=axis)
+    return mine + swap(other.astype(jnp.bfloat16), "tp", second).astype(jnp.float32)
+
+
+def arrival_rows(weight, chips):
+    width = weight.shape[-1]
+    view = weight.reshape(2, 2, chips, 2, 64, width).transpose(2, 0, 3, 1, 4, 5)
+    return jnp.stack([view[:, 0], view[:, 1, ::-1]], axis=1).reshape(-1, width)
+
+
+def natural_rows(grad, chips):
+    width = grad.shape[-1]
+    view = grad.reshape(chips, 2, 2, 2, 64, width)
+    view = jnp.stack([view[:, 0], view[:, 1, ::-1]], axis=1)
+    return view.transpose(1, 3, 0, 2, 4, 5).reshape(2 * 2, -1, width)
+
+
+def matmul(lhs, rhs, dims):
+    return lax.dot_general(lhs, rhs, (dims, ((), ())), preferred_element_type=jnp.float32)
+
+
+def local_fast(
+    tokens,
+    cotangent,
+    w_query,
+    w_key,
+    w_value,
+    w_out,
+    query_gain,
+    key_gain,
+    attn_gain,
+    w_gate,
+    w_up,
+    w_down,
+    mlp_gain,
+    group_ids,
+    span_order,
+):
+    low = jnp.bfloat16
+    batch_rows, local_len, width = tokens.shape
+    members = lax.axis_size("fsdp")
+    parts = lax.axis_size("tp")
+    chips = members // 2
+    member = lax.axis_index("fsdp")
+    part = lax.axis_index("tp")
+    core = member % 2
+    span_len = local_len // 2
+    sub = local_len // parts
+    count = members * sub
+    tile = batch_rows * count
+    pair = 2 * HEAD_DIM
+    bundle = 4 * 64
+    rows_local = w_query.shape[0]
+    unit = w_gate.shape[1] // members
+
+    own_tokens = lax.dynamic_slice_in_dim(tokens, part * sub, sub, axis=1)
+    own_cotangent = lax.dynamic_slice_in_dim(cotangent, part * sub, sub, axis=1)
+
+    def halves(weight):
+        return weight.reshape(rows_local, members, 64)
+
+    packed = jnp.concatenate(
+        [halves(w_query), halves(w_key), halves(w_value), jnp.zeros_like(halves(w_value))], axis=2
+    ).transpose(1, 0, 2)
+    packed = spread(packed, "fsdp").reshape(width, bundle)
+    gain_row = jnp.concatenate(
+        [query_gain, key_gain, jnp.zeros((bundle - 2 * 64,), query_gain.dtype)]
+    )
+    packed = jnp.concatenate(
+        [packed, jnp.broadcast_to(gain_row[None], (16, bundle)).astype(packed.dtype)], axis=0
+    )
+    token_low = lax.all_gather(own_tokens.astype(low), "fsdp", axis=1, tiled=True)
+    packed = share(packed, "tp")
+    own_half = lax.dynamic_slice_in_dim(packed, 2 * core, 2, axis=0)
+    other_half = swap(lax.dynamic_slice_in_dim(packed, 2 - 2 * core, 2, axis=0), "fsdp", 1)
+
+    norm_gains = jnp.concatenate(
+        [attn_gain[None], mlp_gain[None], jnp.zeros((14, attn_gain.shape[0]), attn_gain.dtype)]
+    )
+    out_rows = lax.all_gather(
+        jnp.concatenate([w_out, norm_gains.astype(w_out.dtype)], axis=0),
+        "fsdp",
+        axis=1,
+        tiled=True,
+    )
+    gain_attn = out_rows[w_out.shape[0]].astype(jnp.float32)
+    gain_mlp = out_rows[w_out.shape[0] + 1].astype(jnp.float32)
+    out_full = lax.all_gather(out_rows[: w_out.shape[0]], "tp", axis=0, tiled=True)
+    out_full = arrival_rows(out_full, chips)
+
+    def columns(weight):
+        return weight.reshape(rows_local, members, unit).transpose(1, 0, 2)
+
+    gate_up = spread(jnp.stack([columns(w_gate), columns(w_up)], axis=1), "fsdp")
+    down = spread(w_down.reshape(members, unit, rows_local), "fsdp")
+    gate_all = jnp.concatenate(gather_tp(gate_up[:, 0].reshape(width, unit), 1), axis=1)
+    up_all = jnp.concatenate(gather_tp(gate_up[:, 1].reshape(width, unit), 2), axis=1)
+    down_all = jnp.concatenate(
+        gather_tp(down.transpose(1, 0, 2).reshape(unit, width), 1), axis=0
+    )
+
+    index = jnp.arange(members, dtype=jnp.int32)[:, None] * local_len
+    index = (index + jnp.arange(sub, dtype=jnp.int32)[None, :]).reshape(count)
+    index = index[None, :] + jnp.arange(parts, dtype=jnp.int32)[:, None] * sub
+    spans = jnp.arange(span_order.shape[0], dtype=jnp.int32)
+    picked = jnp.sum(
+        jnp.where((index // span_len)[..., None] == spans, span_order, 0), axis=-1
+    )
+    all_pos = picked * span_len + index % span_len
+    query_pos = lax.dynamic_index_in_dim(all_pos, part, axis=0, keepdims=False)
+    inv_freq = jnp.power(
+        rope_base, -(jnp.arange(64, dtype=jnp.float32) * 2.0 / HEAD_DIM)
+    )
+    angles = query_pos.astype(jnp.float32)[:, None] * jnp.tile(inv_freq, 2)[None, :]
+    cosine = jnp.cos(angles)[None]
+    sine = (jnp.where(core == 0, 1.0, -1.0) * jnp.sin(angles))[None]
+
+    def rotate(value, direction):
+        own, other = value[..., :HEAD_DIM], value[..., HEAD_DIM:]
+        turned = direction * sine
+        return jnp.concatenate(
+            [own * cosine - other * turned, other * cosine + own * turned], axis=-1
+        )
+
+    weight_pieces = [own_half[0], own_half[1], other_half[0], other_half[1]]
+    acts = [
+        matmul(token_low, piece[:width], ((2,), (0,))) for piece in weight_pieces
+    ]
+
+    def lanes(pieces, at):
+        return jnp.concatenate([piece[..., at * 64 : at * 64 + 64] for piece in pieces], axis=-1)
+
+    queries, keys, values = (lanes(acts, at) for at in range(3))
+    gain_rows = [piece[width].astype(jnp.float32) for piece in weight_pieces]
+    gain_query, gain_key = lanes(gain_rows, 0), lanes(gain_rows, 1)
+    key_low = rotate(keys * gain_key, 1.0).astype(low)
+    both = share(jnp.concatenate([key_low, values.astype(low)], axis=-1), "tp")
+    square_sums = lax.psum(
+        jnp.stack([jnp.sum(queries * queries, axis=-1), jnp.sum(keys * keys, axis=-1)]), "fsdp"
+    )
+    scales = lax.rsqrt(square_sums / width + epsilon)
+    query_scale, key_scale = scales[0][..., None], scales[1][..., None]
+    all_key_scale = share(scales[1], "tp").reshape(parts, batch_rows, 1, count)
+    query_low = rotate(queries * query_scale * gain_query, 1.0).astype(low)
+    qpos = query_pos[:, None]
+    kpos = all_pos[:, None, :]
+    attended, log_total = attend_tiles(query_low, both, qpos, kpos, all_key_scale)
+
+    def to_tokens(value):
+        blocks = value.reshape(batch_rows, members, sub, pair).transpose(1, 0, 2, 3)
+        return spread(blocks, "fsdp").transpose(1, 2, 0, 3).reshape(batch_rows, sub, members * pair)
+
+    def to_heads(value):
+        blocks = value.reshape(batch_rows, sub, members, pair).transpose(2, 0, 1, 3)
+        return spread(blocks, "fsdp").transpose(1, 0, 2, 3).reshape(batch_rows, count, pair)
+
+    attended_low = attended.astype(low)
+    branch_attn = matmul(to_tokens(attended_low), out_full, ((2,), (0,)))
+    attn_norm = lax.rsqrt(jnp.mean(branch_attn * branch_attn, axis=-1, keepdims=True) + epsilon)
+    hidden = own_tokens + branch_attn * attn_norm * gain_attn
+    hidden_low = lax.all_gather(hidden.astype(low), "fsdp", axis=1, tiled=True)
+
+    gate_act = matmul(hidden_low, gate_all, ((2,), (0,)))
+    up_act = matmul(hidden_low, up_all, ((2,), (0,)))
+    gate_sigma = jax.nn.sigmoid(gate_act)
+    mixed_low = (gate_act * gate_sigma * up_act).astype(low)
+    branch_mlp = lax.psum_scatter(
+        matmul(mixed_low, down_all, ((2,), (0,))).astype(low),
+        "fsdp",
+        scatter_dimension=1,
+        tiled=True,
+    ).astype(jnp.float32)
+    mlp_norm = lax.rsqrt(jnp.mean(branch_mlp * branch_mlp, axis=-1, keepdims=True) + epsilon)
+    layer_own = hidden + branch_mlp * mlp_norm * gain_mlp
+
+    def whole_span(value):
+        gathered = share(value.astype(low), "tp").astype(jnp.float32)
+        return gathered.transpose(1, 0, 2, 3).reshape(batch_rows, local_len, width)
+
+    grad_gain_mlp, grad_branch_mlp = norm_back(branch_mlp, mlp_norm, gain_mlp, own_cotangent)
+    grad_mlp_low = lax.all_gather(grad_branch_mlp.astype(low), "fsdp", axis=1, tiled=True)
+    layer_out = whole_span(layer_own)
+    grad_mixed = matmul(grad_mlp_low, down_all, ((2,), (1,)))
+    grad_gate_act = (
+        grad_mixed * up_act * gate_sigma * (1.0 + gate_act * (1.0 - gate_sigma))
+    ).astype(low)
+    grad_up_act = (grad_mixed * gate_act * gate_sigma).astype(low)
+    mlp_back_in = matmul(grad_gate_act, gate_all, ((2,), (1,))) + matmul(
+        grad_up_act, up_all, ((2,), (1,))
+    )
+    grad_hidden = own_cotangent + lax.psum_scatter(
+        mlp_back_in.astype(low), "fsdp", scatter_dimension=1, tiled=True
+    ).astype(jnp.float32)
+
+    hidden_flat = hidden_low.reshape(tile, width)
+    grad_flat = grad_mlp_low.reshape(tile, width)
+
+    def block_pair(value, a, b):
+        flat = value.reshape(tile, -1)
+        return jnp.concatenate(
+            [flat[:, a * unit : (a + 1) * unit], flat[:, b * unit : (b + 1) * unit]], axis=1
+        )
+
+    grad_down_w = scatter_tp(
+        matmul(block_pair(mixed_low, 0, 2), grad_flat, ((0,), (0,))),
+        matmul(block_pair(mixed_low, 1, 3), grad_flat, ((0,), (0,))),
+        2,
+        0,
+    )
+    grad_gate_w = scatter_tp(
+        matmul(hidden_flat, block_pair(grad_gate_act, 0, 1), ((0,), (0,))),
+        matmul(hidden_flat, block_pair(grad_gate_act, 2, 3), ((0,), (0,))),
+        1,
+        1,
+    )
+    grad_up_w = scatter_tp(
+        matmul(hidden_flat, block_pair(grad_up_act, 0, 2), ((0,), (0,))),
+        matmul(hidden_flat, block_pair(grad_up_act, 1, 3), ((0,), (0,))),
+        2,
+        1,
+    )
+    down_back = spread(
+        grad_down_w.astype(low).reshape(unit, members, rows_local).transpose(1, 0, 2), "fsdp"
+    )
+    grad_down = down_back.reshape(members * unit, rows_local).astype(jnp.float32)
+
+    def unit_columns(value):
+        blocks = spread(value.astype(low).reshape(members, rows_local, unit), "fsdp")
+        return blocks.transpose(1, 0, 2).reshape(rows_local, members * unit).astype(jnp.float32)
+
+    grad_gate = unit_columns(grad_gate_w)
+    grad_up = unit_columns(grad_up_w)
+
+    grad_gain_attn, grad_branch_attn = norm_back(branch_attn, attn_norm, gain_attn, grad_hidden)
+    grad_attn_low = grad_branch_attn.astype(low)
+    grad_attended = to_heads(matmul(grad_attn_low, out_full, ((2,), (1,))).astype(low))
+    feature_blocks = jnp.concatenate(
+        [
+            grad_attn_low.reshape(batch_rows * sub, width),
+            grad_gain_attn[None].astype(low),
+            grad_gain_mlp[None].astype(low),
+            jnp.zeros((14, width), low),
+        ],
+        axis=0,
+    )
+    feature_blocks = spread(
+        feature_blocks.reshape(-1, members, rows_local).transpose(1, 0, 2), "fsdp"
+    )
+    own_features = feature_blocks[:, : batch_rows * sub].reshape(
+        members, batch_rows, sub, rows_local
+    )
+    gain_sums = jnp.sum(
+        feature_blocks[:, batch_rows * sub :].astype(jnp.float32), axis=0
+    )
+    attended_all = lax.all_gather(attended_low, "fsdp", axis=2, tiled=True)
+    own_features = own_features.transpose(1, 0, 2, 3).reshape(batch_rows, count, rows_local)
+    in_group = (group_ids[:, 0][:, None] == jnp.arange(GROUPS, dtype=jnp.int32)[None, :]).astype(
+        low
+    )
+    out_blocks = []
+    for group in range(GROUPS):
+        masked = own_features * in_group[:, group][:, None, None]
+        product = matmul(
+            attended_all.reshape(tile, -1), masked.reshape(tile, rows_local), ((0,), (0,))
+        )
+        out_blocks.append(natural_rows(product.astype(low), chips))
+    out_blocks.append(
+        jnp.broadcast_to(gain_sums.astype(low)[None], (parts,) + gain_sums.shape)
+    )
+    out_sum = jnp.sum(spread(jnp.concatenate(out_blocks, axis=1), "tp").astype(jnp.float32), axis=0)
+    block_rows = w_out.shape[0]
+    grad_out_groups = out_sum[: GROUPS * block_rows].reshape(GROUPS, block_rows, rows_local)
+    grad_out = jnp.sum(grad_out_groups, axis=0)
+    grad_attn_gain = out_sum[GROUPS * block_rows]
+    grad_mlp_gain = out_sum[GROUPS * block_rows + 1]
+
+    grad_query_rot, grad_both = attend_back_tiles(
+        query_low, both, grad_attended, attended, log_total, qpos, kpos, all_key_scale
+    )
+    grad_both = jnp.sum(spread(grad_both, "tp").astype(jnp.float32), axis=0)
+    grad_qn = rotate(grad_query_rot, -1.0)
+    grad_kn = rotate(grad_both[..., :pair], -1.0)
+    gained_query = grad_qn * gain_query
+    gained_key = grad_kn * gain_key
+    cross_sums = lax.psum(
+        jnp.stack(
+            [jnp.sum(queries * gained_query, axis=-1), jnp.sum(keys * gained_key, axis=-1)]
+        ),
+        "fsdp",
+    )
+    grad_gain_query = jnp.sum(grad_qn * queries * query_scale, axis=(0, 1))
+    grad_gain_key = jnp.sum(grad_kn * keys, axis=(0, 1))
+    grad_queries = (
+        query_scale * gained_query - queries * query_scale**3 * cross_sums[0][..., None] / width
+    ).astype(low)
+    grad_keys = (
+        gained_key - keys * key_scale**2 * cross_sums[1][..., None] / width
+    ).astype(low)
+    grad_values = grad_both[..., pair:].astype(low)
+    grad_acts = [
+        jnp.concatenate(
+            [
+                value[..., at * 64 : at * 64 + 64]
+                for value in (grad_queries, grad_keys, grad_values, jnp.zeros_like(grad_values))
+            ],
+            axis=-1,
+        )
+        for at in range(4)
+    ]
+    attn_back_in = sum(
+        matmul(grad, piece[:width], ((2,), (1,))) for grad, piece in zip(grad_acts, weight_pieces)
+    )
+    input_own = grad_hidden + lax.psum_scatter(
+        attn_back_in.astype(low), "fsdp", scatter_dimension=1, tiled=True
+    ).astype(jnp.float32)
+    input_grad = whole_span(input_own)
+
+    token_flat = token_low.reshape(tile, width)
+
+    def with_gain(at):
+        product = matmul(token_flat, grad_acts[at].reshape(tile, bundle), ((0,), (0,)))
+        gains = jnp.concatenate(
+            [
+                grad_gain_query[at * 64 : at * 64 + 64],
+                grad_gain_key[at * 64 : at * 64 + 64],
+                jnp.zeros((bundle - 2 * 64,), jnp.float32),
+            ]
+        )
+        return jnp.concatenate(
+            [product.astype(low), jnp.broadcast_to(gains[None], (16, bundle)).astype(low)], axis=0
+        )
+
+    sent = swap(jnp.stack([with_gain(2), with_gain(3)]), "fsdp", 1)
+    kept = jnp.stack([with_gain(0), with_gain(1)])
+    proj_blocks = jnp.where(
+        core == 0, jnp.concatenate([kept, sent]), jnp.concatenate([sent, kept])
+    )
+    proj_sum = jnp.sum(spread(proj_blocks, "tp").astype(jnp.float32), axis=0)
+    grad_query_gain = proj_sum[width, :64]
+    grad_key_gain = proj_sum[width, 64:128]
+    proj_back = spread(proj_sum[:width].astype(low).reshape(members, rows_local, bundle), "fsdp")
+
+    def natural_columns(at):
+        block = proj_back[:, :, at * 64 : at * 64 + 64].astype(jnp.float32)
+        return block.transpose(1, 0, 2).reshape(rows_local, members * 64)
+
+    return (
+        layer_out,
+        input_grad,
+        natural_columns(0),
+        natural_columns(1),
+        natural_columns(2),
+        grad_out,
+        grad_query_gain,
+        grad_key_gain,
+        grad_attn_gain,
+        grad_gate,
+        grad_up,
+        grad_down,
+        grad_mlp_gain,
+        grad_out_groups,
+    )
+
+
 def solution(mesh):
     in_specs = (
         P(None, "fsdp", None),
@@ -438,4 +977,8 @@
         P("fsdp"),
         P(None, "tp", "fsdp"),
     )
-    return jax.shard_map(local, mesh=mesh, in_specs=in_specs, out_specs=out_specs, check_vma=False)
+    heads = 2048 // HEAD_DIM
+    members, parts = mesh.shape["fsdp"], mesh.shape["tp"]
+    fits = parts == 4 and heads // parts * 2 == members
+    body = local_fast if fits else local
+    return jax.shard_map(body, mesh=mesh, in_specs=in_specs, out_specs=out_specs, check_vma=False)

time: 1320 us -> 1070 us (0.81)
  waiting for transfers between devices: 922 us -> 583 us
  starting transfers between devices: 1.51 us -> 89.9 us
  local copies, waits for them, and re-layouts: 15.3 us -> 97.7 us
  matrix products: 179 us -> 113 us
  blocking collectives: 118 us -> 55.5 us
  other arithmetic: 59 us -> 77.2 us
  Pallas kernels: 0 us -> 17.8 us
    all_to_all x0 -> x17, waiting for transfers between devices: none -> 351 us  [spread(): return lax.all_to_all(blocks, axis, split_axis=0, concat_axis=0, tiled=True)]
    all_gather x11 -> x6, waiting for transfers between devices: 378 us -> 37.5 us  [the longest x1 37.5 us: local_fast(): lax.all_gather(grad_branch_mlp.astype(low), 'fsdp', axis=1, tiled=True)]
    reduce_scatter x8 -> x3, waiting for transfers between devices: 384 us -> 60.4 us  [the longest x1 38.4 us: local_fast(): lax.psum_scatter(matmul(mixed_low, down_all, ((2,), (0,))).astype(low), '...]
    psum x4 -> x0, waiting for transfers between devices: 155 us -> none  [the longest x1 60.1 us: local(): lax.psum(mlp_back_in.astype(jnp.bfloat16), 'tp').astype(jnp.float32)]
    ppermute x0 -> x17, waiting for transfers between devices: none -> 134 us  [swap(): return lax.ppermute(value, axis, [(i, i ^ bit) for i in range(size)])]
    all_to_all x0 -> x17, starting transfers between devices: none -> 72.3 us  [spread(): return lax.all_to_all(blocks, axis, split_axis=0, concat_axis=0, tiled=True)]
    dot_general x27 -> x28, matrix products: 179 us -> 113 us  [matmul(): lax.dot_general(lhs, rhs, (dims, ((), ())), preferred_element_type=jnp.fl...]
    all_gather x4 -> x0, blocking collectives: 50.7 us -> none  [the longest x1 15.3 us: local(): lax.all_gather(lse_rows, 'fsdp', axis=1, tiled=True)]
  transfers between devices with their start and end apart: 23 -> 43, of which waited for: 20 -> 25; matrix products, arithmetic and copies ran while one was open for 15% -> 23% of each run, Pallas kernels for 0% -> 2%
where the time goes in v1:
time: 1070 us; the launch traced here: 1050 us
  waiting for transfers between devices  583 us (54%)
  matrix products  113 us (11%)
  local copies, waits for them, and re-layouts  97.7 us (9%)
  starting transfers between devices  89.9 us (8%)
  other arithmetic  77.2 us (7%)
  blocking collectives  55.5 us (5%)
  Pallas kernels  17.8 us (2%)
  between operations  15.6 us (1%)
    all_to_all x17, waiting for transfers between devices, spread(): return lax.all_to_all(blocks, axis, split_axis=0, concat_axis=0, tiled=True)  351 us
    ppermute x17, waiting for transfers between devices, swap(): return lax.ppermute(value, axis, [(i, i ^ bit) for i in range(size)])  134 us
    dot_general x28, matrix products, matmul(): lax.dot_general(lhs, rhs, (dims, ((), ())), preferred_element_type=jnp.fl...  113 us
    all_to_all x17, starting transfers between devices, spread(): return lax.all_to_all(blocks, axis, split_axis=0, concat_axis=0, tiled=True)  72.3 us
    reduce_scatter x1, waiting for transfers between devices, local_fast(): lax.psum_scatter(matmul(mixed_low, down_all, ((2,), (0,))).astype(low), '...  38.4 us
    all_gather x1, waiting for transfers between devices, local_fast(): lax.all_gather(grad_branch_mlp.astype(low), 'fsdp', axis=1, tiled=True)  37.5 us
    psum x1, blocking collectives, local_fast(): lax.psum(jnp.stack([jnp.sum(queries * gained_query, axis=-1), jnp.sum(key...  25.8 us
    unnamed x193, local copies, waits for them, and re-layouts  22.8 us
  transfers between devices with their start and end apart: 43, of which 25 were waited for; matrix products, arithmetic and copies ran while one was open for 23% of the time, Pallas kernels for 2%

profile of v1, /device:TPU:0, one launch (start us, length us, event | category | flops | bytes accessed | tf_op | source)
XLA Modules:
  0.0 1049.2 jit_solution(882122673584632876)
XLA Ops:
  17.2 6.4 all-to-all-start
  24.2 40.8 %all-to-all-done = bf16[8,256,256]{1,2,0:T(8,128)(2,1)S(1)} async-done(((bf16[8,256,256]{1,2,0:T(8,128)(2,1)}), bf16[8,256,256]{1,2,0:T(8,128)(2,1)S(1)}, u32[]{:S(2)}, u32[]{:S(2)}) %all-to-all-start) | async-done | bytes 1048608 | tf_op jit(solution)/shard_map/all_to_all | solution.py:564
  71.2 5.0 all-to-all-start.1
  76.6 56.8 %all-to-all-done.1 = bf16[4,2064,256]{2,1,0:T(8,128)(2,1)} async-done(((bf16[4,2064,256]{2,1,0:T(8,128)(2,1)}), bf16[4,2064,256]{2,1,0:T(8,128)(2,1)}, u32[]{:S(2)}, u32[]{:S(2)}) %all-to-all-start.1) | async-done | bytes 4227104 | tf_op jit(solution)/shard_map/all_to_all | solution.py:564
  152.9 14.3 %psum.14 = f32[2,3,256]{2,1,0:T(4,128)S(1)} all-reduce(f32[2,3,256]{2,1,0:T(4,128)S(1)} %pad_maximum_fusion.12), channel_id=1, replica_groups=mesh['fsdp'=8,'tp'=4] {'fsdp'}, use_global_device_ids=true, to_apply=%region_2.3 | all-reduce | flops 1536 | bytes 12288 | tf_op jit(solution)/shard_map/psum | solution.py:719
  178.0 3.7 all-to-all-start.2
  185.5 45.7 %all-to-all-done.2.kv_ref = bf16[4,3,256,512]{3,2,1,0:T(8,128)(2,1)S(1)} async-done(((bf16[4,3,256,512]{3,2,1,0:T(8,128)(2,1)}), bf16[4,3,256,512]{3,2,1,0:T(8,128)(2,1)S(1)}, u32[]{:S(2)}, u32[]{:S(2)}) %all-to-all-start.2) | async-done | bytes 3145760 | tf_op jit(solution)/shard_map/all_to_all | solution.py:564
  232.9 6.4 attend.1
  241.4 5.0 all-to-all-start.4
  254.4 4.4 all-to-all-done.4
  258.8 3.6 all-to-all-start.5
  263.6 8.4 copy.358
  271.9 6.2 fusion.98
  278.2 4.8 rev.9
  283.0 7.6 pad_maximum_fusion
  290.6 4.9 multiply_reduce_fusion.5
  298.3 17.8 %all-to-all-done.5 = bf16[8,2,256,256]{3,2,1,0:T(8,128)(2,1)S(1)} async-done(((bf16[8,2,256,256]{3,2,1,0:T(8,128)(2,1)}), bf16[8,2,256,256]{3,2,1,0:T(8,128)(2,1)S(1)}, u32[]{:S(2)}, u32[]{:S(2)}) %all-to-all-start.5) | async-done | bytes 2097184 | tf_op jit(solution)/shard_map/all_to_all | solution.py:564
  316.1 4.3 all-to-all-start.6
  323.3 35.9 %all-to-all-done.6 = bf16[8,256,256]{2,1,0:T(8,128)(2,1)} async-done(((bf16[8,256,256]{2,1,0:T(8,128)(2,1)}), bf16[8,256,256]{2,1,0:T(8,128)(2,1)}, u32[]{:S(2)}, u32[]{:S(2)}) %all-to-all-start.6) | async-done | bytes 1048608 | tf_op jit(solution)/shard_map/all_to_all | solution.py:564
  366.2 20.6 %collective-permute-done.7 = bf16[256,2048]{1,0:T(8,128)(2,1)} collective-permute-done((bf16[256,2048]{1,0:T(8,128)(2,1)S(1)}, bf16[256,2048]{1,0:T(8,128)(2,1)}, u32[]{:S(2)}, u32[]{:S(2)}) %collective-permute-start.7) | collective-permute-done | bytes 1048608 | tf_op jit(solution)/shard_map/ppermute | solution.py:560
  389.1 21.9 %collective-permute-done.3 = bf16[2048,256]{1,0:T(8,128)(2,1)} collective-permute-done((bf16[2048,256]{1,0:T(8,128)(2,1)S(1)}, bf16[2048,256]{1,0:T(8,128)(2,1)}, u32[]{:S(2)}, u32[]{:S(2)}) %collective-permute-start.3) | collective-permute-done | bytes 1048608 | tf_op jit(solution)/shard_map/ppermute | solution.py:560
  411.0 6.3 fusion.18
  417.3 13.6 %collective-permute-done.6 = bf16[2048,256]{1,0:T(8,128)(2,1)} collective-permute-done((bf16[2048,256]{1,0:T(8,128)(2,1)}, bf16[2048,256]{1,0:T(8,128)(2,1)}, u32[]{:S(2)}, u32[]{:S(2)}) %collective-permute-start.6) | collective-permute-done | bytes 1048608 | tf_op jit(solution)/shard_map/ppermute | solution.py:560
  430.9 7.4 multiply_convert_fusion.2
  438.3 16.5 %collective-permute-done.9 = bf16[256,2048]{1,0:T(8,128)(2,1)} collective-permute-done((bf16[256,2048]{1,0:T(8,128)(2,1)}, bf16[256,2048]{1,0:T(8,128)(2,1)}, u32[]{:S(2)}, u32[]{:S(2)}) %collective-permute-start.9) | collective-permute-done | bytes 1048608 | tf_op jit(solution)/shard_map/ppermute | solution.py:560
  454.7 7.0 convolution_convert_fusion
  461.8 38.4 %reduce-scatter.4.cloned.1.call-done = bf16[3,32,2048]{2,1,0:T(8,128)(2,1)} async-done(((bf16[3,256,2048]{2,1,0:T(8,128)(2,1)}), bf16[3,32,2048]{2,1,0:T(8,128)(2,1)}) %reduce-scatter.4.cloned.1.call-update) | async-done | bytes 393232 | tf_op jit(solution)/shard_map/reduce_scatter | solution.py:748
  504.4 37.5 %all-gather.15.cloned.1.call-done = bf16[3,256,2048]{2,1,0:T(8,128)(2,1)} async-done(((bf16[3,32,2048]{2,1,0:T(8,128)(2,1)}), bf16[3,256,2048]{2,1,0:T(8,128)(2,1)}) %all-gather.15.cloned.1.call-update) | async-done | bytes 3145744 | tf_op jit(solution)/shard_map/all_gather | solution.py:762
  541.9 8.4 multiply_convert_fusion.1
  550.3 6.4 fusion.16
  556.7 6.4 add_convert_fusion.1
  565.3 4.4 convolution_convert_fusion.3
  580.6 21.9 %reduce-scatter.6.cloned.1.call-done = bf16[3,32,2048]{2,1,0:T(8,128)(2,1)} async-done(((bf16[3,256,2048]{2,1,0:T(8,128)(2,1)}), bf16[3,32,2048]{2,1,0:T(8,128)(2,1)}) %reduce-scatter.6.cloned.1.call-update) | async-done | bytes 393232 | tf_op jit(solution)/shard_map/reduce_scatter | solution.py:772
  604.5 6.1 convolution_convert_fusion.4
  610.6 15.3 %all_to_all.90 = bf16[8,3,32,256]{3,2,1,0:T(8,128)(2,1)S(1)} all-to-all(bf16[8,3,32,256]{3,2,1,0:T(8,128)(2,1)S(1)} %bitcast.294), channel_id=1, replica_groups=mesh['fsdp'=8,'tp'=4] {'fsdp'}, dimensions={0} | all-to-all | bytes 786432 | tf_op jit(solution)/shard_map/all_to_all | solution.py:564
  626.7 11.3 %attend_back.1 = (f32[3,256,256]{2,1,0:T(8,128)}, bf16[4,3,256,512]{3,2,1,0:T(8,128)(2,1)}) custom-call(bf16[3,256,256]{2,1,0:T(8,128)(2,1)} %pad_maximum_fusion.11.q_ref, bf16[4,3,256,512]{3,2,1,0:T(8,128)(2,1)} %copy-done, bf16[3,256,256]{2,1,0:T(8,128)(2,1)} %bitcast.293, f32[3,256,256]{2,1,0:T(8,128)} %get-tuple-element.18.out_ref, ...), custom_call_target="tpu_custom_call" | custom-call | tf_op jit(solution)/shard_map/attend_back/pallas_call | solution.py:545
  638.1 3.9 all-to-all-start.9
  642.6 4.9 convert_add_fusion.2
  649.7 3.6 convert_add_fusion.1
  656.1 13.0 %collective-permute-done.15 = bf16[512,2048]{1,0:T(8,128)(2,1)} collective-permute-done((bf16[512,2048]{1,0:T(8,128)(2,1)}, bf16[512,2048]{1,0:T(8,128)(2,1)}, u32[]{:S(2)}, u32[]{:S(2)}) %collective-permute-start.15) | collective-permute-done | bytes 2097184 | tf_op jit(solution)/shard_map/ppermute | solution.py:560
  669.1 3.5 convert_add_fusion
  676.3 47.9 %collective-permute-done.12 = bf16[2048,256]{1,0:T(8,128)(2,1)S(1)} collective-permute-done((bf16[2048,256]{1,0:T(8,128)(2,1)S(1)}, bf16[2048,256]{1,0:T(8,128)(2,1)S(1)}, u32[]{:S(2)}, u32[]{:S(2)}) %collective-permute-start.12) | collective-permute-done | bytes 1048608 | tf_op jit(solution)/shard_map/ppermute | solution.py:560
  725.6 4.3 all-to-all-start.15
  734.2 25.8 %psum.15 = f32[2,3,256]{2,1,0:T(4,128)} all-reduce(f32[2,3,256]{2,1,0:T(4,128)} %pad_maximum_fusion.13), channel_id=1, replica_groups=mesh['fsdp'=8,'tp'=4] {'fsdp'}, use_global_device_ids=true, to_apply=%region_13.14 | all-reduce | flops 1536 | bytes 12288 | tf_op jit(solution)/shard_map/psum | solution.py:866
  770.8 4.2 add_convert_fusion
  782.6 5.7 all-to-all-start.16
  797.6 34.5 %all-to-all-done.16 = bf16[8,256,256]{2,1,0:T(8,128)(2,1)S(1)} async-done(((bf16[8,256,256]{2,1,0:T(8,128)(2,1)}), bf16[8,256,256]{2,1,0:T(8,128)(2,1)S(1)}, u32[]{:S(2)}, u32[]{:S(2)}) %all-to-all-start.16) | async-done | bytes 1048608 | tf_op jit(solution)/shard_map/all_to_all | solution.py:564
  832.1 3.7 all-to-all-start.17
  840.3 4.0 maximum_select_fusion
  844.4 17.9 %all-to-all-done.17 = bf16[8,256,256]{2,1,0:T(8,128)(2,1)S(1)} async-done(((bf16[8,256,256]{2,1,0:T(8,128)(2,1)}), bf16[8,256,256]{2,1,0:T(8,128)(2,1)S(1)}, u32[]{:S(2)}, u32[]{:S(2)}) %all-to-all-start.17) | async-done | bytes 1048608 | tf_op jit(solution)/shard_map/all_to_all | solution.py:564
  863.3 4.9 all-to-all-start.11
  873.3 42.6 %all-to-all-done.11 = bf16[4,2064,256]{2,1,0:T(8,128)(2,1)} async-done(((bf16[4,2064,256]{2,1,0:T(8,128)(2,1)}), bf16[4,2064,256]{2,1,0:T(8,128)(2,1)}, u32[]{:S(2)}, u32[]{:S(2)}) %all-to-all-start.11) | async-done | bytes 4227104 | tf_op jit(solution)/shard_map/all_to_all | solution.py:564
  915.9 3.5 all-to-all-start.13
  924.9 8.3 all-to-all-done.13
  933.2 3.6 all-to-all-start.12
  943.2 20.1 %all-to-all-done.12 = bf16[8,256,256]{2,1,0:T(8,128)(2,1)S(1)} async-done(((bf16[8,256,256]{2,1,0:T(8,128)(2,1)}), bf16[8,256,256]{2,1,0:T(8,128)(2,1)S(1)}, u32[]{:S(2)}, u32[]{:S(2)}) %all-to-all-start.12) | async-done | bytes 1048608 | tf_op jit(solution)/shard_map/all_to_all | solution.py:564
  964.6 3.6 all-to-all-start.7
  973.9 4.0 fusion.6
  977.9 9.5 all-to-all-done.7
  988.9 4.5 all-to-all-start.10
  999.2 13.0 %all-to-all-done.10 = bf16[4,3,32,2048]{3,2,1,0:T(8,128)(2,1)} async-done(((bf16[4,3,32,2048]{3,2,1,0:T(8,128)(2,1)}), bf16[4,3,32,2048]{3,2,1,0:T(8,128)(2,1)}, u32[]{:S(2)}, u32[]{:S(2)}) %all-to-all-start.10) | async-done | bytes 1572896 | tf_op jit(solution)/shard_map/all_to_all | solution.py:564
  1012.2 3.6 all-to-all-start.14
  1031.0 3.4 copy_convert_fusion.1
  1034.4 3.4 copy_convert_fusion
  (415 shorter events, 197.3 us)
Async XLA Ops:
  7.2 58.3 %all-gather.9.cloned.1.call-start = ((), (), s32[]{:S(2)}) async-start(), calls=%async_computation.22 | async-start | bytes 2433024 | tf_op jit(solution)/shard_map/all_gather | solution.py:661
  11.0 126.9 %all-gather.7.cloned.1.call-start = ((), (), s32[]{:S(2)}) async-start(), calls=%async_computation.21 | async-start | bytes 3538944 | tf_op jit(solution)/shard_map/all_gather | solution.py:653
  17.2 47.8 %all-to-all-start = ((bf16[8,256,256]{1,2,0:T(8,128)(2,1)}), bf16[8,256,256]{1,2,0:T(8,128)(2,1)S(1)}, u32[]{:S(2)}, u32[]{:S(2)}) async-start(bf16[8,256,256]{1,2,0:T(8,128)(2,1)} %maximum_bitcast_fusion.13), calls=%async_computation | async-start | bytes 2097152 | tf_op jit(solution)/shard_map/all_to_all | solution.py:564
  23.6 240.0 %all-gather.11.cloned.1.call-start = ((), (), s32[]{:S(2)}) async-start(), calls=%async_computation.23 | async-start | bytes 10485760 | tf_op jit(solution)/shard_map/all_gather | solution.py:669
  71.2 62.3 %all-to-all-start.1 = ((bf16[4,2064,256]{2,1,0:T(8,128)(2,1)}), bf16[4,2064,256]{2,1,0:T(8,128)(2,1)}, u32[]{:S(2)}, u32[]{:S(2)}) async-start(bf16[4,2064,256]{2,1,0:T(8,128)(2,1)} %broadcast_in_dim.47), calls=%async_computation.1 | async-start | bytes 8454144 | tf_op jit(solution)/shard_map/all_to_all | solution.py:564
  135.2 10.1 collective-permute-start
  136.6 34.8 %copy-start.30 = (f32[256,128]{1,0:T(8,128)}, f32[256,128]{1,0:T(8,128)S(1)}, u32[]{:S(2)}) copy-start(f32[256,128]{1,0:T(8,128)S(1)} %get-tuple-element.187) | copy-start | bytes 393220
  151.8 23.7 %copy-start.9 = (f32[3,256,256]{2,1,0:T(8,128)}, f32[3,256,256]{2,1,0:T(8,128)S(1)}, u32[]{:S(2)}) copy-start(f32[3,256,256]{2,1,0:T(8,128)S(1)} %get-tuple-element.107) | copy-start | bytes 2359300
  167.9 8.2 all-to-all-start.3
  178.0 53.2 %all-to-all-start.2 = ((bf16[4,3,256,512]{3,2,1,0:T(8,128)(2,1)}), bf16[4,3,256,512]{3,2,1,0:T(8,128)(2,1)S(1)}, u32[]{:S(2)}, u32[]{:S(2)}) async-start(bf16[4,3,256,512]{3,2,1,0:T(8,128)(2,1)} %broadcast_in_dim.50), calls=%async_computation.2 | async-start | bytes 6291456 | tf_op jit(solution)/shard_map/all_to_all | solution.py:564
  241.4 17.5 %all-to-all-start.4 = ((bf16[8,3,32,256]{3,2,1,0:T(8,128)(2,1)}), bf16[8,3,32,256]{3,2,1,0:T(8,128)(2,1)S(1)}, u32[]{:S(2)}, u32[]{:S(2)}) async-start(bf16[8,3,32,256]{3,2,1,0:T(8,128)(2,1)} %bitcast.260), calls=%async_computation.4 | async-start | bytes 786432 | tf_op jit(solution)/shard_map/all_to_all | solution.py:564
  258.8 57.3 %all-to-all-start.5 = ((bf16[8,2,256,256]{3,2,1,0:T(8,128)(2,1)}), bf16[8,2,256,256]{3,2,1,0:T(8,128)(2,1)S(1)}, u32[]{:S(2)}, u32[]{:S(2)}) async-start(bf16[8,2,256,256]{3,2,1,0:T(8,128)(2,1)} %copy.284), calls=%async_computation.5 | async-start | bytes 4194304 | tf_op jit(solution)/shard_map/all_to_all | solution.py:564
  262.4 148.6 %all-gather.13.cloned.1.call-start = ((), (), s32[]{:S(2)}) async-start(), calls=%async_computation.24 | async-start | bytes 3538944 | tf_op jit(solution)/shard_map/all_gather | solution.py:742
  295.5 307.0 %copy-start.5 = (f32[3,32,2048]{2,1,0:T(8,128)}, f32[3,32,2048]{2,1,0:T(8,128)S(1)}, u32[]{:S(2)}) copy-start(f32[3,32,2048]{2,1,0:T(8,128)S(1)} %get-tuple-element.209) | copy-start | bytes 2359300
  296.2 25.7 %copy-start.57 = (f32[3,32]{1,0:T(4,128)}, f32[3,32]{1,0:T(4,128)S(1)}, u32[]{:S(2)}) copy-start(f32[3,32]{1,0:T(4,128)S(1)} %get-tuple-element.184) | copy-start | bytes 1156
  316.1 43.2 %all-to-all-start.6 = ((bf16[8,256,256]{2,1,0:T(8,128)(2,1)}), bf16[8,256,256]{2,1,0:T(8,128)(2,1)}, u32[]{:S(2)}, u32[]{:S(2)}) async-start(bf16[8,256,256]{2,1,0:T(8,128)(2,1)} %bitcast.298), calls=%async_computation.6 | async-start | bytes 2097152 | tf_op jit(solution)/shard_map/all_to_all | solution.py:564
  320.4 179.9 %reduce-scatter.4.cloned.1.call-start = ((), (), s32[]{:S(2)}) async-start(), calls=%async_computation.25 | async-start | bytes 3538944 | tf_op jit(solution)/shard_map/reduce_scatter | solution.py:748
  321.9 40.9 %collective-permute-start.1 = (bf16[2048,256]{1,0:T(8,128)(2,1)}, bf16[2048,256]{1,0:T(8,128)(2,1)S(1)}, u32[]{:S(2)}, u32[]{:S(2)}) collective-permute-start(bf16[2048,256]{1,0:T(8,128)(2,1)} %bitcast.38), channel_id=1, source_target_pairs={{0,1},{1,0},{2,3},{3,2},{4,5},{5,4},{6,7},{7,6},{8,9},{9,8},{10,11... | collective-permute-start | bytes 3145736 | tf_op jit(solution)/shard_map/ppermute | solution.py:560
  323.3 41.4 %collective-permute-start.5 = (bf16[2048,256]{1,0:T(8,128)(2,1)}, bf16[2048,256]{1,0:T(8,128)(2,1)}, u32[]{:S(2)}, u32[]{:S(2)}) collective-permute-start(bf16[2048,256]{1,0:T(8,128)(2,1)} %bitcast.40), channel_id=1, source_target_pairs={{0,2},{1,3},{2,0},{3,1},{4,6},{5,7},{6,4},{7,5},{8,10},{9,11},{10,... | collective-permute-start | bytes 3145736 | tf_op jit(solution)/shard_map/ppermute | solution.py:560
  360.6 26.2 %collective-permute-start.7 = (bf16[256,2048]{1,0:T(8,128)(2,1)S(1)}, bf16[256,2048]{1,0:T(8,128)(2,1)}, u32[]{:S(2)}, u32[]{:S(2)}) collective-permute-start(bf16[256,2048]{1,0:T(8,128)(2,1)S(1)} %bitcast.299), channel_id=1, source_target_pairs={{0,1},{1,0},{2,3},{3,2},{4,5},{5,4},{6,7},{7,6},{8,9},{9,8},{10,11... | collective-permute-start | bytes 3145736 | tf_op jit(solution)/shard_map/ppermute | solution.py:560
  362.2 26.3 %collective-permute-start.2 = (bf16[2048,256]{1,0:T(8,128)(2,1)}, bf16[2048,256]{1,0:T(8,128)(2,1)}, u32[]{:S(2)}, u32[]{:S(2)}) collective-permute-start(bf16[2048,256]{1,0:T(8,128)(2,1)} %bitcast.38), channel_id=1, source_target_pairs={{0,2},{1,3},{2,0},{3,1},{4,6},{5,7},{6,4},{7,5},{8,10},{9,11},{10,... | collective-permute-start | bytes 3145736 | tf_op jit(solution)/shard_map/ppermute | solution.py:560
  362.7 54.6 %copy-start.85 = (bf16[2048,256]{1,0:T(8,128)(2,1)}, bf16[2048,256]{1,0:T(8,128)(2,1)S(1)}, u32[]{:S(2)}) copy-start(bf16[2048,256]{1,0:T(8,128)(2,1)S(1)} %collective-permute-done.1) | copy-start | bytes 3145732
  362.7 48.3 %collective-permute-start.3 = (bf16[2048,256]{1,0:T(8,128)(2,1)S(1)}, bf16[2048,256]{1,0:T(8,128)(2,1)}, u32[]{:S(2)}, u32[]{:S(2)}) collective-permute-start(bf16[2048,256]{1,0:T(8,128)(2,1)S(1)} %collective-permute-done.1), channel_id=1, source_target_pairs={{0,2},{1,3},{2,0},{3,1},{4,6},{5,7},{6,4},{7,5},{8,10},{9,11},{10,... | collective-permute-start | bytes 3145736 | tf_op jit(solution)/shard_map/ppermute | solution.py:560
  364.2 53.1 %collective-permute-start.4 = (bf16[2048,256]{1,0:T(8,128)(2,1)}, bf16[2048,256]{1,0:T(8,128)(2,1)}, u32[]{:S(2)}, u32[]{:S(2)}) collective-permute-start(bf16[2048,256]{1,0:T(8,128)(2,1)} %bitcast.40), channel_id=1, source_target_pairs={{0,1},{1,0},{2,3},{3,2},{4,5},{5,4},{6,7},{7,6},{8,9},{9,8},{10,11... | collective-permute-start | bytes 3145736 | tf_op jit(solution)/shard_map/ppermute | solution.py:560
  364.8 66.1 %collective-permute-start.6 = (bf16[2048,256]{1,0:T(8,128)(2,1)}, bf16[2048,256]{1,0:T(8,128)(2,1)}, u32[]{:S(2)}, u32[]{:S(2)}) collective-permute-start(bf16[2048,256]{1,0:T(8,128)(2,1)} %collective-permute-done.5), channel_id=1, source_target_pairs={{0,1},{1,0},{2,3},{3,2},{4,5},{5,4},{6,7},{7,6},{8,9},{9,8},{10,11... | collective-permute-start | bytes 3145736 | tf_op jit(solution)/shard_map/ppermute | solution.py:560
  386.8 51.5 %collective-permute-start.8 = (bf16[256,2048]{1,0:T(8,128)(2,1)S(1)}, bf16[256,2048]{1,0:T(8,128)(2,1)}, u32[]{:S(2)}, u32[]{:S(2)}) collective-permute-start(bf16[256,2048]{1,0:T(8,128)(2,1)S(1)} %bitcast.300), channel_id=1, source_target_pairs={{0,2},{1,3},{2,0},{3,1},{4,6},{5,7},{6,4},{7,5},{8,10},{9,11},{10,... | collective-permute-start | bytes 3145736 | tf_op jit(solution)/shard_map/ppermute | solution.py:560
  388.5 66.2 %collective-permute-start.9 = (bf16[256,2048]{1,0:T(8,128)(2,1)}, bf16[256,2048]{1,0:T(8,128)(2,1)}, u32[]{:S(2)}, u32[]{:S(2)}) collective-permute-start(bf16[256,2048]{1,0:T(8,128)(2,1)} %collective-permute-done.7), channel_id=1, source_target_pairs={{0,2},{1,3},{2,0},{3,1},{4,6},{5,7},{6,4},{7,5},{8,10},{9,11},{10,... | collective-permute-start | bytes 3145736 | tf_op jit(solution)/shard_map/ppermute | solution.py:560
  411.0 19.9 %copy-start.82 = (bf16[3,256,2048]{2,1,0:T(8,128)(2,1)S(1)}, bf16[3,256,2048]{2,1,0:T(8,128)(2,1)}, u32[]{:S(2)}) copy-start(bf16[3,256,2048]{2,1,0:T(8,128)(2,1)} %all-gather.13.cloned.1.call-done) | copy-start | bytes 9437188
  417.3 21.0 %copy-start.89 = (f32[3,256,1024]{2,1,0:T(8,128)}, f32[3,256,1024]{2,1,0:T(8,128)S(1)}, u32[]{:S(2)}) copy-start(f32[3,256,1024]{2,1,0:T(8,128)S(1)} %fusion.18) | copy-start | bytes 9437188
  461.8 39.7 %copy-start.55 = (f32[1,2048]{1,0:T(1,128)S(1)}, f32[1,2048]{1,0:T(1,128)}, u32[]{:S(2)}) copy-start(f32[1,2048]{1,0:T(1,128)} %get-tuple-element.115) | copy-start | bytes 24580
  461.8 80.1 %all-gather.15.cloned.1.call-start = ((), (), s32[]{:S(2)}) async-start(), calls=%async_computation.26 | async-start | bytes 3538944 | tf_op jit(solution)/shard_map/all_gather | solution.py:762
  501.4 48.8 %copy-start.66 = (f32[3,32]{1,0:T(4,128)}, f32[3,32]{1,0:T(4,128)S(1)}, u32[]{:S(2)}) copy-start(f32[3,32]{1,0:T(4,128)S(1)} %get-tuple-element.182) | copy-start | bytes 1156
  504.3 98.2 %reduce-scatter.6.cloned.1.call-start = ((), (), s32[]{:S(2)}) async-start(), calls=%async_computation.27 | async-start | bytes 3538944 | tf_op jit(solution)/shard_map/reduce_scatter | solution.py:772
  569.7 72.9 %collective-permute-start.11 = (bf16[2048,512]{1,0:T(8,128)(2,1)}, bf16[2048,512]{1,0:T(8,128)(2,1)}, u32[]{:S(2)}, u32[]{:S(2)}) collective-permute-start(bf16[2048,512]{1,0:T(8,128)(2,1)} %convolution_convert_fusion.3), channel_id=1, source_target_pairs={{0,2},{1,3},{2,0},{3,1},{4,6},{5,7},{6,4},{7,5},{8,10},{9,11},{10,... | collective-permute-start | bytes 6291464 | tf_op jit(solution)/shard_map/ppermute | solution.py:560
  575.3 27.2 %copy-start.58 = (f32[3,32]{1,0:T(4,128)S(1)}, f32[3,32]{1,0:T(4,128)}, u32[]{:S(2)}) copy-start(f32[3,32]{1,0:T(4,128)} %copy-done.57) | copy-start | bytes 1156
  575.3 27.2 %copy-start.68 = (f32[3,32]{1,0:T(4,128)S(1)}, f32[3,32]{1,0:T(4,128)}, u32[]{:S(2)}) copy-start(f32[3,32]{1,0:T(4,128)} %get-tuple-element.183) | copy-start | bytes 1156
  575.3 74.3 %collective-permute-start.13 = (bf16[2048,512]{1,0:T(8,128)(2,1)}, bf16[2048,512]{1,0:T(8,128)(2,1)}, u32[]{:S(2)}, u32[]{:S(2)}) collective-permute-start(bf16[2048,512]{1,0:T(8,128)(2,1)} %convolution_convert_fusion.2), channel_id=1, source_target_pairs={{0,1},{1,0},{2,3},{3,2},{4,5},{5,4},{6,7},{7,6},{8,9},{9,8},{10,11... | collective-permute-start | bytes 6291464 | tf_op jit(solution)/shard_map/ppermute | solution.py:560
  580.0 89.1 %collective-permute-start.15 = (bf16[512,2048]{1,0:T(8,128)(2,1)}, bf16[512,2048]{1,0:T(8,128)(2,1)}, u32[]{:S(2)}, u32[]{:S(2)}) collective-permute-start(bf16[512,2048]{1,0:T(8,128)(2,1)} %convolution_convert_fusion.1), channel_id=1, source_target_pairs={{0,1},{1,0},{2,3},{3,2},{4,5},{5,4},{6,7},{7,6},{8,9},{9,8},{10,11... | collective-permute-start | bytes 6291464 | tf_op jit(solution)/shard_map/ppermute | solution.py:560
  638.1 87.5 %all-to-all-start.9 = ((bf16[4,3,256,512]{3,2,1,0:T(8,128)(2,1)}), bf16[4,3,256,512]{3,2,1,0:T(8,128)(2,1)S(1)}, u32[]{:S(2)}, u32[]{:S(2)}) async-start(bf16[4,3,256,512]{3,2,1,0:T(8,128)(2,1)} %get-tuple-element.21), calls=%async_computation.11 | async-start | bytes 6291456 | tf_op jit(solution)/shard_map/all_to_all | solution.py:564
  647.6 76.6 %collective-permute-start.12 = (bf16[2048,256]{1,0:T(8,128)(2,1)S(1)}, bf16[2048,256]{1,0:T(8,128)(2,1)S(1)}, u32[]{:S(2)}, u32[]{:S(2)}) collective-permute-start(bf16[2048,256]{1,0:T(8,128)(2,1)S(1)} %split.47), channel_id=1, source_target_pairs={{0,1},{1,0},{2,3},{3,2},{4,5},{5,4},{6,7},{7,6},{8,9},{9,8},{10,11... | collective-permute-start | bytes 3145736 | tf_op jit(solution)/shard_map/ppermute | solution.py:560
  649.7 19.4 %copy-start.4 = (bf16[3,256,2048]{2,1,0:T(8,128)(2,1)S(1)}, bf16[3,256,2048]{2,1,0:T(8,128)(2,1)}, u32[]{:S(2)}) copy-start(bf16[3,256,2048]{2,1,0:T(8,128)(2,1)} %all-gather.15.cloned.1.call-done) | copy-start | bytes 9437188
  654.6 120.5 %collective-permute-start.14 = (bf16[2048,256]{1,0:T(8,128)(2,1)}, bf16[2048,256]{1,0:T(8,128)(2,1)}, u32[]{:S(2)}, u32[]{:S(2)}) collective-permute-start(bf16[2048,256]{1,0:T(8,128)(2,1)} %split.46), channel_id=1, source_target_pairs={{0,2},{1,3},{2,0},{3,1},{4,6},{5,7},{6,4},{7,5},{8,10},{9,11},{10,... | collective-permute-start | bytes 3145736 | tf_op jit(solution)/shard_map/ppermute | solution.py:560
  675.8 116.0 %collective-permute-start.16 = (bf16[256,2048]{1,0:T(8,128)(2,1)}, bf16[256,2048]{1,0:T(8,128)(2,1)}, u32[]{:S(2)}, u32[]{:S(2)}) collective-permute-start(bf16[256,2048]{1,0:T(8,128)(2,1)} %split.45), channel_id=1, source_target_pairs={{0,2},{1,3},{2,0},{3,1},{4,6},{5,7},{6,4},{7,5},{8,10},{9,11},{10,... | collective-permute-start | bytes 3145736 | tf_op jit(solution)/shard_map/ppermute | solution.py:560
  725.6 57.1 %all-to-all-start.15 = ((bf16[8,256,256]{2,1,0:T(8,128)(2,1)}), bf16[8,256,256]{2,1,0:T(8,128)(2,1)}, u32[]{:S(2)}, u32[]{:S(2)}) async-start(bf16[8,256,256]{2,1,0:T(8,128)(2,1)} %bitcast.274), calls=%async_computation.18 | async-start | bytes 2097152 | tf_op jit(solution)/shard_map/all_to_all | solution.py:564
  729.8 139.3 %reduce-scatter.8.cloned.1.call-start = ((), (), s32[]{:S(2)}) async-start(), calls=%async_computation.28 | async-start | bytes 3538944 | tf_op jit(solution)/shard_map/reduce_scatter | solution.py:894
  731.8 28.9 %copy-start.18 = (f32[3,256,128]{2,1,0:T(8,128)}, f32[3,256,128]{2,1,0:T(8,128)S(1)}, u32[]{:S(2)}) copy-start(f32[3,256,128]{2,1,0:T(8,128)S(1)} %get-tuple-element.172) | copy-start | bytes 1179652
  782.6 49.4 %all-to-all-start.16 = ((bf16[8,256,256]{2,1,0:T(8,128)(2,1)}), bf16[8,256,256]{2,1,0:T(8,128)(2,1)S(1)}, u32[]{:S(2)}, u32[]{:S(2)}) async-start(bf16[8,256,256]{2,1,0:T(8,128)(2,1)} %bitcast.101), calls=%async_computation.19 | async-start | bytes 2097152 | tf_op jit(solution)/shard_map/all_to_all | solution.py:564
  791.3 49.1 %collective-permute-start.10 = (bf16[2,2064,256]{2,1,0:T(8,128)(2,1)}, bf16[2,2064,256]{2,1,0:T(8,128)(2,1)}, u32[]{:S(2)}, u32[]{:S(2)}) collective-permute-start(bf16[2,2064,256]{2,1,0:T(8,128)(2,1)} %pad_maximum_fusion.2), channel_id=1, source_target_pairs={{0,4},{4,0},{8,12},{12,8},{16,20},{20,16},{24,28},{28,24},{1,5},{5... | collective-permute-start | bytes 6340616 | tf_op jit(solution)/shard_map/ppermute | solution.py:560
  795.4 40.5 %copy-start.69 = (bf16[256]{0:T(256)(128)(2,1)S(1)}, bf16[256]{0:T(256)(128)(2,1)}, u32[]{:S(2)}) copy-start(bf16[256]{0:T(256)(128)(2,1)} %get-tuple-element.197) | copy-start | bytes 1540
  797.6 39.5 %copy-start.38 = (bf16[3,256,64]{2,1,0:T(8,128)(2,1)S(1)}, bf16[3,256,64]{2,1,0:T(8,128)(2,1)}, u32[]{:S(2)}) copy-start(bf16[3,256,64]{2,1,0:T(8,128)(2,1)} %copy-done.37) | copy-start | bytes 294916
  832.1 30.2 %all-to-all-start.17 = ((bf16[8,256,256]{2,1,0:T(8,128)(2,1)}), bf16[8,256,256]{2,1,0:T(8,128)(2,1)S(1)}, u32[]{:S(2)}, u32[]{:S(2)}) async-start(bf16[8,256,256]{2,1,0:T(8,128)(2,1)} %bitcast.269), calls=%async_computation.20 | async-start | bytes 2097152 | tf_op jit(solution)/shard_map/all_to_all | solution.py:564
  844.3 24.5 %copy-start.78 = (bf16[14]{0:T(256)(128)(2,1)S(1)}, bf16[14]{0:T(256)(128)(2,1)}, u32[]{:S(2)}) copy-start(bf16[14]{0:T(256)(128)(2,1)} %copy-done.77) | copy-start | bytes 88
  844.4 24.8 %copy-start.6 = (f32[3,32,2048]{2,1,0:T(8,128)S(1)}, f32[3,32,2048]{2,1,0:T(8,128)}, u32[]{:S(2)}) copy-start(f32[3,32,2048]{2,1,0:T(8,128)} %copy-done.5) | copy-start | bytes 2359300
  844.4 24.8 %copy-start.56 = (f32[1,2048]{1,0:T(1,128)S(1)}, f32[1,2048]{1,0:T(1,128)}, u32[]{:S(2)}) copy-start(f32[1,2048]{1,0:T(1,128)} %get-tuple-element.115) | copy-start | bytes 24580
  844.4 24.8 %copy-start.59 = (f32[3,32]{1,0:T(4,128)S(1)}, f32[3,32]{1,0:T(4,128)}, u32[]{:S(2)}) copy-start(f32[3,32]{1,0:T(4,128)} %copy-done.57) | copy-start | bytes 1156
  844.4 24.8 %copy-start.67 = (f32[3,32]{1,0:T(4,128)S(1)}, f32[3,32]{1,0:T(4,128)}, u32[]{:S(2)}) copy-start(f32[3,32]{1,0:T(4,128)} %copy-done.66) | copy-start | bytes 1156
  863.3 52.6 %all-to-all-start.11 = ((bf16[4,2064,256]{2,1,0:T(8,128)(2,1)}), bf16[4,2064,256]{2,1,0:T(8,128)(2,1)}, u32[]{:S(2)}, u32[]{:S(2)}) async-start(bf16[4,2064,256]{2,1,0:T(8,128)(2,1)} %maximum_select_fusion), calls=%async_computation.14 | async-start | bytes 8454144 | tf_op jit(solution)/shard_map/all_to_all | solution.py:564
  868.1 101.0 %all-gather.17.cloned.1.call-start = ((), (), s32[]{:S(2)}) async-start(), calls=%async_computation.29 | async-start | bytes 3538944 | tf_op jit(solution)/shard_map/all_gather | solution.py:836
  915.9 17.3 %all-to-all-start.13 = ((bf16[8,112,256]{2,1,0:T(8,128)(2,1)}), bf16[8,112,256]{2,1,0:T(8,128)(2,1)S(1)}, u32[]{:S(2)}, u32[]{:S(2)}) async-start(bf16[8,112,256]{2,1,0:T(8,128)(2,1)} %maximum_bitcast_fusion.14), calls=%async_computation.16 | async-start | bytes 917504 | tf_op jit(solution)/shard_map/all_to_all | solution.py:564
  933.2 30.1 %all-to-all-start.12 = ((bf16[8,256,256]{2,1,0:T(8,128)(2,1)}), bf16[8,256,256]{2,1,0:T(8,128)(2,1)S(1)}, u32[]{:S(2)}, u32[]{:S(2)}) async-start(bf16[8,256,256]{2,1,0:T(8,128)(2,1)} %bitcast.272), calls=%async_computation.15 | async-start | bytes 2097152 | tf_op jit(solution)/shard_map/all_to_all | solution.py:564
  941.6 21.7 %copy-start.29 = (bf16[3,32,2048]{2,1,0:T(8,128)(2,1)S(1)}, bf16[3,32,2048]{2,1,0:T(8,128)(2,1)}, u32[]{:S(2)}) copy-start(bf16[3,32,2048]{2,1,0:T(8,128)(2,1)} %get-tuple-element.133) | copy-start | bytes 1179652
  964.6 22.8 %all-to-all-start.7 = ((bf16[4,3,32,2048]{3,2,1,0:T(8,128)(2,1)}), bf16[4,3,32,2048]{3,2,1,0:T(8,128)(2,1)S(1)}, u32[]{:S(2)}, u32[]{:S(2)}) async-start(bf16[4,3,32,2048]{3,2,1,0:T(8,128)(2,1)} %broadcast_in_dim.56), calls=%async_computation.8 | async-start | bytes 3145728 | tf_op jit(solution)/shard_map/all_to_all | solution.py:564
  988.9 23.3 %all-to-all-start.10 = ((bf16[4,3,32,2048]{3,2,1,0:T(8,128)(2,1)}), bf16[4,3,32,2048]{3,2,1,0:T(8,128)(2,1)}, u32[]{:S(2)}, u32[]{:S(2)}) async-start(bf16[4,3,32,2048]{3,2,1,0:T(8,128)(2,1)} %broadcast_in_dim.57), calls=%async_computation.13 | async-start | bytes 3145728 | tf_op jit(solution)/shard_map/all_to_all | solution.py:564
  1012.2 28.3 %all-to-all-start.14 = ((bf16[4,1040,256]{2,1,0:T(8,128)(2,1)}), bf16[4,1040,256]{2,1,0:T(8,128)(2,1)S(1)}, u32[]{:S(2)}, u32[]{:S(2)}) async-start(bf16[4,1040,256]{2,1,0:T(8,128)(2,1)} %pad_maximum_fusion.1), calls=%async_computation.17 | async-start | bytes 4259840 | tf_op jit(solution)/shard_map/all_to_all | solution.py:564
  (69 other events, 347.0 us)
Sparse Core Ops, SparseCore 0:
  11.1 53.5 all-gather.8
  66.9 36.3 all-gather.6
  105.7 122.7 all-gather.10
  298.4 57.7 all-gather.12
  461.9 38.2 reduce-scatter.3
  504.4 37.3 all-gather.14
  563.2 39.2 reduce-scatter.5
  775.2 59.0 reduce-scatter.7
  870.5 38.4 all-gather.16

commit v2 on v1

--- a/solution.py
+++ b/solution.py
@@ -564,9 +564,28 @@
     return lax.all_to_all(blocks, axis, split_axis=0, concat_axis=0, tiled=True)
 
 
-def share(value, axis):
-    size = lax.axis_size(axis)
-    return spread(jnp.broadcast_to(value[None], (size,) + value.shape), axis)
+def others(value):
+    return (value, swap(value, "tp", 1), swap(value, "tp", 2), swap(value, "tp", 3))
+
+
+def in_order(pieces, part):
+    odd = part % 2 == 1
+    high = part // 2 == 1
+    a, b, c, d = pieces
+    a, b, c, d = (jnp.where(odd, p, q) for p, q in ((b, a), (a, b), (d, c), (c, d)))
+    return tuple(jnp.where(high, p, q) for p, q in ((c, a), (d, b), (a, c), (b, d)))
+
+
+def reduce_tp(blocks, part):
+    total = lax.dynamic_index_in_dim(blocks, part, axis=0, keepdims=False).astype(jnp.float32)
+    for bit in range(1, 4):
+        block = lax.dynamic_index_in_dim(blocks, part ^ bit, axis=0, keepdims=False)
+        total = total + swap(block, "tp", bit).astype(jnp.float32)
+    return total
+
+
+def tie(*values):
+    return lax.optimization_barrier(values)
 
 
 def gather_tp(piece, first):
@@ -581,12 +600,6 @@
     merged = keep + swap(send.astype(jnp.bfloat16), "tp", first).astype(jnp.float32)
     mine, other = jnp.split(merged, 2, axis=axis)
     return mine + swap(other.astype(jnp.bfloat16), "tp", second).astype(jnp.float32)
-
-
-def arrival_rows(weight, chips):
-    width = weight.shape[-1]
-    view = weight.reshape(2, 2, chips, 2, 64, width).transpose(2, 0, 3, 1, 4, 5)
-    return jnp.stack([view[:, 0], view[:, 1, ::-1]], axis=1).reshape(-1, width)
 
 
 def natural_rows(grad, chips):
@@ -644,6 +657,14 @@
         [halves(w_query), halves(w_key), halves(w_value), jnp.zeros_like(halves(w_value))], axis=2
     ).transpose(1, 0, 2)
     packed = spread(packed, "fsdp").reshape(width, bundle)
+
+    def columns(weight):
+        return weight.reshape(rows_local, members, unit).transpose(1, 0, 2)
+
+    packed, gate_up = tie(packed, jnp.stack([columns(w_gate), columns(w_up)], axis=1))
+    gate_up = spread(gate_up, "fsdp")
+    gate_up, down = tie(gate_up, w_down.reshape(members, unit, rows_local))
+    down = spread(down, "fsdp")
     gain_row = jnp.concatenate(
         [query_gain, key_gain, jnp.zeros((bundle - 2 * 64,), query_gain.dtype)]
     )
@@ -651,9 +672,19 @@
         [packed, jnp.broadcast_to(gain_row[None], (16, bundle)).astype(packed.dtype)], axis=0
     )
     token_low = lax.all_gather(own_tokens.astype(low), "fsdp", axis=1, tiled=True)
-    packed = share(packed, "tp")
-    own_half = lax.dynamic_slice_in_dim(packed, 2 * core, 2, axis=0)
-    other_half = swap(lax.dynamic_slice_in_dim(packed, 2 - 2 * core, 2, axis=0), "fsdp", 1)
+    cut = width // 2
+    first, second = swap(packed, "tp", 1), swap(packed, "tp", 2)
+    third = jnp.concatenate([swap(first[:cut], "tp", 2), swap(second[cut:], "tp", 1)], axis=0)
+    near = part // 2 == core
+    odd = part % 2 == 1
+    mine = [jnp.where(near, packed, second), jnp.where(near, first, third)]
+    theirs = [jnp.where(near, second, packed), jnp.where(near, third, first)]
+    own_half = [jnp.where(odd, mine[1], mine[0]), jnp.where(odd, mine[0], mine[1])]
+    other_half = swap(
+        jnp.stack([jnp.where(odd, theirs[1], theirs[0]), jnp.where(odd, theirs[0], theirs[1])]),
+        "fsdp",
+        1,
+    )
 
     norm_gains = jnp.concatenate(
         [attn_gain[None], mlp_gain[None], jnp.zeros((14, attn_gain.shape[0]), attn_gain.dtype)]
@@ -666,29 +697,19 @@
     )
     gain_attn = out_rows[w_out.shape[0]].astype(jnp.float32)
     gain_mlp = out_rows[w_out.shape[0] + 1].astype(jnp.float32)
-    out_full = lax.all_gather(out_rows[: w_out.shape[0]], "tp", axis=0, tiled=True)
-    out_full = arrival_rows(out_full, chips)
-
-    def columns(weight):
-        return weight.reshape(rows_local, members, unit).transpose(1, 0, 2)
-
-    gate_up = spread(jnp.stack([columns(w_gate), columns(w_up)], axis=1), "fsdp")
-    down = spread(w_down.reshape(members, unit, rows_local), "fsdp")
-    gate_all = jnp.concatenate(gather_tp(gate_up[:, 0].reshape(width, unit), 1), axis=1)
-    up_all = jnp.concatenate(gather_tp(gate_up[:, 1].reshape(width, unit), 2), axis=1)
-    down_all = jnp.concatenate(
-        gather_tp(down.transpose(1, 0, 2).reshape(unit, width), 1), axis=0
-    )
+    out_full = lax.all_gather(
+        out_rows[: w_out.shape[0]].reshape(2 * chips, 64, width), "tp", axis=1, tiled=True
+    ).reshape(width, width)
 
     index = jnp.arange(members, dtype=jnp.int32)[:, None] * local_len
     index = (index + jnp.arange(sub, dtype=jnp.int32)[None, :]).reshape(count)
-    index = index[None, :] + jnp.arange(parts, dtype=jnp.int32)[:, None] * sub
+    index = index[None, :] + (part ^ jnp.arange(parts, dtype=jnp.int32))[:, None] * sub
     spans = jnp.arange(span_order.shape[0], dtype=jnp.int32)
     picked = jnp.sum(
         jnp.where((index // span_len)[..., None] == spans, span_order, 0), axis=-1
     )
     all_pos = picked * span_len + index % span_len
-    query_pos = lax.dynamic_index_in_dim(all_pos, part, axis=0, keepdims=False)
+    query_pos = all_pos[0]
     inv_freq = jnp.power(
         rope_base, -(jnp.arange(64, dtype=jnp.float32) * 2.0 / HEAD_DIM)
     )
@@ -715,27 +736,56 @@
     gain_rows = [piece[width].astype(jnp.float32) for piece in weight_pieces]
     gain_query, gain_key = lanes(gain_rows, 0), lanes(gain_rows, 1)
     key_low = rotate(keys * gain_key, 1.0).astype(low)
-    both = share(jnp.concatenate([key_low, values.astype(low)], axis=-1), "tp")
+    both = jnp.concatenate([key_low, values.astype(low)], axis=-1)
+    both, gate_up = tie(both, gate_up)
+    gate_all = jnp.concatenate(gather_tp(gate_up[:, 0].reshape(width, unit), 1), axis=1)
+    up_all = jnp.concatenate(gather_tp(gate_up[:, 1].reshape(width, unit), 2), axis=1)
+    both = jnp.stack(others(both))
     square_sums = lax.psum(
         jnp.stack([jnp.sum(queries * queries, axis=-1), jnp.sum(keys * keys, axis=-1)]), "fsdp"
     )
     scales = lax.rsqrt(square_sums / width + epsilon)
     query_scale, key_scale = scales[0][..., None], scales[1][..., None]
-    all_key_scale = share(scales[1], "tp").reshape(parts, batch_rows, 1, count)
+    all_key_scale = jnp.stack(others(scales[1])).reshape(parts, batch_rows, 1, count)
     query_low = rotate(queries * query_scale * gain_query, 1.0).astype(low)
     qpos = query_pos[:, None]
     kpos = all_pos[:, None, :]
     attended, log_total = attend_tiles(query_low, both, qpos, kpos, all_key_scale)
 
+    places = [(chip, half, side) for chip in range(chips) for half in range(2) for side in range(2)]
+
     def to_tokens(value):
         blocks = value.reshape(batch_rows, members, sub, pair).transpose(1, 0, 2, 3)
-        return spread(blocks, "fsdp").transpose(1, 2, 0, 3).reshape(batch_rows, sub, members * pair)
+        blocks = spread(blocks, "fsdp")
+        return jnp.concatenate(
+            [
+                blocks[2 * chip + side][..., (half ^ side) * HEAD_DIM :][..., :HEAD_DIM]
+                for chip, half, side in places
+            ],
+            axis=-1,
+        )
 
     def to_heads(value):
-        blocks = value.reshape(batch_rows, sub, members, pair).transpose(2, 0, 1, 3)
+        def lanes_at(chip, half, side):
+            at = places.index((chip, half, side)) * HEAD_DIM
+            return value[..., at : at + HEAD_DIM]
+
+        blocks = jnp.stack(
+            [
+                jnp.concatenate(
+                    [lanes_at(chip, side, side), lanes_at(chip, 1 - side, side)], axis=-1
+                )
+                for chip in range(chips)
+                for side in range(2)
+            ]
+        )
         return spread(blocks, "fsdp").transpose(1, 0, 2, 3).reshape(batch_rows, count, pair)
 
     attended_low = attended.astype(low)
+    attended_low, down = tie(attended_low, down)
+    down_all = jnp.concatenate(
+        gather_tp(down.transpose(1, 0, 2).reshape(unit, width), 1), axis=0
+    )
     branch_attn = matmul(to_tokens(attended_low), out_full, ((2,), (0,)))
     attn_norm = lax.rsqrt(jnp.mean(branch_attn * branch_attn, axis=-1, keepdims=True) + epsilon)
     hidden = own_tokens + branch_attn * attn_norm * gain_attn
@@ -755,8 +805,8 @@
     layer_own = hidden + branch_mlp * mlp_norm * gain_mlp
 
     def whole_span(value):
-        gathered = share(value.astype(low), "tp").astype(jnp.float32)
-        return gathered.transpose(1, 0, 2, 3).reshape(batch_rows, local_len, width)
+        pieces = in_order(others(value.astype(low)), part)
+        return jnp.concatenate(pieces, axis=1).astype(jnp.float32)
 
     grad_gain_mlp, grad_branch_mlp = norm_back(branch_mlp, mlp_norm, gain_mlp, own_cotangent)
     grad_mlp_low = lax.all_gather(grad_branch_mlp.astype(low), "fsdp", axis=1, tiled=True)
@@ -803,14 +853,15 @@
     down_back = spread(
         grad_down_w.astype(low).reshape(unit, members, rows_local).transpose(1, 0, 2), "fsdp"
     )
-    grad_down = down_back.reshape(members * unit, rows_local).astype(jnp.float32)
-
-    def unit_columns(value):
-        blocks = spread(value.astype(low).reshape(members, rows_local, unit), "fsdp")
+
+    def unit_back(value):
+        return spread(value.astype(low).reshape(members, rows_local, unit), "fsdp")
+
+    def unit_columns(blocks):
         return blocks.transpose(1, 0, 2).reshape(rows_local, members * unit).astype(jnp.float32)
 
-    grad_gate = unit_columns(grad_gate_w)
-    grad_up = unit_columns(grad_up_w)
+    gate_back = unit_back(grad_gate_w)
+    up_back = unit_back(grad_up_w)
 
     grad_gain_attn, grad_branch_attn = norm_back(branch_attn, attn_norm, gain_attn, grad_hidden)
     grad_attn_low = grad_branch_attn.astype(low)
@@ -848,7 +899,7 @@
     out_blocks.append(
         jnp.broadcast_to(gain_sums.astype(low)[None], (parts,) + gain_sums.shape)
     )
-    out_sum = jnp.sum(spread(jnp.concatenate(out_blocks, axis=1), "tp").astype(jnp.float32), axis=0)
+    out_sum = reduce_tp(jnp.concatenate(out_blocks, axis=1), part)
     block_rows = w_out.shape[0]
     grad_out_groups = out_sum[: GROUPS * block_rows].reshape(GROUPS, block_rows, rows_local)
     grad_out = jnp.sum(grad_out_groups, axis=0)
@@ -858,7 +909,10 @@
     grad_query_rot, grad_both = attend_back_tiles(
         query_low, both, grad_attended, attended, log_total, qpos, kpos, all_key_scale
     )
-    grad_both = jnp.sum(spread(grad_both, "tp").astype(jnp.float32), axis=0)
+    grad_both = sum(
+        value.astype(jnp.float32)
+        for value in [grad_both[0]] + [swap(grad_both[bit], "tp", bit) for bit in range(1, 4)]
+    )
     grad_qn = rotate(grad_query_rot, -1.0)
     grad_kn = rotate(grad_both[..., :pair], -1.0)
     gained_query = grad_qn * gain_query
@@ -891,8 +945,11 @@
     attn_back_in = sum(
         matmul(grad, piece[:width], ((2,), (1,))) for grad, piece in zip(grad_acts, weight_pieces)
     )
+    attn_back_low, down_back, gate_back = tie(attn_back_in.astype(low), down_back, gate_back)
+    grad_down = down_back.reshape(members * unit, rows_local).astype(jnp.float32)
+    grad_gate = unit_columns(gate_back)
     input_own = grad_hidden + lax.psum_scatter(
-        attn_back_in.astype(low), "fsdp", scatter_dimension=1, tiled=True
+        attn_back_low, "fsdp", scatter_dimension=1, tiled=True
     ).astype(jnp.float32)
     input_grad = whole_span(input_own)
 
@@ -916,10 +973,12 @@
     proj_blocks = jnp.where(
         core == 0, jnp.concatenate([kept, sent]), jnp.concatenate([sent, kept])
     )
-    proj_sum = jnp.sum(spread(proj_blocks, "tp").astype(jnp.float32), axis=0)
+    proj_sum = reduce_tp(proj_blocks, part)
     grad_query_gain = proj_sum[width, :64]
     grad_key_gain = proj_sum[width, 64:128]
-    proj_back = spread(proj_sum[:width].astype(low).reshape(members, rows_local, bundle), "fsdp")
+    proj_low, up_back = tie(proj_sum[:width].astype(low), up_back)
+    grad_up = unit_columns(up_back)
+    proj_back = spread(proj_low.reshape(members, rows_local, bundle), "fsdp")
 
     def natural_columns(at):
         block = proj_back[:, :, at * 64 : at * 64 + 64].astype(jnp.float32)

time: 1070 us -> 931 us (0.87); the launches traced: 1050 us -> 921 us
  waiting for transfers between devices: 583 us -> 493 us
  local copies, waits for them, and re-layouts: 97.7 us -> 82 us
  blocking collectives: 55.5 us -> 40.9 us
  matrix products: 113 us -> 99.6 us
    all_to_all x17 -> x10, waiting for transfers between devices: 351 us -> 102 us  [spread(): return lax.all_to_all(blocks, axis, split_axis=0, concat_axis=0, tiled=True)]
    ppermute x17 -> x42, waiting for transfers between devices: 134 us -> 314 us  [swap(): return lax.ppermute(value, axis, [(i, i ^ bit) for i in range(size)])]
    all_to_all x17 -> x10, starting transfers between devices: 72.3 us -> 42.8 us  [spread(): return lax.all_to_all(blocks, axis, split_axis=0, concat_axis=0, tiled=True)]
    ppermute x17 -> x42, starting transfers between devices: 17.2 us -> 45.4 us  [swap(): return lax.ppermute(value, axis, [(i, i ^ bit) for i in range(size)])]
    reduce_scatter x1, waiting for transfers between devices: 21.9 us -> 0.01 us  [local_fast(): lax.psum_scatter(mlp_back_in.astype(low), 'fsdp', scatter_dimension=1, ti...]
    all_to_all x1 -> x0, blocking collectives: 15.3 us -> none  [spread(): return lax.all_to_all(blocks, axis, split_axis=0, concat_axis=0, tiled=True)]
    reshape x7 -> x3, local copies, waits for them, and re-layouts: 15.9 us -> 2.99 us  [the longest x1 2.27 us: local_fast(): proj_back = spread(proj_low.reshape(members, rows_local, bundle), 'fsdp')]
    dot_general x28, matrix products: 113 us -> 99.6 us  [matmul(): lax.dot_general(lhs, rhs, (dims, ((), ())), preferred_element_type=jnp.fl...]
  transfers between devices with their start and end apart: 43 -> 61, of which waited for: 25 -> 28; matrix products, arithmetic and copies ran while one was open for 23% -> 22% of each run, Pallas kernels for 2% -> 2%
where the time goes in v2:
time: 931 us; the launch traced here: 921 us
  waiting for transfers between devices  493 us (53%)
  matrix products  99.6 us (11%)
  starting transfers between devices  89.2 us (10%)
  other arithmetic  82.3 us (9%)
  local copies, waits for them, and re-layouts  82 us (9%)
  blocking collectives  40.9 us (4%)
  Pallas kernels  17.8 us (2%)
  between operations  16 us (2%)
    ppermute x42, waiting for transfers between devices, swap(): return lax.ppermute(value, axis, [(i, i ^ bit) for i in range(size)])  314 us
    all_to_all x10, waiting for transfers between devices, spread(): return lax.all_to_all(blocks, axis, split_axis=0, concat_axis=0, tiled=True)  102 us
    dot_general x28, matrix products, matmul(): lax.dot_general(lhs, rhs, (dims, ((), ())), preferred_element_type=jnp.fl...  99.6 us
    ppermute x42, starting transfers between devices, swap(): return lax.ppermute(value, axis, [(i, i ^ bit) for i in range(size)])  45.4 us
    all_to_all x10, starting transfers between devices, spread(): return lax.all_to_all(blocks, axis, split_axis=0, concat_axis=0, tiled=True)  42.8 us
    reduce_scatter x1, waiting for transfers between devices, local_fast(): lax.psum_scatter(matmul(mixed_low, down_all, ((2,), (0,))).astype(low), '...  39.2 us
    all_gather x1, waiting for transfers between devices, local_fast(): lax.all_gather(grad_branch_mlp.astype(low), 'fsdp', axis=1, tiled=True)  37.4 us
    psum x1, blocking collectives, local_fast(): lax.psum(jnp.stack([jnp.sum(queries * queries, axis=-1), jnp.sum(keys * k...  24.3 us
  transfers between devices with their start and end apart: 61, of which 28 were waited for; matrix products, arithmetic and copies ran while one was open for 22% of the time, Pallas kernels for 2%

profile of v2, /device:TPU:0, one launch (start us, length us, event | category | flops | bytes accessed | tf_op | source)
XLA Modules:
  0.0 921.3 jit_solution(8461867803240922100)
XLA Ops:
  16.7 6.5 all-to-all-start
  27.3 37.6 %all-to-all-done = bf16[8,256,256]{1,2,0:T(8,128)(2,1)S(1)} async-done(((bf16[8,256,256]{1,2,0:T(8,128)(2,1)}), bf16[8,256,256]{1,2,0:T(8,128)(2,1)S(1)}, u32[]{:S(2)}, u32[]{:S(2)}) %all-to-all-start) | async-done | bytes 1048608 | tf_op jit(solution)/shard_map/all_to_all | solution.py:564
  69.8 22.5 %collective-permute-done = bf16[2064,256]{1,0:T(8,128)(2,1)} collective-permute-done((bf16[2064,256]{1,0:T(8,128)(2,1)}, bf16[2064,256]{1,0:T(8,128)(2,1)}, u32[]{:S(2)}, u32[]{:S(2)}) %collective-permute-start) | collective-permute-done | bytes 1056800 | tf_op jit(solution)/shard_map/ppermute | solution.py:560
  98.8 3.9 copy.254
  102.7 4.4 all-to-all-start.1
  112.5 3.2 slice.700
  117.6 3.4 broadcast_select_fusion.5
  127.7 3.3 fusion.32
  134.5 21.7 %all-to-all-done.1 = bf16[8,2,256,256]{3,2,1,0:T(8,128)(2,1)} async-done(((bf16[8,2,256,256]{3,2,1,0:T(8,128)(2,1)}), bf16[8,2,256,256]{3,2,1,0:T(8,128)(2,1)}, u32[]{:S(2)}, u32[]{:S(2)}) %all-to-all-start.1) | async-done | bytes 2097184 | tf_op jit(solution)/shard_map/all_to_all | solution.py:564
  156.2 3.7 all-to-all-start.2
  165.8 24.3 %psum.14 = f32[2,3,256]{2,1,0:T(4,128)} all-reduce(f32[2,3,256]{2,1,0:T(4,128)S(1)} %pad_maximum_fusion.14), channel_id=1, replica_groups=mesh['fsdp'=8,'tp'=4] {'fsdp'}, use_global_device_ids=true, to_apply=%region_2.3 | all-reduce | flops 1536 | bytes 12288 | tf_op jit(solution)/shard_map/psum | solution.py:744
  206.8 29.6 %collective-permute-done.8 = f32[3,256]{1,0:T(4,128)S(1)} collective-permute-done((f32[3,256]{1,0:T(4,128)}, f32[3,256]{1,0:T(4,128)S(1)}, u32[]{:S(2)}, u32[]{:S(2)}) %collective-permute-start.8) | collective-permute-done | bytes 3104 | tf_op jit(solution)/shard_map/ppermute | solution.py:560
  241.7 3.1 pad_maximum_fusion.kv_ref
  244.8 6.4 attend.1
  253.3 4.2 all-to-all-start.3
  258.4 11.6 %all-to-all-done.3 = bf16[8,3,32,256]{3,2,1,0:T(8,128)(2,1)S(1)} async-done(((bf16[8,3,32,256]{3,2,1,0:T(8,128)(2,1)}), bf16[8,3,32,256]{3,2,1,0:T(8,128)(2,1)S(1)}, u32[]{:S(2)}, u32[]{:S(2)}) %all-to-all-start.3) | async-done | bytes 393248 | tf_op jit(solution)/shard_map/all_to_all | solution.py:564
  271.1 5.1 multiply_reduce_fusion.5
  286.9 20.9 %collective-permute-done.11 = bf16[2048,256]{1,0:T(8,128)(2,1)S(1)} collective-permute-done((bf16[2048,256]{1,0:T(8,128)(2,1)S(1)}, bf16[2048,256]{1,0:T(8,128)(2,1)S(1)}, u32[]{:S(2)}, u32[]{:S(2)}) %collective-permute-start.11) | collective-permute-done | bytes 1048608 | tf_op jit(solution)/shard_map/ppermute | solution.py:560
  310.4 20.7 %collective-permute-done.12 = bf16[2048,256]{1,0:T(8,128)(2,1)S(1)} collective-permute-done((bf16[2048,256]{1,0:T(8,128)(2,1)S(1)}, bf16[2048,256]{1,0:T(8,128)(2,1)S(1)}, u32[]{:S(2)}, u32[]{:S(2)}) %collective-permute-start.12) | collective-permute-done | bytes 1048608 | tf_op jit(solution)/shard_map/ppermute | solution.py:560
  333.1 20.4 %collective-permute-done.13 = bf16[2048,256]{1,0:T(8,128)(2,1)S(1)} collective-permute-done((bf16[2048,256]{1,0:T(8,128)(2,1)S(1)}, bf16[2048,256]{1,0:T(8,128)(2,1)S(1)}, u32[]{:S(2)}, u32[]{:S(2)}) %collective-permute-start.13) | collective-permute-done | bytes 1048608 | tf_op jit(solution)/shard_map/ppermute | solution.py:560
  353.6 6.9 fusion.20
  360.5 13.2 %collective-permute-done.16 = bf16[2048,256]{1,0:T(8,128)(2,1)} collective-permute-done((bf16[2048,256]{1,0:T(8,128)(2,1)}, bf16[2048,256]{1,0:T(8,128)(2,1)}, u32[]{:S(2)}, u32[]{:S(2)}) %collective-permute-start.16) | collective-permute-done | bytes 1048608 | tf_op jit(solution)/shard_map/ppermute | solution.py:560
  373.6 7.5 multiply_convert_fusion.2
  381.2 15.5 %collective-permute-done.19 = bf16[256,2048]{1,0:T(8,128)(2,1)} collective-permute-done((bf16[256,2048]{1,0:T(8,128)(2,1)}, bf16[256,2048]{1,0:T(8,128)(2,1)}, u32[]{:S(2)}, u32[]{:S(2)}) %collective-permute-start.19) | collective-permute-done | bytes 1048608 | tf_op jit(solution)/shard_map/ppermute | solution.py:560
  396.6 7.2 convolution_convert_fusion
  403.9 39.2 %reduce-scatter.4.cloned.1.call-done = bf16[3,32,2048]{2,1,0:T(8,128)(2,1)} async-done(((bf16[3,256,2048]{2,1,0:T(8,128)(2,1)}), bf16[3,32,2048]{2,1,0:T(8,128)(2,1)}) %reduce-scatter.4.cloned.1.call-update) | async-done | bytes 393232 | tf_op jit(solution)/shard_map/reduce_scatter | solution.py:798
  447.3 37.4 %all-gather.15.cloned.1.call-done = bf16[3,256,2048]{2,1,0:T(8,128)(2,1)} async-done(((bf16[3,32,2048]{2,1,0:T(8,128)(2,1)}), bf16[3,256,2048]{2,1,0:T(8,128)(2,1)}) %all-gather.15.cloned.1.call-update) | async-done | bytes 3145744 | tf_op jit(solution)/shard_map/all_gather | solution.py:812
  484.7 8.6 multiply_convert_fusion.1
  493.4 6.4 fusion.18
  499.8 5.3 add_convert_fusion.1
  505.1 4.0 convolution_convert_fusion.2
  511.5 3.2 convolution_convert_fusion.3
  517.4 39.6 %collective-permute-done.28 = bf16[2048,512]{1,0:T(8,128)(2,1)S(1)} collective-permute-done((bf16[2048,512]{1,0:T(8,128)(2,1)S(1)}, bf16[2048,512]{1,0:T(8,128)(2,1)S(1)}, u32[]{:S(2)}, u32[]{:S(2)}) %collective-permute-start.28) | collective-permute-done | bytes 2097184 | tf_op jit(solution)/shard_map/ppermute | solution.py:560
  565.5 6.1 convolution_convert_fusion.4
  576.7 4.3 all-to-all-start.4
  581.0 4.6 convert_add_fusion.2
  588.4 3.2 convolution_convert_fusion.1
  595.3 11.4 %attend_back.1 = (f32[3,256,256]{2,1,0:T(8,128)}, bf16[4,3,256,512]{3,2,1,0:T(8,128)(2,1)}) custom-call(bf16[3,256,256]{2,1,0:T(8,128)(2,1)} %pad_maximum_fusion.13.q_ref, bf16[4,3,256,512]{3,2,1,0:T(8,128)(2,1)} %pad_maximum_fusion.kv_ref, bf16[3,256,256]{2,1,0:T(8,128)(2,1)} %bitcast.351, f32[3,256,256]{2,1,0:T(8,128)} %get-tuple-element.35.out_ref, ...), custom_call_target="tpu_custom_call" | custom-call | tf_op jit(solution)/shard_map/attend_back/pallas_call | solution.py:545
  606.7 3.1 slice_bitcast_fusion.16
  615.9 4.3 all-to-all-start.6
  623.3 34.0 %collective-permute-done.23 = bf16[3,256,512]{2,1,0:T(8,128)(2,1)} collective-permute-done((bf16[3,256,512]{2,1,0:T(8,128)(2,1)}, bf16[3,256,512]{2,1,0:T(8,128)(2,1)}, u32[]{:S(2)}, u32[]{:S(2)}) %collective-permute-start.23) | collective-permute-done | bytes 786464 | tf_op jit(solution)/shard_map/ppermute | solution.py:560
  657.3 16.0 %collective-permute-done.25 = bf16[3,256,512]{2,1,0:T(8,128)(2,1)} collective-permute-done((bf16[3,256,512]{2,1,0:T(8,128)(2,1)S(1)}, bf16[3,256,512]{2,1,0:T(8,128)(2,1)}, u32[]{:S(2)}, u32[]{:S(2)}) %collective-permute-start.25) | collective-permute-done | bytes 786464 | tf_op jit(solution)/shard_map/ppermute | solution.py:560
  673.3 3.2 fusion.97
  678.9 16.6 %psum.15 = f32[2,3,256]{2,1,0:T(4,128)} all-reduce(f32[2,3,256]{2,1,0:T(4,128)} %pad_maximum_fusion.15), channel_id=1, replica_groups=mesh['fsdp'=8,'tp'=4] {'fsdp'}, use_global_device_ids=true, to_apply=%region_12.13 | all-reduce | flops 1536 | bytes 12288 | tf_op jit(solution)/shard_map/psum | solution.py:920
  701.5 4.2 all-to-all-start.5
  710.2 3.0 add_convert_fusion
  713.2 19.2 %all-to-all-done.5 = bf16[8,256,256]{2,1,0:T(8,128)(2,1)} async-done(((bf16[8,256,256]{2,1,0:T(8,128)(2,1)}), bf16[8,256,256]{2,1,0:T(8,128)(2,1)}, u32[]{:S(2)}, u32[]{:S(2)}) %all-to-all-start.5) | async-done | bytes 1048608 | tf_op jit(solution)/shard_map/all_to_all | solution.py:564
  732.6 3.2 fusion.4
  738.9 4.5 convert_add_fusion
  747.8 3.0 maximum_select_fusion
  757.4 12.2 %collective-permute-done.38 = bf16[2048,256]{1,0:T(8,128)(2,1)S(1)} collective-permute-done((bf16[2048,256]{1,0:T(8,128)(2,1)S(1)}, bf16[2048,256]{1,0:T(8,128)(2,1)S(1)}, u32[]{:S(2)}, u32[]{:S(2)}) %collective-permute-start.38) | collective-permute-done | bytes 1048608 | tf_op jit(solution)/shard_map/ppermute | solution.py:560
  771.0 3.6 all-to-all-start.7
  775.9 4.6 collective-permute-done.34
  780.5 34.2 %collective-permute-done.35 = bf16[2064,256]{1,0:T(8,128)(2,1)} collective-permute-done((bf16[2064,256]{1,0:T(8,128)(2,1)}, bf16[2064,256]{1,0:T(8,128)(2,1)}, u32[]{:S(2)}, u32[]{:S(2)}) %collective-permute-start.35) | collective-permute-done | bytes 1056800 | tf_op jit(solution)/shard_map/ppermute | solution.py:560
  822.0 4.3 all-to-all-start.8
  830.0 2.7 bitcast_convert_fusion
  835.8 3.3 multiply_reduce_fusion
  842.7 10.2 %all-to-all-done.8 = bf16[8,256,256]{1,2,0:T(8,128)(2,1)} async-done(((bf16[8,256,256]{1,2,0:T(8,128)(2,1)}), bf16[8,256,256]{1,2,0:T(8,128)(2,1)}, u32[]{:S(2)}, u32[]{:S(2)}) %all-to-all-start.8) | async-done | bytes 1048608 | tf_op jit(solution)/shard_map/all_to_all | solution.py:564
  860.1 3.5 all-to-all-start.9
  870.0 7.2 collective-permute-done.21
  879.9 2.9 fusion.6
  883.0 2.9 fusion.7
  894.4 7.4 collective-permute-done.39
  901.8 10.7 %collective-permute-done.40 = bf16[1040,256]{1,0:T(8,128)(2,1)S(1)} collective-permute-done((bf16[1040,256]{1,0:T(8,128)(2,1)S(1)}, bf16[1040,256]{1,0:T(8,128)(2,1)S(1)}, u32[]{:S(2)}, u32[]{:S(2)}) %collective-permute-start.40) | collective-permute-done | bytes 532512 | tf_op jit(solution)/shard_map/ppermute | solution.py:560
  (515 shorter events, 201.4 us)
Async XLA Ops:
  7.2 105.4 %all-gather.9.cloned.1.call-start = ((), (), s32[]{:S(2)}) async-start(), calls=%async_computation.14 | async-start | bytes 2433024 | tf_op jit(solution)/shard_map/all_gather | solution.py:692
  11.0 116.8 %all-gather.7.cloned.1.call-start = ((), (), s32[]{:S(2)}) async-start(), calls=%async_computation.13 | async-start | bytes 3538944 | tf_op jit(solution)/shard_map/all_gather | solution.py:674
  16.7 48.3 %all-to-all-start = ((bf16[8,256,256]{1,2,0:T(8,128)(2,1)}), bf16[8,256,256]{1,2,0:T(8,128)(2,1)S(1)}, u32[]{:S(2)}, u32[]{:S(2)}) async-start(bf16[8,256,256]{1,2,0:T(8,128)(2,1)} %maximum_bitcast_fusion.13), calls=%async_computation | async-start | bytes 2097152 | tf_op jit(solution)/shard_map/all_to_all | solution.py:564
  66.6 25.7 %collective-permute-start = (bf16[2064,256]{1,0:T(8,128)(2,1)}, bf16[2064,256]{1,0:T(8,128)(2,1)}, u32[]{:S(2)}, u32[]{:S(2)}) collective-permute-start(bf16[2064,256]{1,0:T(8,128)(2,1)} %copy.231), channel_id=1, source_target_pairs={{0,1},{1,0},{2,3},{3,2},{4,5},{5,4},{6,7},{7,6},{8,9},{9,8},{10,11... | collective-permute-start | bytes 3170312 | tf_op jit(solution)/shard_map/ppermute | solution.py:560
  68.1 28.2 %collective-permute-start.2 = (bf16[2064,256]{1,0:T(8,128)(2,1)}, bf16[2064,256]{1,0:T(8,128)(2,1)S(1)}, u32[]{:S(2)}, u32[]{:S(2)}) collective-permute-start(bf16[2064,256]{1,0:T(8,128)(2,1)} %copy.231), channel_id=1, source_target_pairs={{0,2},{1,3},{2,0},{3,1},{4,6},{5,7},{6,4},{7,5},{8,10},{9,11},{10,... | collective-permute-start | bytes 3170312 | tf_op jit(solution)/shard_map/ppermute | solution.py:560
  69.7 53.9 %copy-start.75 = (s32[256]{0:T(256)}, s32[256]{0:T(256)S(1)}, u32[]{:S(2)}) copy-start(s32[256]{0:T(256)S(1)} %add.255) | copy-start | bytes 3076
  94.8 20.9 %collective-permute-start.1 = (bf16[1024,256]{0,1:T(8,128)(2,1)}, bf16[1024,256]{0,1:T(8,128)(2,1)}, u32[]{:S(2)}, u32[]{:S(2)}) collective-permute-start(bf16[1024,256]{0,1:T(8,128)(2,1)} %slice.637), channel_id=1, source_target_pairs={{0,2},{1,3},{2,0},{3,1},{4,6},{5,7},{6,4},{7,5},{8,10},{9,11},{10,... | collective-permute-start | bytes 1572872 | tf_op jit(solution)/shard_map/ppermute | solution.py:560
  97.1 13.3 %collective-permute-start.3 = (bf16[1040,256]{1,0:T(8,128)(2,1)}, bf16[1040,256]{1,0:T(8,128)(2,1)}, u32[]{:S(2)}, u32[]{:S(2)}) collective-permute-start(bf16[1040,256]{1,0:T(8,128)(2,1)} %slice.638), channel_id=1, source_target_pairs={{0,1},{1,0},{2,3},{3,2},{4,5},{5,4},{6,7},{7,6},{8,9},{9,8},{10,11... | collective-permute-start | bytes 1597448 | tf_op jit(solution)/shard_map/ppermute | solution.py:560
  102.7 53.4 %all-to-all-start.1 = ((bf16[8,2,256,256]{3,2,1,0:T(8,128)(2,1)}), bf16[8,2,256,256]{3,2,1,0:T(8,128)(2,1)}, u32[]{:S(2)}, u32[]{:S(2)}) async-start(bf16[8,2,256,256]{3,2,1,0:T(8,128)(2,1)} %copy.254), calls=%async_computation.1 | async-start | bytes 4194304 | tf_op jit(solution)/shard_map/all_to_all | solution.py:564
  107.1 163.2 %all-gather.11.cloned.1.call-start = ((), (), s32[]{:S(2)}) async-start(), calls=%async_computation.15 | async-start | bytes 10485760 | tf_op jit(solution)/shard_map/all_gather | solution.py:700
  123.6 38.1 %collective-permute-start.4 = (bf16[2,2064,256]{2,1,0:T(8,128)(2,1)}, bf16[2,2064,256]{2,1,0:T(8,128)(2,1)S(1)}, u32[]{:S(2)}, u32[]{:S(2)}) collective-permute-start(bf16[2,2064,256]{2,1,0:T(8,128)(2,1)} %copy.241), channel_id=1, source_target_pairs={{0,4},{4,0},{8,12},{12,8},{16,20},{20,16},{24,28},{28,24},{1,5},{5... | collective-permute-start | bytes 6340616 | tf_op jit(solution)/shard_map/ppermute | solution.py:560
  125.6 70.2 %copy-start.36 = (f32[256,128]{1,0:T(8,128)}, f32[256,128]{1,0:T(8,128)S(1)}, u32[]{:S(2)}) copy-start(f32[256,128]{1,0:T(8,128)S(1)} %get-tuple-element.242) | copy-start | bytes 393220
  156.2 96.3 %all-to-all-start.2 = ((bf16[8,256,256]{2,1,0:T(8,128)(2,1)}), bf16[8,256,256]{2,1,0:T(8,128)(2,1)S(1)}, u32[]{:S(2)}, u32[]{:S(2)}) async-start(bf16[8,256,256]{2,1,0:T(8,128)(2,1)} %bitcast.355), calls=%async_computation.2 | async-start | bytes 2097152 | tf_op jit(solution)/shard_map/all_to_all | solution.py:564
  199.3 42.5 %collective-permute-start.5 = (bf16[3,256,512]{2,1,0:T(8,128)(2,1)S(1)}, bf16[3,256,512]{2,1,0:T(8,128)(2,1)}, u32[]{:S(2)}, u32[]{:S(2)}) collective-permute-start(bf16[3,256,512]{2,1,0:T(8,128)(2,1)S(1)} %concatenate.171), channel_id=1, source_target_pairs={{0,1},{1,0},{2,3},{3,2},{4,5},{5,4},{6,7},{7,6},{8,9},{9,8},{10,11... | collective-permute-start | bytes 2359304 | tf_op jit(solution)/shard_map/ppermute | solution.py:560
  199.9 41.9 %collective-permute-start.6 = (bf16[3,256,512]{2,1,0:T(8,128)(2,1)S(1)}, bf16[3,256,512]{2,1,0:T(8,128)(2,1)}, u32[]{:S(2)}, u32[]{:S(2)}) collective-permute-start(bf16[3,256,512]{2,1,0:T(8,128)(2,1)S(1)} %concatenate.171), channel_id=1, source_target_pairs={{0,2},{1,3},{2,0},{3,1},{4,6},{5,7},{6,4},{7,5},{8,10},{9,11},{10,... | collective-permute-start | bytes 2359304 | tf_op jit(solution)/shard_map/ppermute | solution.py:560
  200.5 41.3 %collective-permute-start.7 = (bf16[3,256,512]{2,1,0:T(8,128)(2,1)S(1)}, bf16[3,256,512]{2,1,0:T(8,128)(2,1)}, u32[]{:S(2)}, u32[]{:S(2)}) collective-permute-start(bf16[3,256,512]{2,1,0:T(8,128)(2,1)S(1)} %concatenate.171), channel_id=1, source_target_pairs={{0,3},{1,2},{2,1},{3,0},{4,7},{5,6},{6,5},{7,4},{8,11},{9,10},{10,... | collective-permute-start | bytes 2359304 | tf_op jit(solution)/shard_map/ppermute | solution.py:560
  202.8 33.6 %collective-permute-start.8 = (f32[3,256]{1,0:T(4,128)}, f32[3,256]{1,0:T(4,128)S(1)}, u32[]{:S(2)}, u32[]{:S(2)}) collective-permute-start(f32[3,256]{1,0:T(4,128)} %get-tuple-element.234), channel_id=1, source_target_pairs={{0,1},{1,0},{2,3},{3,2},{4,5},{5,4},{6,7},{7,6},{8,9},{9,8},{10,11... | collective-permute-start | bytes 9224 | tf_op jit(solution)/shard_map/ppermute | solution.py:560
  206.2 33.3 %collective-permute-start.9 = (f32[3,256]{1,0:T(4,128)}, f32[3,256]{1,0:T(4,128)S(1)}, u32[]{:S(2)}, u32[]{:S(2)}) collective-permute-start(f32[3,256]{1,0:T(4,128)} %get-tuple-element.234), channel_id=1, source_target_pairs={{0,2},{1,3},{2,0},{3,1},{4,6},{5,7},{6,4},{7,5},{8,10},{9,11},{10,... | collective-permute-start | bytes 9224 | tf_op jit(solution)/shard_map/ppermute | solution.py:560
  236.4 4.7 collective-permute-start.10
  253.3 16.7 %all-to-all-start.3 = ((bf16[8,3,32,256]{3,2,1,0:T(8,128)(2,1)}), bf16[8,3,32,256]{3,2,1,0:T(8,128)(2,1)S(1)}, u32[]{:S(2)}, u32[]{:S(2)}) async-start(bf16[8,3,32,256]{3,2,1,0:T(8,128)(2,1)} %bitcast.352), calls=%async_computation.3 | async-start | bytes 786432 | tf_op jit(solution)/shard_map/all_to_all | solution.py:564
  257.5 96.1 %all-gather.13.cloned.1.call-start = ((), (), s32[]{:S(2)}) async-start(), calls=%async_computation.16 | async-start | bytes 3538944 | tf_op jit(solution)/shard_map/all_gather | solution.py:792
  258.4 185.9 %copy-start.62 = (f32[1,2048]{1,0:T(1,128)}, f32[1,2048]{1,0:T(1,128)S(1)}, u32[]{:S(2)}) copy-start(f32[1,2048]{1,0:T(1,128)S(1)} %get-tuple-element.134) | copy-start | bytes 24580
  278.9 164.3 %reduce-scatter.4.cloned.1.call-start = ((), (), s32[]{:S(2)}) async-start(), calls=%async_computation.17 | async-start | bytes 3538944 | tf_op jit(solution)/shard_map/reduce_scatter | solution.py:798
  281.8 26.0 %collective-permute-start.11 = (bf16[2048,256]{1,0:T(8,128)(2,1)S(1)}, bf16[2048,256]{1,0:T(8,128)(2,1)S(1)}, u32[]{:S(2)}, u32[]{:S(2)}) collective-permute-start(bf16[2048,256]{1,0:T(8,128)(2,1)S(1)} %bitcast.361), channel_id=1, source_target_pairs={{0,1},{1,0},{2,3},{3,2},{4,5},{5,4},{6,7},{7,6},{8,9},{9,8},{10,11... | collective-permute-start | bytes 3145736 | tf_op jit(solution)/shard_map/ppermute | solution.py:560
  282.4 26.8 %collective-permute-start.15 = (bf16[2048,256]{1,0:T(8,128)(2,1)}, bf16[2048,256]{1,0:T(8,128)(2,1)}, u32[]{:S(2)}, u32[]{:S(2)}) collective-permute-start(bf16[2048,256]{1,0:T(8,128)(2,1)} %bitcast.52), channel_id=1, source_target_pairs={{0,2},{1,3},{2,0},{3,1},{4,6},{5,7},{6,4},{7,5},{8,10},{9,11},{10,... | collective-permute-start | bytes 3145736 | tf_op jit(solution)/shard_map/ppermute | solution.py:560
  283.1 48.0 %collective-permute-start.12 = (bf16[2048,256]{1,0:T(8,128)(2,1)S(1)}, bf16[2048,256]{1,0:T(8,128)(2,1)S(1)}, u32[]{:S(2)}, u32[]{:S(2)}) collective-permute-start(bf16[2048,256]{1,0:T(8,128)(2,1)S(1)} %bitcast.362), channel_id=1, source_target_pairs={{0,2},{1,3},{2,0},{3,1},{4,6},{5,7},{6,4},{7,5},{8,10},{9,11},{10,... | collective-permute-start | bytes 3145736 | tf_op jit(solution)/shard_map/ppermute | solution.py:560
  285.5 46.5 %collective-permute-start.17 = (bf16[256,2048]{1,0:T(8,128)(2,1)}, bf16[256,2048]{1,0:T(8,128)(2,1)}, u32[]{:S(2)}, u32[]{:S(2)}) collective-permute-start(bf16[256,2048]{1,0:T(8,128)(2,1)} %bitcast.159), channel_id=1, source_target_pairs={{0,1},{1,0},{2,3},{3,2},{4,5},{5,4},{6,7},{7,6},{8,9},{9,8},{10,11... | collective-permute-start | bytes 3145736 | tf_op jit(solution)/shard_map/ppermute | solution.py:560
  307.8 45.7 %collective-permute-start.13 = (bf16[2048,256]{1,0:T(8,128)(2,1)S(1)}, bf16[2048,256]{1,0:T(8,128)(2,1)S(1)}, u32[]{:S(2)}, u32[]{:S(2)}) collective-permute-start(bf16[2048,256]{1,0:T(8,128)(2,1)S(1)} %collective-permute-done.11), channel_id=1, source_target_pairs={{0,2},{1,3},{2,0},{3,1},{4,6},{5,7},{6,4},{7,5},{8,10},{9,11},{10,... | collective-permute-start | bytes 3145736 | tf_op jit(solution)/shard_map/ppermute | solution.py:560
  308.4 52.1 %collective-permute-start.14 = (bf16[2048,256]{1,0:T(8,128)(2,1)}, bf16[2048,256]{1,0:T(8,128)(2,1)}, u32[]{:S(2)}, u32[]{:S(2)}) collective-permute-start(bf16[2048,256]{1,0:T(8,128)(2,1)} %bitcast.52), channel_id=1, source_target_pairs={{0,1},{1,0},{2,3},{3,2},{4,5},{5,4},{6,7},{7,6},{8,9},{9,8},{10,11... | collective-permute-start | bytes 3145736 | tf_op jit(solution)/shard_map/ppermute | solution.py:560
  309.1 64.5 %collective-permute-start.16 = (bf16[2048,256]{1,0:T(8,128)(2,1)}, bf16[2048,256]{1,0:T(8,128)(2,1)}, u32[]{:S(2)}, u32[]{:S(2)}) collective-permute-start(bf16[2048,256]{1,0:T(8,128)(2,1)} %collective-permute-done.15), channel_id=1, source_target_pairs={{0,1},{1,0},{2,3},{3,2},{4,5},{5,4},{6,7},{7,6},{8,9},{9,8},{10,11... | collective-permute-start | bytes 3145736 | tf_op jit(solution)/shard_map/ppermute | solution.py:560
  331.1 50.1 %collective-permute-start.18 = (bf16[256,2048]{1,0:T(8,128)(2,1)}, bf16[256,2048]{1,0:T(8,128)(2,1)}, u32[]{:S(2)}, u32[]{:S(2)}) collective-permute-start(bf16[256,2048]{1,0:T(8,128)(2,1)} %bitcast.159), channel_id=1, source_target_pairs={{0,2},{1,3},{2,0},{3,1},{4,6},{5,7},{6,4},{7,5},{8,10},{9,11},{10,... | collective-permute-start | bytes 3145736 | tf_op jit(solution)/shard_map/ppermute | solution.py:560
  332.0 64.6 %collective-permute-start.19 = (bf16[256,2048]{1,0:T(8,128)(2,1)}, bf16[256,2048]{1,0:T(8,128)(2,1)}, u32[]{:S(2)}, u32[]{:S(2)}) collective-permute-start(bf16[256,2048]{1,0:T(8,128)(2,1)} %collective-permute-done.17), channel_id=1, source_target_pairs={{0,2},{1,3},{2,0},{3,1},{4,6},{5,7},{6,4},{7,5},{8,10},{9,11},{10,... | collective-permute-start | bytes 3145736 | tf_op jit(solution)/shard_map/ppermute | solution.py:560
  403.9 80.8 %all-gather.15.cloned.1.call-start = ((), (), s32[]{:S(2)}) async-start(), calls=%async_computation.18 | async-start | bytes 3538944 | tf_op jit(solution)/shard_map/all_gather | solution.py:812
  447.0 116.5 %reduce-scatter.6.cloned.1.call-start = ((), (), s32[]{:S(2)}) async-start(), calls=%async_computation.19 | async-start | bytes 3538944 | tf_op jit(solution)/shard_map/reduce_scatter | solution.py:822
  509.2 47.8 %collective-permute-start.28 = (bf16[2048,512]{1,0:T(8,128)(2,1)S(1)}, bf16[2048,512]{1,0:T(8,128)(2,1)S(1)}, u32[]{:S(2)}, u32[]{:S(2)}) collective-permute-start(bf16[2048,512]{1,0:T(8,128)(2,1)S(1)} %convolution_convert_fusion.2), channel_id=1, source_target_pairs={{0,2},{1,3},{2,0},{3,1},{4,6},{5,7},{6,4},{7,5},{8,10},{9,11},{10,... | collective-permute-start | bytes 6291464 | tf_op jit(solution)/shard_map/ppermute | solution.py:560
  514.7 66.3 %collective-permute-start.26 = (bf16[512,2048]{1,0:T(8,128)(2,1)}, bf16[512,2048]{1,0:T(8,128)(2,1)}, u32[]{:S(2)}, u32[]{:S(2)}) collective-permute-start(bf16[512,2048]{1,0:T(8,128)(2,1)} %convolution_convert_fusion.3), channel_id=1, source_target_pairs={{0,1},{1,0},{2,3},{3,2},{4,5},{5,4},{6,7},{7,6},{8,9},{9,8},{10,11... | collective-permute-start | bytes 6291464 | tf_op jit(solution)/shard_map/ppermute | solution.py:560
  562.0 49.8 %collective-permute-start.29 = (bf16[2048,256]{1,0:T(8,128)(2,1)}, bf16[2048,256]{1,0:T(8,128)(2,1)}, u32[]{:S(2)}, u32[]{:S(2)}) collective-permute-start(bf16[2048,256]{1,0:T(8,128)(2,1)} %split.46), channel_id=1, source_target_pairs={{0,1},{1,0},{2,3},{3,2},{4,5},{5,4},{6,7},{7,6},{8,9},{9,8},{10,11... | collective-permute-start | bytes 3145736 | tf_op jit(solution)/shard_map/ppermute | solution.py:560
  576.7 16.8 %all-to-all-start.4 = ((bf16[8,3,32,256]{3,2,1,0:T(8,128)(2,1)}), bf16[8,3,32,256]{3,2,1,0:T(8,128)(2,1)}, u32[]{:S(2)}, u32[]{:S(2)}) async-start(bf16[8,3,32,256]{3,2,1,0:T(8,128)(2,1)} %constant_dynamic-update-slice_fusion.16), calls=%async_computation.6 | async-start | bytes 786432 | tf_op jit(solution)/shard_map/all_to_all | solution.py:564
  586.9 33.2 %collective-permute-start.27 = (bf16[256,2048]{1,0:T(8,128)(2,1)}, bf16[256,2048]{1,0:T(8,128)(2,1)}, u32[]{:S(2)}, u32[]{:S(2)}) collective-permute-start(bf16[256,2048]{1,0:T(8,128)(2,1)} %split.47), channel_id=1, source_target_pairs={{0,2},{1,3},{2,0},{3,1},{4,6},{5,7},{6,4},{7,5},{8,10},{9,11},{10,... | collective-permute-start | bytes 3145736 | tf_op jit(solution)/shard_map/ppermute | solution.py:560
  591.6 147.2 %collective-permute-start.37 = (bf16[2048,512]{1,0:T(8,128)(2,1)}, bf16[2048,512]{1,0:T(8,128)(2,1)}, u32[]{:S(2)}, u32[]{:S(2)}) collective-permute-start(bf16[2048,512]{1,0:T(8,128)(2,1)} %convolution_convert_fusion.1), channel_id=1, source_target_pairs={{0,1},{1,0},{2,3},{3,2},{4,5},{5,4},{6,7},{7,6},{8,9},{9,8},{10,11... | collective-permute-start | bytes 6291464 | tf_op jit(solution)/shard_map/ppermute | solution.py:560
  609.7 47.5 %collective-permute-start.23 = (bf16[3,256,512]{2,1,0:T(8,128)(2,1)}, bf16[3,256,512]{2,1,0:T(8,128)(2,1)}, u32[]{:S(2)}, u32[]{:S(2)}) collective-permute-start(bf16[3,256,512]{2,1,0:T(8,128)(2,1)} %get-tuple-element.131), channel_id=1, source_target_pairs={{0,1},{1,0},{2,3},{3,2},{4,5},{5,4},{6,7},{7,6},{8,9},{9,8},{10,11... | collective-permute-start | bytes 2359304 | tf_op jit(solution)/shard_map/ppermute | solution.py:560
  610.4 46.9 %collective-permute-start.24 = (bf16[3,256,512]{2,1,0:T(8,128)(2,1)}, bf16[3,256,512]{2,1,0:T(8,128)(2,1)}, u32[]{:S(2)}, u32[]{:S(2)}) collective-permute-start(bf16[3,256,512]{2,1,0:T(8,128)(2,1)} %get-tuple-element.133), channel_id=1, source_target_pairs={{0,2},{1,3},{2,0},{3,1},{4,6},{5,7},{6,4},{7,5},{8,10},{9,11},{10,... | collective-permute-start | bytes 2359304 | tf_op jit(solution)/shard_map/ppermute | solution.py:560
  611.8 61.5 %collective-permute-start.25 = (bf16[3,256,512]{2,1,0:T(8,128)(2,1)S(1)}, bf16[3,256,512]{2,1,0:T(8,128)(2,1)}, u32[]{:S(2)}, u32[]{:S(2)}) collective-permute-start(bf16[3,256,512]{2,1,0:T(8,128)(2,1)S(1)} %get-tuple-element.132), channel_id=1, source_target_pairs={{0,3},{1,2},{2,1},{3,0},{4,7},{5,6},{6,5},{7,4},{8,11},{9,10},{10,... | collective-permute-start | bytes 2359304 | tf_op jit(solution)/shard_map/ppermute | solution.py:560
  615.9 85.7 %all-to-all-start.6 = ((bf16[8,256,256]{2,1,0:T(8,128)(2,1)}), bf16[8,256,256]{2,1,0:T(8,128)(2,1)}, u32[]{:S(2)}, u32[]{:S(2)}) async-start(bf16[8,256,256]{2,1,0:T(8,128)(2,1)} %bitcast.335), calls=%async_computation.8 | async-start | bytes 2097152 | tf_op jit(solution)/shard_map/all_to_all | solution.py:564
  701.5 30.8 %all-to-all-start.5 = ((bf16[8,256,256]{2,1,0:T(8,128)(2,1)}), bf16[8,256,256]{2,1,0:T(8,128)(2,1)}, u32[]{:S(2)}, u32[]{:S(2)}) async-start(bf16[8,256,256]{2,1,0:T(8,128)(2,1)} %bitcast.330), calls=%async_computation.7 | async-start | bytes 2097152 | tf_op jit(solution)/shard_map/all_to_all | solution.py:564
  705.8 130.0 %reduce-scatter.8.cloned.1.call-start = ((), (), s32[]{:S(2)}) async-start(), calls=%async_computation.20 | async-start | bytes 3538944 | tf_op jit(solution)/shard_map/reduce_scatter | solution.py:951
  738.8 9.0 collective-permute-start.33
  743.5 26.1 %collective-permute-start.38 = (bf16[2048,256]{1,0:T(8,128)(2,1)S(1)}, bf16[2048,256]{1,0:T(8,128)(2,1)S(1)}, u32[]{:S(2)}, u32[]{:S(2)}) collective-permute-start(bf16[2048,256]{1,0:T(8,128)(2,1)S(1)} %split.45), channel_id=1, source_target_pairs={{0,2},{1,3},{2,0},{3,1},{4,6},{5,7},{6,4},{7,5},{8,10},{9,11},{10,... | collective-permute-start | bytes 3145736 | tf_op jit(solution)/shard_map/ppermute | solution.py:560
  753.9 26.5 %collective-permute-start.34 = (bf16[2064,256]{1,0:T(8,128)(2,1)}, bf16[2064,256]{1,0:T(8,128)(2,1)}, u32[]{:S(2)}, u32[]{:S(2)}) collective-permute-start(bf16[2064,256]{1,0:T(8,128)(2,1)} %get-tuple-element.127), channel_id=1, source_target_pairs={{0,1},{1,0},{2,3},{3,2},{4,5},{5,4},{6,7},{7,6},{8,9},{9,8},{10,11... | collective-permute-start | bytes 3170312 | tf_op jit(solution)/shard_map/ppermute | solution.py:560
  754.5 60.2 %collective-permute-start.35 = (bf16[2064,256]{1,0:T(8,128)(2,1)}, bf16[2064,256]{1,0:T(8,128)(2,1)}, u32[]{:S(2)}, u32[]{:S(2)}) collective-permute-start(bf16[2064,256]{1,0:T(8,128)(2,1)} %get-tuple-element.129), channel_id=1, source_target_pairs={{0,2},{1,3},{2,0},{3,1},{4,6},{5,7},{6,4},{7,5},{8,10},{9,11},{10,... | collective-permute-start | bytes 3170312 | tf_op jit(solution)/shard_map/ppermute | solution.py:560
  755.1 59.6 %collective-permute-start.36 = (bf16[2064,256]{1,0:T(8,128)(2,1)}, bf16[2064,256]{1,0:T(8,128)(2,1)}, u32[]{:S(2)}, u32[]{:S(2)}) collective-permute-start(bf16[2064,256]{1,0:T(8,128)(2,1)} %get-tuple-element.128), channel_id=1, source_target_pairs={{0,3},{1,2},{2,1},{3,0},{4,7},{5,6},{6,5},{7,4},{8,11},{9,10},{10,... | collective-permute-start | bytes 3170312 | tf_op jit(solution)/shard_map/ppermute | solution.py:560
  771.0 48.8 %all-to-all-start.7 = ((bf16[8,256,256]{2,1,0:T(8,128)(2,1)}), bf16[8,256,256]{2,1,0:T(8,128)(2,1)S(1)}, u32[]{:S(2)}, u32[]{:S(2)}) async-start(bf16[8,256,256]{2,1,0:T(8,128)(2,1)} %bitcast.336), calls=%async_computation.10 | async-start | bytes 2097152 | tf_op jit(solution)/shard_map/all_to_all | solution.py:564
  774.5 105.4 %all-gather.17.cloned.1.call-start = ((), (), s32[]{:S(2)}) async-start(), calls=%async_computation.21 | async-start | bytes 3538944 | tf_op jit(solution)/shard_map/all_gather | solution.py:887
  822.0 30.8 %all-to-all-start.8 = ((bf16[8,256,256]{1,2,0:T(8,128)(2,1)}), bf16[8,256,256]{1,2,0:T(8,128)(2,1)}, u32[]{:S(2)}, u32[]{:S(2)}) async-start(bf16[8,256,256]{1,2,0:T(8,128)(2,1)} %copy.270), calls=%async_computation.11 | async-start | bytes 2097152 | tf_op jit(solution)/shard_map/all_to_all | solution.py:564
  839.2 24.4 %collective-permute-start.30 = (bf16[3,32,2048]{2,1,0:T(8,128)(2,1)S(1)}, bf16[3,32,2048]{2,1,0:T(8,128)(2,1)S(1)}, u32[]{:S(2)}, u32[]{:S(2)}) collective-permute-start(bf16[3,32,2048]{2,1,0:T(8,128)(2,1)S(1)} %get-tuple-element.130), channel_id=1, source_target_pairs={{0,3},{1,2},{2,1},{3,0},{4,7},{5,6},{6,5},{7,4},{8,11},{9,10},{10,... | collective-permute-start | bytes 1179656 | tf_op jit(solution)/shard_map/ppermute | solution.py:560
  840.6 24.4 %collective-permute-start.31 = (bf16[3,32,2048]{2,1,0:T(8,128)(2,1)S(1)}, bf16[3,32,2048]{2,1,0:T(8,128)(2,1)S(1)}, u32[]{:S(2)}, u32[]{:S(2)}) collective-permute-start(bf16[3,32,2048]{2,1,0:T(8,128)(2,1)S(1)} %get-tuple-element.130), channel_id=1, source_target_pairs={{0,2},{1,3},{2,0},{3,1},{4,6},{5,7},{6,4},{7,5},{8,10},{9,11},{10,... | collective-permute-start | bytes 1179656 | tf_op jit(solution)/shard_map/ppermute | solution.py:560
  841.3 23.8 %collective-permute-start.32 = (bf16[3,32,2048]{2,1,0:T(8,128)(2,1)S(1)}, bf16[3,32,2048]{2,1,0:T(8,128)(2,1)}, u32[]{:S(2)}, u32[]{:S(2)}) collective-permute-start(bf16[3,32,2048]{2,1,0:T(8,128)(2,1)S(1)} %get-tuple-element.130), channel_id=1, source_target_pairs={{0,1},{1,0},{2,3},{3,2},{4,5},{5,4},{6,7},{7,6},{8,9},{9,8},{10,11... | collective-permute-start | bytes 1179656 | tf_op jit(solution)/shard_map/ppermute | solution.py:560
  857.1 12.9 %collective-permute-start.20 = (bf16[3,32,2048]{2,1,0:T(8,128)(2,1)}, bf16[3,32,2048]{2,1,0:T(8,128)(2,1)S(1)}, u32[]{:S(2)}, u32[]{:S(2)}) collective-permute-start(bf16[3,32,2048]{2,1,0:T(8,128)(2,1)} %get-tuple-element.163), channel_id=1, source_target_pairs={{0,3},{1,2},{2,1},{3,0},{4,7},{5,6},{6,5},{7,4},{8,11},{9,10},{10,... | collective-permute-start | bytes 1179656 | tf_op jit(solution)/shard_map/ppermute | solution.py:560
  858.6 18.6 %collective-permute-start.21 = (bf16[3,32,2048]{2,1,0:T(8,128)(2,1)}, bf16[3,32,2048]{2,1,0:T(8,128)(2,1)S(1)}, u32[]{:S(2)}, u32[]{:S(2)}) collective-permute-start(bf16[3,32,2048]{2,1,0:T(8,128)(2,1)} %get-tuple-element.163), channel_id=1, source_target_pairs={{0,2},{1,3},{2,0},{3,1},{4,6},{5,7},{6,4},{7,5},{8,10},{9,11},{10,... | collective-permute-start | bytes 1179656 | tf_op jit(solution)/shard_map/ppermute | solution.py:560
  860.1 19.5 %all-to-all-start.9 = ((bf16[8,112,256]{2,1,0:T(8,128)(2,1)}), bf16[8,112,256]{2,1,0:T(8,128)(2,1)S(1)}, u32[]{:S(2)}, u32[]{:S(2)}) async-start(bf16[8,112,256]{2,1,0:T(8,128)(2,1)} %maximum_bitcast_fusion.14), calls=%async_computation.12 | async-start | bytes 917504 | tf_op jit(solution)/shard_map/all_to_all | solution.py:564
  863.6 13.7 %collective-permute-start.22 = (bf16[3,32,2048]{2,1,0:T(8,128)(2,1)}, bf16[3,32,2048]{2,1,0:T(8,128)(2,1)S(1)}, u32[]{:S(2)}, u32[]{:S(2)}) collective-permute-start(bf16[3,32,2048]{2,1,0:T(8,128)(2,1)} %get-tuple-element.163), channel_id=1, source_target_pairs={{0,1},{1,0},{2,3},{3,2},{4,5},{5,4},{6,7},{7,6},{8,9},{9,8},{10,11... | collective-permute-start | bytes 1179656 | tf_op jit(solution)/shard_map/ppermute | solution.py:560
  886.7 15.0 %collective-permute-start.39 = (bf16[1040,256]{1,0:T(8,128)(2,1)S(1)}, bf16[1040,256]{1,0:T(8,128)(2,1)S(1)}, u32[]{:S(2)}, u32[]{:S(2)}) collective-permute-start(bf16[1040,256]{1,0:T(8,128)(2,1)S(1)} %get-tuple-element.136), channel_id=1, source_target_pairs={{0,1},{1,0},{2,3},{3,2},{4,5},{5,4},{6,7},{7,6},{8,9},{9,8},{10,11... | collective-permute-start | bytes 1597448 | tf_op jit(solution)/shard_map/ppermute | solution.py:560
  887.3 25.2 %collective-permute-start.40 = (bf16[1040,256]{1,0:T(8,128)(2,1)S(1)}, bf16[1040,256]{1,0:T(8,128)(2,1)S(1)}, u32[]{:S(2)}, u32[]{:S(2)}) collective-permute-start(bf16[1040,256]{1,0:T(8,128)(2,1)S(1)} %get-tuple-element.138), channel_id=1, source_target_pairs={{0,2},{1,3},{2,0},{3,1},{4,6},{5,7},{6,4},{7,5},{8,10},{9,11},{10,... | collective-permute-start | bytes 1597448 | tf_op jit(solution)/shard_map/ppermute | solution.py:560
  888.7 23.8 %collective-permute-start.41 = (bf16[1040,256]{1,0:T(8,128)(2,1)S(1)}, bf16[1040,256]{1,0:T(8,128)(2,1)S(1)}, u32[]{:S(2)}, u32[]{:S(2)}) collective-permute-start(bf16[1040,256]{1,0:T(8,128)(2,1)S(1)} %get-tuple-element.137), channel_id=1, source_target_pairs={{0,3},{1,2},{2,1},{3,0},{4,7},{5,6},{6,5},{7,4},{8,11},{9,10},{10,... | collective-permute-start | bytes 1597448 | tf_op jit(solution)/shard_map/ppermute | solution.py:560
  (107 other events, 1180.6 us)
Sparse Core Ops, SparseCore 0:
  11.1 53.5 all-gather.8
  66.8 36.3 all-gather.6
  115.8 85.4 all-gather.10
  279.0 35.4 all-gather.12
  404.0 39.0 reduce-scatter.3
  447.1 37.5 all-gather.14
  505.3 39.2 reduce-scatter.5
  732.5 38.3 reduce-scatter.7
  776.9 51.0 all-gather.16

commit v3 on v2

--- a/solution.py
+++ b/solution.py
@@ -588,9 +588,7 @@
     return lax.optimization_barrier(values)
 
 
-def gather_tp(piece, first):
-    one = swap(piece, "tp", 1)
-    two = swap(piece, "tp", 2)
+def gather_tp(piece, one, two, first):
     three = swap(one, "tp", 2) if first == 1 else swap(two, "tp", 1)
     return (piece, one, two, three)
 
@@ -738,9 +736,9 @@
     key_low = rotate(keys * gain_key, 1.0).astype(low)
     both = jnp.concatenate([key_low, values.astype(low)], axis=-1)
     both, gate_up = tie(both, gate_up)
-    gate_all = jnp.concatenate(gather_tp(gate_up[:, 0].reshape(width, unit), 1), axis=1)
-    up_all = jnp.concatenate(gather_tp(gate_up[:, 1].reshape(width, unit), 2), axis=1)
     both = jnp.stack(others(both))
+    gate_own, up_own = gate_up[:, 0].reshape(width, unit), gate_up[:, 1].reshape(width, unit)
+    near_weights = [swap(weight, "tp", bit) for weight in (gate_own, up_own) for bit in (1, 2)]
     square_sums = lax.psum(
         jnp.stack([jnp.sum(queries * queries, axis=-1), jnp.sum(keys * keys, axis=-1)]), "fsdp"
     )
@@ -750,6 +748,9 @@
     query_low = rotate(queries * query_scale * gain_query, 1.0).astype(low)
     qpos = query_pos[:, None]
     kpos = all_pos[:, None, :]
+    query_low, down = tie(query_low, down)
+    down_own = down.transpose(1, 0, 2).reshape(unit, width)
+    near_weights += [swap(down_own, "tp", bit) for bit in (1, 2)]
     attended, log_total = attend_tiles(query_low, both, qpos, kpos, all_key_scale)
 
     places = [(chip, half, side) for chip in range(chips) for half in range(2) for side in range(2)]
@@ -782,10 +783,10 @@
         return spread(blocks, "fsdp").transpose(1, 0, 2, 3).reshape(batch_rows, count, pair)
 
     attended_low = attended.astype(low)
-    attended_low, down = tie(attended_low, down)
-    down_all = jnp.concatenate(
-        gather_tp(down.transpose(1, 0, 2).reshape(unit, width), 1), axis=0
-    )
+    attended_low, *near_weights = tie(attended_low, *near_weights)
+    gate_all = jnp.concatenate(gather_tp(gate_own, *near_weights[:2], 1), axis=1)
+    up_all = jnp.concatenate(gather_tp(up_own, *near_weights[2:4], 2), axis=1)
+    down_all = jnp.concatenate(gather_tp(down_own, *near_weights[4:], 1), axis=0)
     branch_attn = matmul(to_tokens(attended_low), out_full, ((2,), (0,)))
     attn_norm = lax.rsqrt(jnp.mean(branch_attn * branch_attn, axis=-1, keepdims=True) + epsilon)
     hidden = own_tokens + branch_attn * attn_norm * gain_attn
@@ -795,8 +796,12 @@
     up_act = matmul(hidden_low, up_all, ((2,), (0,)))
     gate_sigma = jax.nn.sigmoid(gate_act)
     mixed_low = (gate_act * gate_sigma * up_act).astype(low)
+    attended_all = lax.all_gather(attended_low, "fsdp", axis=2, tiled=True)
+    branch_low, attended_all = tie(
+        matmul(mixed_low, down_all, ((2,), (0,))).astype(low), attended_all
+    )
     branch_mlp = lax.psum_scatter(
-        matmul(mixed_low, down_all, ((2,), (0,))).astype(low),
+        branch_low,
         "fsdp",
         scatter_dimension=1,
         tiled=True,
@@ -804,13 +809,13 @@
     mlp_norm = lax.rsqrt(jnp.mean(branch_mlp * branch_mlp, axis=-1, keepdims=True) + epsilon)
     layer_own = hidden + branch_mlp * mlp_norm * gain_mlp
 
-    def whole_span(value):
-        pieces = in_order(others(value.astype(low)), part)
+    def whole_span(pieces):
+        pieces = in_order(pieces, part)
         return jnp.concatenate(pieces, axis=1).astype(jnp.float32)
 
     grad_gain_mlp, grad_branch_mlp = norm_back(branch_mlp, mlp_norm, gain_mlp, own_cotangent)
     grad_mlp_low = lax.all_gather(grad_branch_mlp.astype(low), "fsdp", axis=1, tiled=True)
-    layer_out = whole_span(layer_own)
+    layer_pieces = others(layer_own.astype(low))
     grad_mixed = matmul(grad_mlp_low, down_all, ((2,), (1,)))
     grad_gate_act = (
         grad_mixed * up_act * gate_sigma * (1.0 + gate_act * (1.0 - gate_sigma))
@@ -819,8 +824,10 @@
     mlp_back_in = matmul(grad_gate_act, gate_all, ((2,), (1,))) + matmul(
         grad_up_act, up_all, ((2,), (1,))
     )
+    mlp_back_low, *layer_pieces = tie(mlp_back_in.astype(low), *layer_pieces)
+    layer_out = whole_span(layer_pieces)
     grad_hidden = own_cotangent + lax.psum_scatter(
-        mlp_back_in.astype(low), "fsdp", scatter_dimension=1, tiled=True
+        mlp_back_low, "fsdp", scatter_dimension=1, tiled=True
     ).astype(jnp.float32)
 
     hidden_flat = hidden_low.reshape(tile, width)
@@ -884,7 +891,6 @@
     gain_sums = jnp.sum(
         feature_blocks[:, batch_rows * sub :].astype(jnp.float32), axis=0
     )
-    attended_all = lax.all_gather(attended_low, "fsdp", axis=2, tiled=True)
     own_features = own_features.transpose(1, 0, 2, 3).reshape(batch_rows, count, rows_local)
     in_group = (group_ids[:, 0][:, None] == jnp.arange(GROUPS, dtype=jnp.int32)[None, :]).astype(
         low
@@ -945,13 +951,12 @@
     attn_back_in = sum(
         matmul(grad, piece[:width], ((2,), (1,))) for grad, piece in zip(grad_acts, weight_pieces)
     )
-    attn_back_low, down_back, gate_back = tie(attn_back_in.astype(low), down_back, gate_back)
+    attn_back_low, down_back = tie(attn_back_in.astype(low), down_back)
     grad_down = down_back.reshape(members * unit, rows_local).astype(jnp.float32)
-    grad_gate = unit_columns(gate_back)
     input_own = grad_hidden + lax.psum_scatter(
         attn_back_low, "fsdp", scatter_dimension=1, tiled=True
     ).astype(jnp.float32)
-    input_grad = whole_span(input_own)
+    input_grad = whole_span(others(input_own.astype(low)))
 
     token_flat = token_low.reshape(tile, width)
 
@@ -976,7 +981,8 @@
     proj_sum = reduce_tp(proj_blocks, part)
     grad_query_gain = proj_sum[width, :64]
     grad_key_gain = proj_sum[width, 64:128]
-    proj_low, up_back = tie(proj_sum[:width].astype(low), up_back)
+    proj_low, gate_back, up_back = tie(proj_sum[:width].astype(low), gate_back, up_back)
+    grad_gate = unit_columns(gate_back)
     grad_up = unit_columns(up_back)
     proj_back = spread(proj_low.reshape(members, rows_local, bundle), "fsdp")
 

time: 931 us -> 945 us (1.015)
  waiting for transfers between devices: 493 us -> 506 us
    ppermute x42, waiting for transfers between devices: 314 us -> 297 us  [swap(): return lax.ppermute(value, axis, [(i, i ^ bit) for i in range(size)])]
    all_gather x1, waiting for transfers between devices: 0.02 us -> 16.1 us  [local_fast(): attended_all = lax.all_gather(attended_low, 'fsdp', axis=2, tiled=True)]
    unnamed x246 -> x200, local copies, waits for them, and re-layouts: 16.5 us -> 22.4 us
  transfers between devices with their start and end apart: 61 -> 61, of which waited for: 28 -> 30; matrix products, arithmetic and copies ran while one was open for 22% -> 26% of each run, Pallas kernels for 2% -> 2%
where the time goes in v3:
time: 945 us; the launch traced here: 936 us
  waiting for transfers between devices  506 us (54%)
  matrix products  104 us (11%)
  starting transfers between devices  90.4 us (10%)
  local copies, waits for them, and re-layouts  85.7 us (9%)
  other arithmetic  82.8 us (9%)
  blocking collectives  34 us (4%)
  Pallas kernels  17.8 us (2%)
  between operations  15.9 us (2%)
    ppermute x42, waiting for transfers between devices, swap(): return lax.ppermute(value, axis, [(i, i ^ bit) for i in range(size)])  297 us
    all_to_all x10, waiting for transfers between devices, spread(): return lax.all_to_all(blocks, axis, split_axis=0, concat_axis=0, tiled=True)  109 us
    dot_general x28, matrix products, matmul(): lax.dot_general(lhs, rhs, (dims, ((), ())), preferred_element_type=jnp.fl...  104 us
    ppermute x42, starting transfers between devices, swap(): return lax.ppermute(value, axis, [(i, i ^ bit) for i in range(size)])  47.5 us
    all_to_all x10, starting transfers between devices, spread(): return lax.all_to_all(blocks, axis, split_axis=0, concat_axis=0, tiled=True)  42.4 us
    reduce_scatter x1, waiting for transfers between devices, local_fast(): lax.psum_scatter(branch_low, 'fsdp', scatter_dimension=1, tiled=True)  40.7 us
    all_gather x1, waiting for transfers between devices, local_fast(): lax.all_gather(grad_branch_mlp.astype(low), 'fsdp', axis=1, tiled=True)  32.3 us
    unnamed x200, local copies, waits for them, and re-layouts  22.4 us
  transfers between devices with their start and end apart: 61, of which 30 were waited for; matrix products, arithmetic and copies ran while one was open for 26% of the time, Pallas kernels for 2%

profile of v3, /device:TPU:0, one launch (start us, length us, event | category | flops | bytes accessed | tf_op | source)
XLA Modules:
  0.0 936.4 jit_solution(10555866455481682971)
XLA Ops:
  16.7 6.5 all-to-all-start
  28.1 36.9 %all-to-all-done = bf16[8,256,256]{1,2,0:T(8,128)(2,1)S(1)} async-done(((bf16[8,256,256]{1,2,0:T(8,128)(2,1)}), bf16[8,256,256]{1,2,0:T(8,128)(2,1)S(1)}, u32[]{:S(2)}, u32[]{:S(2)}) %all-to-all-start) | async-done | bytes 1048608 | tf_op jit(solution)/shard_map/all_to_all | solution.py:564
  76.4 4.4 all-to-all-start.1
  80.8 15.6 %collective-permute-done.2 = bf16[2064,256]{1,0:T(8,128)(2,1)} collective-permute-done((bf16[2064,256]{1,0:T(8,128)(2,1)}, bf16[2064,256]{1,0:T(8,128)(2,1)}, u32[]{:S(2)}, u32[]{:S(2)}) %collective-permute-start.2) | collective-permute-done | bytes 1056800 | tf_op jit(solution)/shard_map/ppermute | solution.py:560
  105.6 6.3 collective-permute-done.3
  118.2 4.4 broadcast_select_fusion.5
  122.6 3.3 slice.700
  132.8 13.9 %all-to-all-done.1 = bf16[8,2,256,256]{3,2,1,0:T(8,128)(2,1)} async-done(((bf16[8,2,256,256]{3,2,1,0:T(8,128)(2,1)}), bf16[8,2,256,256]{3,2,1,0:T(8,128)(2,1)}, u32[]{:S(2)}, u32[]{:S(2)}) %all-to-all-start.1) | async-done | bytes 2097184 | tf_op jit(solution)/shard_map/all_to_all | solution.py:564
  146.8 4.4 all-to-all-start.2
  151.3 3.3 fusion.34
  161.7 19.2 %psum.14 = f32[2,3,256]{2,1,0:T(4,128)S(1)} all-reduce(f32[2,3,256]{2,1,0:T(4,128)S(1)} %pad_maximum_fusion.14), channel_id=1, replica_groups=mesh['fsdp'=8,'tp'=4] {'fsdp'}, use_global_device_ids=true, to_apply=%region_2.3 | all-reduce | flops 1536 | bytes 12288 | tf_op jit(solution)/shard_map/psum | solution.py:742
  185.3 3.0 fusion.102
  194.8 78.3 %collective-permute-done.10 = f32[3,256]{1,0:T(4,128)S(1)} collective-permute-done((f32[3,256]{1,0:T(4,128)}, f32[3,256]{1,0:T(4,128)S(1)}, u32[]{:S(2)}, u32[]{:S(2)}) %collective-permute-start.10) | collective-permute-done | bytes 3104 | tf_op jit(solution)/shard_map/ppermute | solution.py:560
  273.7 3.4 collective-permute-done.9
  291.1 3.0 pad_maximum_fusion.kv_ref
  294.1 6.4 attend.1
  301.7 5.6 collective-permute-done.12
  307.9 21.9 %collective-permute-done.14 = bf16[2048,256]{1,0:T(8,128)(2,1)} collective-permute-done((bf16[2048,256]{1,0:T(8,128)(2,1)}, bf16[2048,256]{1,0:T(8,128)(2,1)}, u32[]{:S(2)}, u32[]{:S(2)}) %collective-permute-start.14) | collective-permute-done | bytes 1048608 | tf_op jit(solution)/shard_map/ppermute | solution.py:560
  329.8 19.9 %collective-permute-done.16 = bf16[256,2048]{1,0:T(8,128)(2,1)} collective-permute-done((bf16[256,2048]{1,0:T(8,128)(2,1)}, bf16[256,2048]{1,0:T(8,128)(2,1)}, u32[]{:S(2)}, u32[]{:S(2)}) %collective-permute-start.16) | collective-permute-done | bytes 1048608 | tf_op jit(solution)/shard_map/ppermute | solution.py:560
  350.5 3.6 all-to-all-start.3
  355.0 11.6 %all-to-all-done.3 = bf16[8,3,32,256]{3,2,1,0:T(8,128)(2,1)S(1)} async-done(((bf16[8,3,32,256]{3,2,1,0:T(8,128)(2,1)}), bf16[8,3,32,256]{3,2,1,0:T(8,128)(2,1)S(1)}, u32[]{:S(2)}, u32[]{:S(2)}) %all-to-all-start.3) | async-done | bytes 393248 | tf_op jit(solution)/shard_map/all_to_all | solution.py:564
  367.0 4.9 multiply_reduce_fusion.5
  378.9 22.9 %collective-permute-done.17 = bf16[2048,256]{1,0:T(8,128)(2,1)} collective-permute-done((bf16[2048,256]{1,0:T(8,128)(2,1)}, bf16[2048,256]{1,0:T(8,128)(2,1)}, u32[]{:S(2)}, u32[]{:S(2)}) %collective-permute-start.17) | collective-permute-done | bytes 1048608 | tf_op jit(solution)/shard_map/ppermute | solution.py:560
  401.8 9.1 all-gather.13.cloned.1.call-done
  410.9 6.6 fusion.24
  417.4 8.8 multiply_convert_fusion.2
  427.4 7.5 convolution_convert_fusion
  434.9 16.1 %all-gather.15.cloned.1.call-done = bf16[3,256,2048]{2,1,0:T(8,128)(2,1)} async-done(((bf16[3,256,256]{2,1,0:T(8,128)(2,1)}), bf16[3,256,2048]{2,1,0:T(8,128)(2,1)}) %all-gather.15.cloned.1.call-update) | async-done | bytes 3145744 | tf_op jit(solution)/shard_map/all_gather | solution.py:799
  451.0 40.7 %reduce-scatter.4.cloned.1.call-done = bf16[3,32,2048]{2,1,0:T(8,128)(2,1)} async-done(((bf16[3,256,2048]{2,1,0:T(8,128)(2,1)}), bf16[3,32,2048]{2,1,0:T(8,128)(2,1)}) %reduce-scatter.4.cloned.1.call-update) | async-done | bytes 393232 | tf_op jit(solution)/shard_map/reduce_scatter | solution.py:803
  500.9 32.3 %all-gather.17.cloned.1.call-done = bf16[3,256,2048]{2,1,0:T(8,128)(2,1)} async-done(((bf16[3,32,2048]{2,1,0:T(8,128)(2,1)}), bf16[3,256,2048]{2,1,0:T(8,128)(2,1)}) %all-gather.17.cloned.1.call-update) | async-done | bytes 3145744 | tf_op jit(solution)/shard_map/all_gather | solution.py:817
  533.2 8.6 multiply_convert_fusion.1
  541.8 6.3 fusion.22
  548.2 6.7 add_convert_fusion.1
  558.0 3.2 convolution_convert_fusion.3
  563.3 5.3 convolution_convert_fusion.2
  571.0 3.2 convolution_convert_fusion.1
  574.8 35.3 %collective-permute-done.26 = bf16[512,2048]{1,0:T(8,128)(2,1)} collective-permute-done((bf16[512,2048]{1,0:T(8,128)(2,1)}, bf16[512,2048]{1,0:T(8,128)(2,1)}, u32[]{:S(2)}, u32[]{:S(2)}) %collective-permute-start.26) | collective-permute-done | bytes 2097184 | tf_op jit(solution)/shard_map/ppermute | solution.py:560
  610.1 3.5 convert_add_fusion.2
  620.3 6.1 convolution_convert_fusion.4
  631.5 3.6 all-to-all-start.4
  635.2 4.9 convert_add_fusion.1
  642.7 12.3 %collective-permute-done.37 = bf16[2048,512]{1,0:T(8,128)(2,1)} collective-permute-done((bf16[2048,512]{1,0:T(8,128)(2,1)}, bf16[2048,512]{1,0:T(8,128)(2,1)}, u32[]{:S(2)}, u32[]{:S(2)}) %collective-permute-start.37) | collective-permute-done | bytes 2097184 | tf_op jit(solution)/shard_map/ppermute | solution.py:560
  655.0 3.5 convert_add_fusion
  664.0 11.3 %attend_back.1 = (f32[3,256,256]{2,1,0:T(8,128)}, bf16[4,3,256,512]{3,2,1,0:T(8,128)(2,1)}) custom-call(bf16[3,256,256]{2,1,0:T(8,128)(2,1)} %pad_maximum_fusion.13.q_ref, bf16[4,3,256,512]{3,2,1,0:T(8,128)(2,1)} %pad_maximum_fusion.kv_ref, bf16[3,256,256]{2,1,0:T(8,128)(2,1)} %bitcast.351, f32[3,256,256]{2,1,0:T(8,128)} %get-tuple-element.51.out_ref, ...), custom_call_target="tpu_custom_call" | custom-call | tf_op jit(solution)/shard_map/attend_back/pallas_call | solution.py:545
  675.3 3.1 slice_bitcast_fusion.16
  684.6 4.2 all-to-all-start.5
  688.8 3.1 fusion.19
  691.9 8.2 collective-permute-done.25
  700.1 19.3 %collective-permute-done.24 = bf16[3,256,512]{2,1,0:T(8,128)(2,1)} collective-permute-done((bf16[3,256,512]{2,1,0:T(8,128)(2,1)}, bf16[3,256,512]{2,1,0:T(8,128)(2,1)}, u32[]{:S(2)}, u32[]{:S(2)}) %collective-permute-start.24) | collective-permute-done | bytes 786464 | tf_op jit(solution)/shard_map/ppermute | solution.py:560
  725.8 14.8 %psum.15 = f32[2,3,256]{2,1,0:T(4,128)} all-reduce(f32[2,3,256]{2,1,0:T(4,128)} %pad_maximum_fusion.15), channel_id=1, replica_groups=mesh['fsdp'=8,'tp'=4] {'fsdp'}, use_global_device_ids=true, to_apply=%region_12.13 | all-reduce | flops 1536 | bytes 12288 | tf_op jit(solution)/shard_map/psum | solution.py:926
  753.4 3.0 add_convert_fusion
  756.3 3.7 all-to-all-start.6
  760.8 3.2 fusion.3
  765.5 3.0 maximum_select_fusion
  778.3 18.8 %all-to-all-done.6 = bf16[8,256,256]{2,1,0:T(8,128)(2,1)S(1)} async-done(((bf16[8,256,256]{2,1,0:T(8,128)(2,1)}), bf16[8,256,256]{2,1,0:T(8,128)(2,1)S(1)}, u32[]{:S(2)}, u32[]{:S(2)}) %all-to-all-start.6) | async-done | bytes 1048608 | tf_op jit(solution)/shard_map/all_to_all | solution.py:564
  797.1 4.3 all-to-all-start.7
  802.0 19.8 %collective-permute-done.33 = bf16[2064,256]{1,0:T(8,128)(2,1)} collective-permute-done((bf16[2064,256]{1,0:T(8,128)(2,1)}, bf16[2064,256]{1,0:T(8,128)(2,1)}, u32[]{:S(2)}, u32[]{:S(2)}) %collective-permute-start.33) | collective-permute-done | bytes 1056800 | tf_op jit(solution)/shard_map/ppermute | solution.py:560
  826.9 10.1 %all-to-all-done.7 = bf16[8,256,256]{2,1,0:T(8,128)(2,1)} async-done(((bf16[8,256,256]{2,1,0:T(8,128)(2,1)}), bf16[8,256,256]{2,1,0:T(8,128)(2,1)}, u32[]{:S(2)}, u32[]{:S(2)}) %all-to-all-start.7) | async-done | bytes 1048608 | tf_op jit(solution)/shard_map/all_to_all | solution.py:564
  839.3 4.2 all-to-all-start.8
  852.4 17.8 %all-to-all-done.8 = bf16[8,256,256]{1,2,0:T(8,128)(2,1)} async-done(((bf16[8,256,256]{1,2,0:T(8,128)(2,1)}), bf16[8,256,256]{1,2,0:T(8,128)(2,1)}, u32[]{:S(2)}, u32[]{:S(2)}) %all-to-all-start.8) | async-done | bytes 1048608 | tf_op jit(solution)/shard_map/all_to_all | solution.py:564
  870.1 3.5 all-to-all-start.9
  898.4 7.0 collective-permute-done.29
  908.9 7.9 collective-permute-done.41
  916.8 10.8 %collective-permute-done.40 = bf16[1040,256]{1,0:T(8,128)(2,1)S(1)} collective-permute-done((bf16[1040,256]{1,0:T(8,128)(2,1)S(1)}, bf16[1040,256]{1,0:T(8,128)(2,1)S(1)}, u32[]{:S(2)}, u32[]{:S(2)}) %collective-permute-start.40) | collective-permute-done | bytes 532512 | tf_op jit(solution)/shard_map/ppermute | solution.py:560
  (470 shorter events, 213.1 us)
Async XLA Ops:
  7.2 115.4 %all-gather.9.cloned.1.call-start = ((), (), s32[]{:S(2)}) async-start(), calls=%async_computation.14 | async-start | bytes 2433024 | tf_op jit(solution)/shard_map/all_gather | solution.py:690
  11.0 140.2 %all-gather.7.cloned.1.call-start = ((), (), s32[]{:S(2)}) async-start(), calls=%async_computation.13 | async-start | bytes 3538944 | tf_op jit(solution)/shard_map/all_gather | solution.py:672
  16.7 48.2 %all-to-all-start = ((bf16[8,256,256]{1,2,0:T(8,128)(2,1)}), bf16[8,256,256]{1,2,0:T(8,128)(2,1)S(1)}, u32[]{:S(2)}, u32[]{:S(2)}) async-start(bf16[8,256,256]{1,2,0:T(8,128)(2,1)} %maximum_bitcast_fusion.13), calls=%async_computation | async-start | bytes 2097152 | tf_op jit(solution)/shard_map/all_to_all | solution.py:564
  70.8 25.7 %collective-permute-start.2 = (bf16[2064,256]{1,0:T(8,128)(2,1)}, bf16[2064,256]{1,0:T(8,128)(2,1)}, u32[]{:S(2)}, u32[]{:S(2)}) collective-permute-start(bf16[2064,256]{1,0:T(8,128)(2,1)} %copy.231), channel_id=1, source_target_pairs={{0,2},{1,3},{2,0},{3,1},{4,6},{5,7},{6,4},{7,5},{8,10},{9,11},{10,... | collective-permute-start | bytes 3170312 | tf_op jit(solution)/shard_map/ppermute | solution.py:560
  72.2 27.5 %collective-permute-start = (bf16[2064,256]{1,0:T(8,128)(2,1)}, bf16[2064,256]{1,0:T(8,128)(2,1)}, u32[]{:S(2)}, u32[]{:S(2)}) collective-permute-start(bf16[2064,256]{1,0:T(8,128)(2,1)} %copy.231), channel_id=1, source_target_pairs={{0,1},{1,0},{2,3},{3,2},{4,5},{5,4},{6,7},{7,6},{8,9},{9,8},{10,11... | collective-permute-start | bytes 3170312 | tf_op jit(solution)/shard_map/ppermute | solution.py:560
  76.4 70.4 %all-to-all-start.1 = ((bf16[8,2,256,256]{3,2,1,0:T(8,128)(2,1)}), bf16[8,2,256,256]{3,2,1,0:T(8,128)(2,1)}, u32[]{:S(2)}, u32[]{:S(2)}) async-start(bf16[8,2,256,256]{3,2,1,0:T(8,128)(2,1)} %copy.250), calls=%async_computation.1 | async-start | bytes 4194304 | tf_op jit(solution)/shard_map/all_to_all | solution.py:564
  80.7 286.2 %all-gather.11.cloned.1.call-start = ((), (), s32[]{:S(2)}) async-start(), calls=%async_computation.15 | async-start | bytes 10485760 | tf_op jit(solution)/shard_map/all_gather | solution.py:698
  98.3 13.6 %collective-permute-start.3 = (bf16[1040,256]{1,0:T(8,128)(2,1)}, bf16[1040,256]{1,0:T(8,128)(2,1)}, u32[]{:S(2)}, u32[]{:S(2)}) collective-permute-start(bf16[1040,256]{1,0:T(8,128)(2,1)} %slice.638), channel_id=1, source_target_pairs={{0,1},{1,0},{2,3},{3,2},{4,5},{5,4},{6,7},{7,6},{8,9},{9,8},{10,11... | collective-permute-start | bytes 1597448 | tf_op jit(solution)/shard_map/ppermute | solution.py:560
  102.3 13.1 %collective-permute-start.1 = (bf16[1024,256]{0,1:T(8,128)(2,1)}, bf16[1024,256]{0,1:T(8,128)(2,1)}, u32[]{:S(2)}, u32[]{:S(2)}) collective-permute-start(bf16[1024,256]{0,1:T(8,128)(2,1)} %slice.637), channel_id=1, source_target_pairs={{0,2},{1,3},{2,0},{3,1},{4,6},{5,7},{6,4},{7,5},{8,10},{9,11},{10,... | collective-permute-start | bytes 1572872 | tf_op jit(solution)/shard_map/ppermute | solution.py:560
  129.8 26.9 %collective-permute-start.4 = (bf16[2,2064,256]{2,1,0:T(8,128)(2,1)}, bf16[2,2064,256]{2,1,0:T(8,128)(2,1)S(1)}, u32[]{:S(2)}, u32[]{:S(2)}) collective-permute-start(bf16[2,2064,256]{2,1,0:T(8,128)(2,1)} %copy.241), channel_id=1, source_target_pairs={{0,4},{4,0},{8,12},{12,8},{16,20},{20,16},{24,28},{28,24},{1,5},{5... | collective-permute-start | bytes 6340616 | tf_op jit(solution)/shard_map/ppermute | solution.py:560
  146.8 131.6 %all-to-all-start.2 = ((bf16[8,256,256]{2,1,0:T(8,128)(2,1)}), bf16[8,256,256]{2,1,0:T(8,128)(2,1)}, u32[]{:S(2)}, u32[]{:S(2)}) async-start(bf16[8,256,256]{2,1,0:T(8,128)(2,1)} %bitcast.354), calls=%async_computation.2 | async-start | bytes 2097152 | tf_op jit(solution)/shard_map/all_to_all | solution.py:564
  183.9 93.7 %copy-start.35 = (bf16[3,256,128]{2,1,0:T(8,128)(2,1)S(1)}, bf16[3,256,128]{2,1,0:T(8,128)(2,1)}, u32[]{:S(2)}) copy-start(bf16[3,256,128]{2,1,0:T(8,128)(2,1)} %get-tuple-element.255) | copy-start | bytes 589828
  188.4 96.7 %collective-permute-start.11 = (bf16[2048,256]{1,0:T(8,128)(2,1)}, bf16[2048,256]{1,0:T(8,128)(2,1)}, u32[]{:S(2)}, u32[]{:S(2)}) collective-permute-start(bf16[2048,256]{1,0:T(8,128)(2,1)} %bitcast.36), channel_id=1, source_target_pairs={{0,1},{1,0},{2,3},{3,2},{4,5},{5,4},{6,7},{7,6},{8,9},{9,8},{10,11... | collective-permute-start | bytes 3145736 | tf_op jit(solution)/shard_map/ppermute | solution.py:560
  189.8 91.7 %collective-permute-start.7 = (bf16[3,256,512]{2,1,0:T(8,128)(2,1)S(1)}, bf16[3,256,512]{2,1,0:T(8,128)(2,1)S(1)}, u32[]{:S(2)}, u32[]{:S(2)}) collective-permute-start(bf16[3,256,512]{2,1,0:T(8,128)(2,1)S(1)} %concatenate.171), channel_id=1, source_target_pairs={{0,3},{1,2},{2,1},{3,0},{4,7},{5,6},{6,5},{7,4},{8,11},{9,10},{10,... | collective-permute-start | bytes 2359304 | tf_op jit(solution)/shard_map/ppermute | solution.py:560
  191.3 91.5 %collective-permute-start.6 = (bf16[3,256,512]{2,1,0:T(8,128)(2,1)S(1)}, bf16[3,256,512]{2,1,0:T(8,128)(2,1)}, u32[]{:S(2)}, u32[]{:S(2)}) collective-permute-start(bf16[3,256,512]{2,1,0:T(8,128)(2,1)S(1)} %concatenate.171), channel_id=1, source_target_pairs={{0,2},{1,3},{2,0},{3,1},{4,6},{5,7},{6,4},{7,5},{8,10},{9,11},{10,... | collective-permute-start | bytes 2359304 | tf_op jit(solution)/shard_map/ppermute | solution.py:560
  191.9 92.4 %collective-permute-start.5 = (bf16[3,256,512]{2,1,0:T(8,128)(2,1)S(1)}, bf16[3,256,512]{2,1,0:T(8,128)(2,1)}, u32[]{:S(2)}, u32[]{:S(2)}) collective-permute-start(bf16[3,256,512]{2,1,0:T(8,128)(2,1)S(1)} %concatenate.171), channel_id=1, source_target_pairs={{0,1},{1,0},{2,3},{3,2},{4,5},{5,4},{6,7},{7,6},{8,9},{9,8},{10,11... | collective-permute-start | bytes 2359304 | tf_op jit(solution)/shard_map/ppermute | solution.py:560
  193.3 79.8 %collective-permute-start.10 = (f32[3,256]{1,0:T(4,128)}, f32[3,256]{1,0:T(4,128)S(1)}, u32[]{:S(2)}, u32[]{:S(2)}) collective-permute-start(f32[3,256]{1,0:T(4,128)} %get-tuple-element.261), channel_id=1, source_target_pairs={{0,3},{1,2},{2,1},{3,0},{4,7},{5,6},{6,5},{7,4},{8,11},{9,10},{10,... | collective-permute-start | bytes 9224 | tf_op jit(solution)/shard_map/ppermute | solution.py:560
  273.1 3.9 collective-permute-start.9
  277.1 3.9 collective-permute-start.8
  281.0 26.3 %collective-permute-start.12 = (bf16[2048,256]{1,0:T(8,128)(2,1)}, bf16[2048,256]{1,0:T(8,128)(2,1)}, u32[]{:S(2)}, u32[]{:S(2)}) collective-permute-start(bf16[2048,256]{1,0:T(8,128)(2,1)} %bitcast.36), channel_id=1, source_target_pairs={{0,2},{1,3},{2,0},{3,1},{4,6},{5,7},{6,4},{7,5},{8,10},{9,11},{10,... | collective-permute-start | bytes 3145736 | tf_op jit(solution)/shard_map/ppermute | solution.py:560
  281.5 26.3 %collective-permute-start.13 = (bf16[2048,256]{1,0:T(8,128)(2,1)}, bf16[2048,256]{1,0:T(8,128)(2,1)}, u32[]{:S(2)}, u32[]{:S(2)}) collective-permute-start(bf16[2048,256]{1,0:T(8,128)(2,1)} %bitcast.37), channel_id=1, source_target_pairs={{0,1},{1,0},{2,3},{3,2},{4,5},{5,4},{6,7},{7,6},{8,9},{9,8},{10,11... | collective-permute-start | bytes 3145736 | tf_op jit(solution)/shard_map/ppermute | solution.py:560
  282.8 47.0 %collective-permute-start.14 = (bf16[2048,256]{1,0:T(8,128)(2,1)}, bf16[2048,256]{1,0:T(8,128)(2,1)}, u32[]{:S(2)}, u32[]{:S(2)}) collective-permute-start(bf16[2048,256]{1,0:T(8,128)(2,1)} %bitcast.37), channel_id=1, source_target_pairs={{0,2},{1,3},{2,0},{3,1},{4,6},{5,7},{6,4},{7,5},{8,10},{9,11},{10,... | collective-permute-start | bytes 3145736 | tf_op jit(solution)/shard_map/ppermute | solution.py:560
  284.2 45.6 %collective-permute-start.15 = (bf16[256,2048]{1,0:T(8,128)(2,1)}, bf16[256,2048]{1,0:T(8,128)(2,1)}, u32[]{:S(2)}, u32[]{:S(2)}) collective-permute-start(bf16[256,2048]{1,0:T(8,128)(2,1)} %bitcast.159), channel_id=1, source_target_pairs={{0,1},{1,0},{2,3},{3,2},{4,5},{5,4},{6,7},{7,6},{8,9},{9,8},{10,11... | collective-permute-start | bytes 3145736 | tf_op jit(solution)/shard_map/ppermute | solution.py:560
  285.0 64.7 %collective-permute-start.16 = (bf16[256,2048]{1,0:T(8,128)(2,1)}, bf16[256,2048]{1,0:T(8,128)(2,1)}, u32[]{:S(2)}, u32[]{:S(2)}) collective-permute-start(bf16[256,2048]{1,0:T(8,128)(2,1)} %bitcast.159), channel_id=1, source_target_pairs={{0,2},{1,3},{2,0},{3,1},{4,6},{5,7},{6,4},{7,5},{8,10},{9,11},{10,... | collective-permute-start | bytes 3145736 | tf_op jit(solution)/shard_map/ppermute | solution.py:560
  301.7 70.2 %copy-start.13 = (bf16[3,256,256]{2,1,0:T(8,128)(2,1)}, bf16[3,256,256]{2,1,0:T(8,128)(2,1)S(1)}, u32[]{:S(2)}) copy-start(bf16[3,256,256]{2,1,0:T(8,128)(2,1)S(1)} %convert_element_type.293) | copy-start | bytes 1179652
  350.5 16.1 %all-to-all-start.3 = ((bf16[8,3,32,256]{3,2,1,0:T(8,128)(2,1)}), bf16[8,3,32,256]{3,2,1,0:T(8,128)(2,1)S(1)}, u32[]{:S(2)}, u32[]{:S(2)}) async-start(bf16[8,3,32,256]{3,2,1,0:T(8,128)(2,1)} %bitcast.319), calls=%async_computation.3 | async-start | bytes 786432 | tf_op jit(solution)/shard_map/all_to_all | solution.py:564
  354.1 56.8 %all-gather.13.cloned.1.call-start = ((), (), s32[]{:S(2)}) async-start(), calls=%async_computation.16 | async-start | bytes 3538944 | tf_op jit(solution)/shard_map/all_gather | solution.py:793
  372.5 123.4 %copy-start.53 = (f32[3,32]{1,0:T(4,128)}, f32[3,32]{1,0:T(4,128)S(1)}, u32[]{:S(2)}) copy-start(f32[3,32]{1,0:T(4,128)S(1)} %get-tuple-element.264) | copy-start | bytes 1156
  374.5 76.4 %all-gather.15.cloned.1.call-start = ((), (), s32[]{:S(2)}) async-start(), calls=%async_computation.17 | async-start | bytes 3538944 | tf_op jit(solution)/shard_map/all_gather | solution.py:799
  375.1 116.6 %reduce-scatter.4.cloned.1.call-start = ((), (), s32[]{:S(2)}) async-start(), calls=%async_computation.18 | async-start | bytes 3538944 | tf_op jit(solution)/shard_map/reduce_scatter | solution.py:803
  375.4 26.4 %collective-permute-start.17 = (bf16[2048,256]{1,0:T(8,128)(2,1)}, bf16[2048,256]{1,0:T(8,128)(2,1)}, u32[]{:S(2)}, u32[]{:S(2)}) collective-permute-start(bf16[2048,256]{1,0:T(8,128)(2,1)} %collective-permute-done.11), channel_id=1, source_target_pairs={{0,2},{1,3},{2,0},{3,1},{4,6},{5,7},{6,4},{7,5},{8,10},{9,11},{10,... | collective-permute-start | bytes 3145736 | tf_op jit(solution)/shard_map/ppermute | solution.py:560
  376.0 41.4 %collective-permute-start.18 = (bf16[2048,256]{1,0:T(8,128)(2,1)}, bf16[2048,256]{1,0:T(8,128)(2,1)}, u32[]{:S(2)}, u32[]{:S(2)}) collective-permute-start(bf16[2048,256]{1,0:T(8,128)(2,1)} %collective-permute-done.14), channel_id=1, source_target_pairs={{0,1},{1,0},{2,3},{3,2},{4,5},{5,4},{6,7},{7,6},{8,9},{9,8},{10,11... | collective-permute-start | bytes 3145736 | tf_op jit(solution)/shard_map/ppermute | solution.py:560
  377.5 48.8 %collective-permute-start.19 = (bf16[256,2048]{1,0:T(8,128)(2,1)}, bf16[256,2048]{1,0:T(8,128)(2,1)}, u32[]{:S(2)}, u32[]{:S(2)}) collective-permute-start(bf16[256,2048]{1,0:T(8,128)(2,1)} %collective-permute-done.15), channel_id=1, source_target_pairs={{0,2},{1,3},{2,0},{3,1},{4,6},{5,7},{6,4},{7,5},{8,10},{9,11},{10,... | collective-permute-start | bytes 3145736 | tf_op jit(solution)/shard_map/ppermute | solution.py:560
  451.0 82.2 %all-gather.17.cloned.1.call-start = ((), (), s32[]{:S(2)}) async-start(), calls=%async_computation.19 | async-start | bytes 3538944 | tf_op jit(solution)/shard_map/all_gather | solution.py:817
  495.8 122.4 %reduce-scatter.6.cloned.1.call-start = ((), (), s32[]{:S(2)}) async-start(), calls=%async_computation.20 | async-start | bytes 3538944 | tf_op jit(solution)/shard_map/reduce_scatter | solution.py:829
  497.3 57.6 %collective-permute-start.20 = (bf16[3,32,2048]{2,1,0:T(8,128)(2,1)S(1)}, bf16[3,32,2048]{2,1,0:T(8,128)(2,1)S(1)}, u32[]{:S(2)}, u32[]{:S(2)}) collective-permute-start(bf16[3,32,2048]{2,1,0:T(8,128)(2,1)S(1)} %fusion.40), channel_id=1, source_target_pairs={{0,1},{1,0},{2,3},{3,2},{4,5},{5,4},{6,7},{7,6},{8,9},{9,8},{10,11... | collective-permute-start | bytes 1179656 | tf_op jit(solution)/shard_map/ppermute | solution.py:560
  498.7 56.2 %collective-permute-start.21 = (bf16[3,32,2048]{2,1,0:T(8,128)(2,1)S(1)}, bf16[3,32,2048]{2,1,0:T(8,128)(2,1)S(1)}, u32[]{:S(2)}, u32[]{:S(2)}) collective-permute-start(bf16[3,32,2048]{2,1,0:T(8,128)(2,1)S(1)} %fusion.40), channel_id=1, source_target_pairs={{0,2},{1,3},{2,0},{3,1},{4,6},{5,7},{6,4},{7,5},{8,10},{9,11},{10,... | collective-permute-start | bytes 1179656 | tf_op jit(solution)/shard_map/ppermute | solution.py:560
  500.2 54.7 %collective-permute-start.22 = (bf16[3,32,2048]{2,1,0:T(8,128)(2,1)S(1)}, bf16[3,32,2048]{2,1,0:T(8,128)(2,1)}, u32[]{:S(2)}, u32[]{:S(2)}) collective-permute-start(bf16[3,32,2048]{2,1,0:T(8,128)(2,1)S(1)} %fusion.40), channel_id=1, source_target_pairs={{0,3},{1,2},{2,1},{3,0},{4,7},{5,6},{6,5},{7,4},{8,11},{9,10},{10,... | collective-permute-start | bytes 1179656 | tf_op jit(solution)/shard_map/ppermute | solution.py:560
  561.2 48.8 %collective-permute-start.26 = (bf16[512,2048]{1,0:T(8,128)(2,1)}, bf16[512,2048]{1,0:T(8,128)(2,1)}, u32[]{:S(2)}, u32[]{:S(2)}) collective-permute-start(bf16[512,2048]{1,0:T(8,128)(2,1)} %convolution_convert_fusion.3), channel_id=1, source_target_pairs={{0,1},{1,0},{2,3},{3,2},{4,5},{5,4},{6,7},{7,6},{8,9},{9,8},{10,11... | collective-permute-start | bytes 6291464 | tf_op jit(solution)/shard_map/ppermute | solution.py:560
  568.7 66.5 %collective-permute-start.35 = (bf16[2048,512]{1,0:T(8,128)(2,1)}, bf16[2048,512]{1,0:T(8,128)(2,1)}, u32[]{:S(2)}, u32[]{:S(2)}) collective-permute-start(bf16[2048,512]{1,0:T(8,128)(2,1)} %convolution_convert_fusion.2), channel_id=1, source_target_pairs={{0,2},{1,3},{2,0},{3,1},{4,6},{5,7},{6,4},{7,5},{8,10},{9,11},{10,... | collective-permute-start | bytes 6291464 | tf_op jit(solution)/shard_map/ppermute | solution.py:560
  574.2 80.8 %collective-permute-start.37 = (bf16[2048,512]{1,0:T(8,128)(2,1)}, bf16[2048,512]{1,0:T(8,128)(2,1)}, u32[]{:S(2)}, u32[]{:S(2)}) collective-permute-start(bf16[2048,512]{1,0:T(8,128)(2,1)} %convolution_convert_fusion.1), channel_id=1, source_target_pairs={{0,1},{1,0},{2,3},{3,2},{4,5},{5,4},{6,7},{7,6},{8,9},{9,8},{10,11... | collective-permute-start | bytes 6291464 | tf_op jit(solution)/shard_map/ppermute | solution.py:560
  616.7 64.7 %collective-permute-start.27 = (bf16[256,2048]{1,0:T(8,128)(2,1)}, bf16[256,2048]{1,0:T(8,128)(2,1)}, u32[]{:S(2)}, u32[]{:S(2)}) collective-permute-start(bf16[256,2048]{1,0:T(8,128)(2,1)} %split.47), channel_id=1, source_target_pairs={{0,2},{1,3},{2,0},{3,1},{4,6},{5,7},{6,4},{7,5},{8,10},{9,11},{10,... | collective-permute-start | bytes 3145736 | tf_op jit(solution)/shard_map/ppermute | solution.py:560
  631.5 31.7 %all-to-all-start.4 = ((bf16[8,3,32,256]{3,2,1,0:T(8,128)(2,1)}), bf16[8,3,32,256]{3,2,1,0:T(8,128)(2,1)S(1)}, u32[]{:S(2)}, u32[]{:S(2)}) async-start(bf16[8,3,32,256]{3,2,1,0:T(8,128)(2,1)} %constant_dynamic-update-slice_fusion.16), calls=%async_computation.6 | async-start | bytes 786432 | tf_op jit(solution)/shard_map/all_to_all | solution.py:564
  641.3 47.6 %collective-permute-start.36 = (bf16[2048,256]{1,0:T(8,128)(2,1)}, bf16[2048,256]{1,0:T(8,128)(2,1)}, u32[]{:S(2)}, u32[]{:S(2)}) collective-permute-start(bf16[2048,256]{1,0:T(8,128)(2,1)} %split.46), channel_id=1, source_target_pairs={{0,1},{1,0},{2,3},{3,2},{4,5},{5,4},{6,7},{7,6},{8,9},{9,8},{10,11... | collective-permute-start | bytes 3145736 | tf_op jit(solution)/shard_map/ppermute | solution.py:560
  661.7 114.1 %collective-permute-start.38 = (bf16[2048,256]{1,0:T(8,128)(2,1)}, bf16[2048,256]{1,0:T(8,128)(2,1)}, u32[]{:S(2)}, u32[]{:S(2)}) collective-permute-start(bf16[2048,256]{1,0:T(8,128)(2,1)} %split.45), channel_id=1, source_target_pairs={{0,2},{1,3},{2,0},{3,1},{4,6},{5,7},{6,4},{7,5},{8,10},{9,11},{10,... | collective-permute-start | bytes 3145736 | tf_op jit(solution)/shard_map/ppermute | solution.py:560
  678.5 21.6 %collective-permute-start.25 = (bf16[3,256,512]{2,1,0:T(8,128)(2,1)}, bf16[3,256,512]{2,1,0:T(8,128)(2,1)}, u32[]{:S(2)}, u32[]{:S(2)}) collective-permute-start(bf16[3,256,512]{2,1,0:T(8,128)(2,1)} %get-tuple-element.160), channel_id=1, source_target_pairs={{0,3},{1,2},{2,1},{3,0},{4,7},{5,6},{6,5},{7,4},{8,11},{9,10},{10,... | collective-permute-start | bytes 2359304 | tf_op jit(solution)/shard_map/ppermute | solution.py:560
  679.9 39.5 %collective-permute-start.24 = (bf16[3,256,512]{2,1,0:T(8,128)(2,1)}, bf16[3,256,512]{2,1,0:T(8,128)(2,1)}, u32[]{:S(2)}, u32[]{:S(2)}) collective-permute-start(bf16[3,256,512]{2,1,0:T(8,128)(2,1)} %get-tuple-element.161), channel_id=1, source_target_pairs={{0,2},{1,3},{2,0},{3,1},{4,6},{5,7},{6,4},{7,5},{8,10},{9,11},{10,... | collective-permute-start | bytes 2359304 | tf_op jit(solution)/shard_map/ppermute | solution.py:560
  681.4 38.0 %collective-permute-start.23 = (bf16[3,256,512]{2,1,0:T(8,128)(2,1)S(1)}, bf16[3,256,512]{2,1,0:T(8,128)(2,1)}, u32[]{:S(2)}, u32[]{:S(2)}) collective-permute-start(bf16[3,256,512]{2,1,0:T(8,128)(2,1)S(1)} %get-tuple-element.159), channel_id=1, source_target_pairs={{0,1},{1,0},{2,3},{3,2},{4,5},{5,4},{6,7},{7,6},{8,9},{9,8},{10,11... | collective-permute-start | bytes 2359304 | tf_op jit(solution)/shard_map/ppermute | solution.py:560
  684.6 71.8 %all-to-all-start.5 = ((bf16[8,256,256]{2,1,0:T(8,128)(2,1)}), bf16[8,256,256]{2,1,0:T(8,128)(2,1)}, u32[]{:S(2)}, u32[]{:S(2)}) async-start(bf16[8,256,256]{2,1,0:T(8,128)(2,1)} %bitcast.329), calls=%async_computation.7 | async-start | bytes 2097152 | tf_op jit(solution)/shard_map/all_to_all | solution.py:564
  749.5 16.1 %collective-permute-start.31 = (bf16[2,2064,256]{2,1,0:T(8,128)(2,1)}, bf16[2,2064,256]{2,1,0:T(8,128)(2,1)}, u32[]{:S(2)}, u32[]{:S(2)}) collective-permute-start(bf16[2,2064,256]{2,1,0:T(8,128)(2,1)} %pad_maximum_fusion.3), channel_id=1, source_target_pairs={{0,4},{4,0},{8,12},{12,8},{16,20},{20,16},{24,28},{28,24},{1,5},{5... | collective-permute-start | bytes 6340616 | tf_op jit(solution)/shard_map/ppermute | solution.py:560
  756.3 40.8 %all-to-all-start.6 = ((bf16[8,256,256]{2,1,0:T(8,128)(2,1)}), bf16[8,256,256]{2,1,0:T(8,128)(2,1)S(1)}, u32[]{:S(2)}, u32[]{:S(2)}) async-start(bf16[8,256,256]{2,1,0:T(8,128)(2,1)} %bitcast.334), calls=%async_computation.9 | async-start | bytes 2097152 | tf_op jit(solution)/shard_map/all_to_all | solution.py:564
  760.0 89.8 %reduce-scatter.8.cloned.1.call-start = ((), (), s32[]{:S(2)}) async-start(), calls=%async_computation.21 | async-start | bytes 3538944 | tf_op jit(solution)/shard_map/reduce_scatter | solution.py:956
  772.3 29.8 %collective-permute-start.34 = (bf16[2064,256]{1,0:T(8,128)(2,1)}, bf16[2064,256]{1,0:T(8,128)(2,1)}, u32[]{:S(2)}, u32[]{:S(2)}) collective-permute-start(bf16[2064,256]{1,0:T(8,128)(2,1)} %get-tuple-element.156), channel_id=1, source_target_pairs={{0,3},{1,2},{2,1},{3,0},{4,7},{5,6},{6,5},{7,4},{8,11},{9,10},{10,... | collective-permute-start | bytes 3170312 | tf_op jit(solution)/shard_map/ppermute | solution.py:560
  774.6 47.2 %collective-permute-start.33 = (bf16[2064,256]{1,0:T(8,128)(2,1)}, bf16[2064,256]{1,0:T(8,128)(2,1)}, u32[]{:S(2)}, u32[]{:S(2)}) collective-permute-start(bf16[2064,256]{1,0:T(8,128)(2,1)} %get-tuple-element.157), channel_id=1, source_target_pairs={{0,2},{1,3},{2,0},{3,1},{4,6},{5,7},{6,4},{7,5},{8,10},{9,11},{10,... | collective-permute-start | bytes 3170312 | tf_op jit(solution)/shard_map/ppermute | solution.py:560
  775.2 46.7 %collective-permute-start.32 = (bf16[2064,256]{1,0:T(8,128)(2,1)}, bf16[2064,256]{1,0:T(8,128)(2,1)}, u32[]{:S(2)}, u32[]{:S(2)}) collective-permute-start(bf16[2064,256]{1,0:T(8,128)(2,1)} %get-tuple-element.155), channel_id=1, source_target_pairs={{0,1},{1,0},{2,3},{3,2},{4,5},{5,4},{6,7},{7,6},{8,9},{9,8},{10,11... | collective-permute-start | bytes 3170312 | tf_op jit(solution)/shard_map/ppermute | solution.py:560
  797.1 39.9 %all-to-all-start.7 = ((bf16[8,256,256]{2,1,0:T(8,128)(2,1)}), bf16[8,256,256]{2,1,0:T(8,128)(2,1)}, u32[]{:S(2)}, u32[]{:S(2)}) async-start(bf16[8,256,256]{2,1,0:T(8,128)(2,1)} %bitcast.335), calls=%async_computation.10 | async-start | bytes 2097152 | tf_op jit(solution)/shard_map/all_to_all | solution.py:564
  839.3 30.8 %all-to-all-start.8 = ((bf16[8,256,256]{1,2,0:T(8,128)(2,1)}), bf16[8,256,256]{1,2,0:T(8,128)(2,1)}, u32[]{:S(2)}, u32[]{:S(2)}) async-start(bf16[8,256,256]{1,2,0:T(8,128)(2,1)} %copy.270), calls=%async_computation.11 | async-start | bytes 2097152 | tf_op jit(solution)/shard_map/all_to_all | solution.py:564
  870.1 17.3 %all-to-all-start.9 = ((bf16[8,112,256]{2,1,0:T(8,128)(2,1)}), bf16[8,112,256]{2,1,0:T(8,128)(2,1)S(1)}, u32[]{:S(2)}, u32[]{:S(2)}) async-start(bf16[8,112,256]{2,1,0:T(8,128)(2,1)} %maximum_bitcast_fusion.14), calls=%async_computation.12 | async-start | bytes 917504 | tf_op jit(solution)/shard_map/all_to_all | solution.py:564
  884.0 13.4 %collective-permute-start.28 = (bf16[3,32,2048]{2,1,0:T(8,128)(2,1)S(1)}, bf16[3,32,2048]{2,1,0:T(8,128)(2,1)}, u32[]{:S(2)}, u32[]{:S(2)}) collective-permute-start(bf16[3,32,2048]{2,1,0:T(8,128)(2,1)S(1)} %get-tuple-element.158), channel_id=1, source_target_pairs={{0,3},{1,2},{2,1},{3,0},{4,7},{5,6},{6,5},{7,4},{8,11},{9,10},{10,... | collective-permute-start | bytes 1179656 | tf_op jit(solution)/shard_map/ppermute | solution.py:560
  886.3 19.2 %collective-permute-start.29 = (bf16[3,32,2048]{2,1,0:T(8,128)(2,1)S(1)}, bf16[3,32,2048]{2,1,0:T(8,128)(2,1)}, u32[]{:S(2)}, u32[]{:S(2)}) collective-permute-start(bf16[3,32,2048]{2,1,0:T(8,128)(2,1)S(1)} %get-tuple-element.158), channel_id=1, source_target_pairs={{0,2},{1,3},{2,0},{3,1},{4,6},{5,7},{6,4},{7,5},{8,10},{9,11},{10,... | collective-permute-start | bytes 1179656 | tf_op jit(solution)/shard_map/ppermute | solution.py:560
  886.9 18.6 %collective-permute-start.30 = (bf16[3,32,2048]{2,1,0:T(8,128)(2,1)S(1)}, bf16[3,32,2048]{2,1,0:T(8,128)(2,1)}, u32[]{:S(2)}, u32[]{:S(2)}) collective-permute-start(bf16[3,32,2048]{2,1,0:T(8,128)(2,1)S(1)} %get-tuple-element.158), channel_id=1, source_target_pairs={{0,1},{1,0},{2,3},{3,2},{4,5},{5,4},{6,7},{7,6},{8,9},{9,8},{10,11... | collective-permute-start | bytes 1179656 | tf_op jit(solution)/shard_map/ppermute | solution.py:560
  894.4 22.4 %collective-permute-start.41 = (bf16[1040,256]{1,0:T(8,128)(2,1)S(1)}, bf16[1040,256]{1,0:T(8,128)(2,1)S(1)}, u32[]{:S(2)}, u32[]{:S(2)}) collective-permute-start(bf16[1040,256]{1,0:T(8,128)(2,1)S(1)} %get-tuple-element.165), channel_id=1, source_target_pairs={{0,3},{1,2},{2,1},{3,0},{4,7},{5,6},{6,5},{7,4},{8,11},{9,10},{10,... | collective-permute-start | bytes 1597448 | tf_op jit(solution)/shard_map/ppermute | solution.py:560
  896.8 30.7 %collective-permute-start.40 = (bf16[1040,256]{1,0:T(8,128)(2,1)S(1)}, bf16[1040,256]{1,0:T(8,128)(2,1)S(1)}, u32[]{:S(2)}, u32[]{:S(2)}) collective-permute-start(bf16[1040,256]{1,0:T(8,128)(2,1)S(1)} %get-tuple-element.166), channel_id=1, source_target_pairs={{0,2},{1,3},{2,0},{3,1},{4,6},{5,7},{6,4},{7,5},{8,10},{9,11},{10,... | collective-permute-start | bytes 1597448 | tf_op jit(solution)/shard_map/ppermute | solution.py:560
  897.4 30.2 %collective-permute-start.39 = (bf16[1040,256]{1,0:T(8,128)(2,1)S(1)}, bf16[1040,256]{1,0:T(8,128)(2,1)S(1)}, u32[]{:S(2)}, u32[]{:S(2)}) collective-permute-start(bf16[1040,256]{1,0:T(8,128)(2,1)S(1)} %get-tuple-element.164), channel_id=1, source_target_pairs={{0,1},{1,0},{2,3},{3,2},{4,5},{5,4},{6,7},{7,6},{8,9},{9,8},{10,11... | collective-permute-start | bytes 1597448 | tf_op jit(solution)/shard_map/ppermute | solution.py:560
  (84 other events, 783.4 us)
Sparse Core Ops, SparseCore 0:
  11.1 53.5 all-gather.8
  66.9 53.2 all-gather.6
  126.0 114.2 all-gather.10
  374.6 36.1 all-gather.12
  412.9 38.0 all-gather.14
  453.1 38.5 reduce-scatter.3
  495.9 37.2 all-gather.16
  555.1 39.2 reduce-scatter.5
  763.7 62.5 reduce-scatter.7
